TPU v7x, 32 devices: a whole 2x2x4 slice. The times are simulated.
32 devices in a mesh: dp: 8 (over z, core), tensor: 4 (over y, x).
Axes of the slice: x: 2, y: 2, z: 4, core: 2. Of those that a mesh axis runs over, the one named last changes fastest.
Arguments:
- tokens: bfloat16 [16384, 2048], P(('dp', 'tensor')), may hold values from -6 to 6
- cotangent: bfloat16 [16384, 2048], P(('dp', 'tensor')), may hold values from -12 to 12
- lengths: int32 [8], P('dp'), may hold values from 512 to 2048, as said below
- query_weight: bfloat16 [2048, 2048], P('dp', 'tensor'), may hold values from -0.125 to 0.125
- key_weight: bfloat16 [2048, 2048], P('dp', 'tensor'), may hold values from -0.125 to 0.125
- value_weight: bfloat16 [2048, 2048], P('dp', 'tensor'), may hold values from -0.125 to 0.125
- out_weight: bfloat16 [2048, 2048], P('dp', 'tensor'), may hold values from -3 to 3
- up_weight: bfloat16 [2048, 8192], P('dp', 'tensor'), may hold values from -0.125 to 0.125
- down_weight: bfloat16 [2048, 8192], P('dp', 'tensor'), may hold values from -0.0625 to 0.0625
- query_bias: float32 [2048], replicated, may hold values from -1.25 to 1.25
- value_bias: float32 [2048], replicated, may hold values from -0.0625 to 0.0625
- out_bias: float32 [2048], replicated, may hold values from -0.625 to 0.625
- norm1_gain: float32 [2048], replicated, may hold values from 0.5 to 1.5
- norm1_shift: float32 [2048], replicated, may hold values from -0.625 to 0.625
- up_bias: float32 [8192], replicated, may hold values from -0.625 to 0.625
- down_bias: float32 [2048], replicated, may hold values from -0.625 to 0.625
- norm2_gain: float32 [2048], replicated, may hold values from 0.5 to 1.5
- norm2_shift: float32 [2048], replicated, may hold values from -0.625 to 0.625
Outputs:
- layer_out: bfloat16 [16384, 2048], P(('dp', 'tensor'))
- tokens_grad: bfloat16 [16384, 2048], P(('dp', 'tensor'))
- query_weight_grad: float32 [2048, 2048], P('dp', 'tensor')
- key_weight_grad: float32 [2048, 2048], P('dp', 'tensor')
- value_weight_grad: float32 [2048, 2048], P('dp', 'tensor')
- out_weight_grad: float32 [2048, 2048], P('dp', 'tensor')
- up_weight_grad: float32 [2048, 8192], P('dp', 'tensor')
- down_weight_grad: float32 [2048, 8192], P('dp', 'tensor')
- query_bias_grad: float32 [2048], P(('dp', 'tensor'))
- value_bias_grad: float32 [2048], P(('dp', 'tensor'))
- out_bias_grad: float32 [2048], P(('dp', 'tensor'))
- norm1_gain_grad: float32 [2048], P(('dp', 'tensor'))
- norm1_shift_grad: float32 [2048], P(('dp', 'tensor'))
- up_bias_grad: float32 [8192], P(('dp', 'tensor'))
- down_bias_grad: float32 [2048], P(('dp', 'tensor'))
- norm2_gain_grad: float32 [2048], P(('dp', 'tensor'))
- norm2_shift_grad: float32 [2048], P(('dp', 'tensor'))
Inputs may be any that keep to these rules, and one draw needn't show every extreme that they name: `lengths`: in every draw one slot holds a sequence of the full 2048 tokens.
All inputs are finite; a program needn't handle non-finite values.
Results may differ from a plain program's by a relative error of at most 0.025.
Values may be sent and summed in bfloat16 or wider, within the bound.
No kernel may reach another device: no remote copies, remote signals or barrier semaphores. Data moves between devices by JAX's collectives and lax.ppermute only.
A program may use at most 256 MiB of HBM per device.

v0:
```python
import jax
import jax.numpy as jnp
from jax import lax
from jax.sharding import PartitionSpec as P

HEADS = 16
HEAD_DIM = 128
FF = 8192


norm_eps = 1e-06
masked_score = -1e30


def contract_rows(left, right):
    return lax.dot_general(
        left, right, (((0,), (0,)), ((), ())), preferred_element_type=jnp.float32
    )


def contract_cols(left, right):
    return lax.dot_general(
        left, right, (((1,), (1,)), ((), ())), preferred_element_type=jnp.float32
    )


def norm_rows(value, gain, shift):
    centred = value - jnp.mean(value, axis=-1, keepdims=True)
    inverse = lax.rsqrt(jnp.mean(centred * centred, axis=-1, keepdims=True) + norm_eps)
    unit = centred * inverse
    return (unit * gain + shift, unit, inverse)


def norm_back(grad_out, unit, inverse, gain):
    grad_unit = grad_out * gain
    inner = jnp.mean(grad_unit * unit, axis=-1, keepdims=True)
    grad_in = inverse * (grad_unit - jnp.mean(grad_unit, axis=-1, keepdims=True) - unit * inner)
    return (grad_in, jnp.sum(grad_out * unit, axis=0), jnp.sum(grad_out, axis=0))


def smooth_gate(value):
    return jax.nn.gelu(value, approximate=True)


def placed(part, start, total):
    return lax.dynamic_update_slice_in_dim(jnp.zeros((total,), jnp.float32), part, start, 0)


def per_device(
    tokens,
    cotangent,
    lengths,
    query_weight,
    key_weight,
    value_weight,
    out_weight,
    up_weight,
    down_weight,
    query_bias,
    value_bias,
    out_bias,
    norm1_gain,
    norm1_shift,
    up_bias,
    down_bias,
    norm2_gain,
    norm2_shift,
):
    rows = tokens.shape[0]
    width = tokens.shape[1]
    groups = lax.axis_size("tensor")
    position = lax.axis_index("tensor")
    seq_len = rows * groups
    head_count = HEADS // groups
    head_cols = width // groups
    hidden_cols = FF // groups
    scale = HEAD_DIM ** (-0.5)
    slot_len = lengths[0]
    key_live = jnp.arange(seq_len, dtype=jnp.int32) < slot_len
    row_live = (position * rows + jnp.arange(rows, dtype=jnp.int32) < slot_len).astype(jnp.float32)[
        :, None
    ]
    col_start = position * head_cols
    hid_start = position * hidden_cols
    bias_query = lax.dynamic_slice_in_dim(query_bias, col_start, head_cols)
    bias_value = lax.dynamic_slice_in_dim(value_bias, col_start, head_cols)
    bias_up = lax.dynamic_slice_in_dim(up_bias, hid_start, hidden_cols)
    query_full, key_full, value_full, out_full = (
        lax.all_gather(query_weight, "dp", axis=0, tiled=True),
        lax.all_gather(key_weight, "dp", axis=0, tiled=True),
        lax.all_gather(value_weight, "dp", axis=0, tiled=True),
        lax.all_gather(out_weight, "dp", axis=0, tiled=True),
    )
    piece = lax.all_gather(tokens, "tensor", axis=0, tiled=True)
    queries = (jnp.dot(piece, query_full, preferred_element_type=jnp.float32) + bias_query).astype(
        jnp.bfloat16
    )
    keys = jnp.dot(piece, key_full, preferred_element_type=jnp.float32).astype(jnp.bfloat16)
    values = (jnp.dot(piece, value_full, preferred_element_type=jnp.float32) + bias_value).astype(
        jnp.bfloat16
    )
    seq_tokens, queries, keys, values = (piece, queries, keys, values)
    block = min(512, seq_len)
    blocks = seq_len // block
    key_heads = keys.reshape(seq_len, head_count, HEAD_DIM)
    value_heads = values.reshape(seq_len, head_count, HEAD_DIM)
    query_blocks = queries.reshape(blocks, block, head_count, HEAD_DIM)

    def scores_of(query_block):
        raw = (
            jnp.einsum("qhd,khd->hqk", query_block, key_heads, preferred_element_type=jnp.float32)
            * scale
        )
        return jnp.where(key_live, raw, masked_score)

    def attend(query_block):
        scores = scores_of(query_block)
        highest = jnp.max(scores, axis=-1, keepdims=True)
        normal = highest + jnp.log(jnp.sum(jnp.exp(scores - highest), axis=-1, keepdims=True))
        probs = jnp.exp(scores - normal).astype(jnp.bfloat16)
        context = jnp.einsum("hqk,khd->qhd", probs, value_heads, preferred_element_type=jnp.float32)
        return (context.astype(jnp.bfloat16), normal)

    context_blocks, totals = lax.map(attend, query_blocks)
    context = context_blocks.reshape(seq_len, head_cols)
    attn_sum = lax.psum_scatter(
        contract_cols(context, out_full).astype(jnp.bfloat16),
        "tensor",
        scatter_dimension=0,
        tiled=True,
    ).astype(jnp.float32)
    mid, mid_unit, mid_inverse = norm_rows(
        tokens.astype(jnp.float32) + attn_sum + out_bias, norm1_gain, norm1_shift
    )
    mid_low = mid.astype(jnp.bfloat16)
    up_full, down_full = (
        lax.all_gather(up_weight, "dp", axis=0, tiled=True),
        lax.all_gather(down_weight, "dp", axis=0, tiled=True),
    )
    piece = lax.all_gather(mid_low, "tensor", axis=0, tiled=True)
    pre = jnp.dot(piece, up_full, preferred_element_type=jnp.float32) + bias_up
    mid_seq = piece
    activ = smooth_gate(pre).astype(jnp.bfloat16)
    ffn_sum = lax.psum_scatter(
        contract_cols(activ, down_full).astype(jnp.bfloat16),
        "tensor",
        scatter_dimension=0,
        tiled=True,
    ).astype(jnp.float32)
    final, final_unit, final_inverse = norm_rows(mid + ffn_sum + down_bias, norm2_gain, norm2_shift)
    layer_out = (final * row_live).astype(jnp.bfloat16)
    grad_final = cotangent.astype(jnp.float32) * row_live
    grad_sum2, norm2_gain_grad, norm2_shift_grad = norm_back(
        grad_final, final_unit, final_inverse, norm2_gain
    )
    down_bias_grad = jnp.sum(grad_sum2, axis=0)
    piece = lax.all_gather(grad_sum2.astype(jnp.bfloat16), "tensor", axis=0, tiled=True)
    grad_act = jnp.dot(piece, down_full, preferred_element_type=jnp.float32)
    unused, gate_back = jax.vjp(smooth_gate, pre)
    grad_ffn = piece
    grad_pre = gate_back(grad_act)[0].astype(jnp.bfloat16)
    down_grad = contract_rows(grad_ffn, activ)
    up_grad = contract_rows(mid_seq, grad_pre)
    up_bias_part = jnp.sum(grad_pre.astype(jnp.float32), axis=0)
    grad_mid = grad_sum2 + lax.psum_scatter(
        contract_cols(grad_pre, up_full).astype(jnp.bfloat16),
        "tensor",
        scatter_dimension=0,
        tiled=True,
    ).astype(jnp.float32)
    grad_sum1, norm1_gain_grad, norm1_shift_grad = norm_back(
        grad_mid, mid_unit, mid_inverse, norm1_gain
    )
    out_bias_grad = jnp.sum(grad_sum1, axis=0)
    piece = lax.all_gather(grad_sum1.astype(jnp.bfloat16), "tensor", axis=0, tiled=True)
    grad_context = jnp.dot(piece, out_full, preferred_element_type=jnp.float32).astype(jnp.bfloat16)
    out_grad = contract_rows(piece, context)
    grad_context_blocks = grad_context.reshape(blocks, block, head_count, HEAD_DIM)

    def attend_back(carry, item):
        key_acc, value_acc = carry
        query_block, grad_block, normal = item
        probs = jnp.exp(scores_of(query_block) - normal)
        grad_probs = jnp.einsum(
            "qhd,khd->hqk", grad_block, value_heads, preferred_element_type=jnp.float32
        )
        inner = jnp.sum(probs * grad_probs, axis=-1, keepdims=True)
        grad_scores = (probs * (grad_probs - inner)).astype(jnp.bfloat16)
        grad_query = (
            jnp.einsum("hqk,khd->qhd", grad_scores, key_heads, preferred_element_type=jnp.float32)
            * scale
        )
        key_acc = (
            key_acc
            + jnp.einsum(
                "hqk,qhd->khd", grad_scores, query_block, preferred_element_type=jnp.float32
            )
            * scale
        )
        value_acc = value_acc + jnp.einsum(
            "hqk,qhd->khd",
            probs.astype(jnp.bfloat16),
            grad_block,
            preferred_element_type=jnp.float32,
        )
        return ((key_acc, value_acc), grad_query.astype(jnp.bfloat16))

    zero_heads = jnp.zeros((seq_len, head_count, HEAD_DIM), jnp.float32)
    (key_acc, value_acc), grad_query_blocks = lax.scan(
        attend_back, (zero_heads, zero_heads), (query_blocks, grad_context_blocks, totals)
    )
    grad_queries = grad_query_blocks.reshape(seq_len, head_cols)
    grad_keys = key_acc.reshape(seq_len, head_cols).astype(jnp.bfloat16)
    grad_values = value_acc.reshape(seq_len, head_cols).astype(jnp.bfloat16)
    query_grad = contract_rows(seq_tokens, grad_queries)
    key_grad = contract_rows(seq_tokens, grad_keys)
    value_grad = contract_rows(seq_tokens, grad_values)
    query_bias_part = jnp.sum(grad_queries.astype(jnp.float32), axis=0)
    value_bias_part = jnp.sum(grad_values.astype(jnp.float32), axis=0)
    total = contract_cols(grad_queries, query_full)
    total = total + contract_cols(grad_keys, key_full)
    tokens_grad = (
        grad_sum1
        + lax.psum_scatter(
            (total + contract_cols(grad_values, value_full)).astype(jnp.bfloat16),
            "tensor",
            scatter_dimension=0,
            tiled=True,
        ).astype(jnp.float32)
    ).astype(jnp.bfloat16)
    query_part, key_part, value_part, out_part, up_part, down_part = (
        lax.psum_scatter(
            query_grad.astype(jnp.bfloat16), "dp", scatter_dimension=0, tiled=True
        ).astype(jnp.float32),
        lax.psum_scatter(
            key_grad.astype(jnp.bfloat16), "dp", scatter_dimension=0, tiled=True
        ).astype(jnp.float32),
        lax.psum_scatter(
            value_grad.astype(jnp.bfloat16), "dp", scatter_dimension=0, tiled=True
        ).astype(jnp.float32),
        lax.psum_scatter(
            out_grad.astype(jnp.bfloat16), "dp", scatter_dimension=0, tiled=True
        ).astype(jnp.float32),
        lax.psum_scatter(
            up_grad.astype(jnp.bfloat16), "dp", scatter_dimension=0, tiled=True
        ).astype(jnp.float32),
        lax.psum_scatter(
            down_grad.astype(jnp.bfloat16), "dp", scatter_dimension=0, tiled=True
        ).astype(jnp.float32),
    )
    (
        query_bias_grad,
        value_bias_grad,
        out_bias_sum,
        norm1_gain_sum,
        norm1_shift_sum,
        up_bias_grad,
        down_bias_sum,
        norm2_gain_sum,
        norm2_shift_sum,
    ) = (
        lax.psum_scatter(
            placed(query_bias_part, col_start, width),
            ("dp", "tensor"),
            scatter_dimension=0,
            tiled=True,
        ),
        lax.psum_scatter(
            placed(value_bias_part, col_start, width),
            ("dp", "tensor"),
            scatter_dimension=0,
            tiled=True,
        ),
        lax.psum_scatter(out_bias_grad, ("dp", "tensor"), scatter_dimension=0, tiled=True),
        lax.psum_scatter(norm1_gain_grad, ("dp", "tensor"), scatter_dimension=0, tiled=True),
        lax.psum_scatter(norm1_shift_grad, ("dp", "tensor"), scatter_dimension=0, tiled=True),
        lax.psum_scatter(
            placed(up_bias_part, hid_start, FF), ("dp", "tensor"), scatter_dimension=0, tiled=True
        ),
        lax.psum_scatter(down_bias_grad, ("dp", "tensor"), scatter_dimension=0, tiled=True),
        lax.psum_scatter(norm2_gain_grad, ("dp", "tensor"), scatter_dimension=0, tiled=True),
        lax.psum_scatter(norm2_shift_grad, ("dp", "tensor"), scatter_dimension=0, tiled=True),
    )
    return (
        layer_out,
        tokens_grad,
        query_part,
        key_part,
        value_part,
        out_part,
        up_part,
        down_part,
        query_bias_grad,
        value_bias_grad,
        out_bias_sum,
        norm1_gain_sum,
        norm1_shift_sum,
        up_bias_grad,
        down_bias_sum,
        norm2_gain_sum,
        norm2_shift_sum,
    )


def solution(mesh):
    placed = (
        P(("dp", "tensor"), None),
        P(("dp", "tensor"), None),
        P("dp"),
        P("dp", "tensor"),
        P("dp", "tensor"),
        P("dp", "tensor"),
        P("dp", "tensor"),
        P("dp", "tensor"),
        P("dp", "tensor"),
        P(),
        P(),
        P(),
        P(),
        P(),
        P(),
        P(),
        P(),
        P(),
    )
    return jax.shard_map(
        per_device,
        mesh=mesh,
        in_specs=placed,
        out_specs=(
            P(("dp", "tensor"), None),
            P(("dp", "tensor"), None),
            P("dp", "tensor"),
            P("dp", "tensor"),
            P("dp", "tensor"),
            P("dp", "tensor"),
            P("dp", "tensor"),
            P("dp", "tensor"),
            P(("dp", "tensor")),
            P(("dp", "tensor")),
            P(("dp", "tensor")),
            P(("dp", "tensor")),
            P(("dp", "tensor")),
            P(("dp", "tensor")),
            P(("dp", "tensor")),
            P(("dp", "tensor")),
            P(("dp", "tensor")),
        ),
        check_vma=False,
    )
```

profile of v0, /device:TPU:0, one launch (start us, length us, event | category | flops | bytes accessed | tf_op | source)
XLA Modules:
  0.0 1707.2 jit_solution(15198329520281651258)
XLA Ops:
  12.2 29.3 %all-gather.17.cloned.1.call-done = bf16[2048,512]{1,0:T(8,128)(2,1)} async-done(((bf16[256,512]{1,0:T(8,128)(2,1)}), bf16[2048,512]{1,0:T(8,128)(2,1)}) %all-gather.17.cloned.1.call-update) | async-done | bytes 2097168 | tf_op jit(solution)/shard_map/all_gather | solution.py:91
  41.5 88.7 %all-gather.11.cloned.1.call-done = bf16[2048,2048]{1,0:T(8,128)(2,1)} async-done(((bf16[512,2048]{1,0:T(8,128)(2,1)}), bf16[2048,2048]{1,0:T(8,128)(2,1)}) %all-gather.11.cloned.1.call-update) | async-done | bytes 8388624 | tf_op jit(solution)/shard_map/all_gather | solution.py:94
  141.5 19.5 %all-gather.13.cloned.1.call-done = bf16[2048,512]{1,0:T(8,128)(2,1)} async-done(((bf16[256,512]{1,0:T(8,128)(2,1)}), bf16[2048,512]{1,0:T(8,128)(2,1)}) %all-gather.13.cloned.1.call-update) | async-done | bytes 2097168 | tf_op jit(solution)/shard_map/all_gather | solution.py:89
  175.1 16.0 all-gather.15.cloned.1.call-done
  204.0 87.2 %while.28 = (s32[]{:T(128)}, bf16[4,512,4,128]{3,2,1,0:T(4,128)(2,1)}, f32[4,4,512,1]{2,1,3,0:T(4,128)}, bf16[4,512,4,128]{3,1,2,0:T(8,128)(2,1)}, bf16[2048,4,1...) while((s32[]{:T(128)}, bf16[4,512,4,128]{3,2,1,0:T(4,128)(2,1)}, ...), condition=%wide.region_3.4_spmd.clone, body=%wide.region_0.3_spmd.clone.sunk | while | flops 2193883136 | bytes 132194472 | solution.py:124
  303.0 84.9 %reduce-scatter.11.cloned.1.call-done = bf16[512,2048]{1,0:T(8,128)(2,1)} async-done(((bf16[2048,2048]{1,0:T(8,128)(2,1)}), bf16[512,2048]{1,0:T(8,128)(2,1)}) %reduce-scatter.11.cloned.1.call-update) | async-done | bytes 2097168 | tf_op jit(solution)/shard_map/reduce_scatter | solution.py:126
  395.6 76.0 %all-gather.23.cloned.1.call-done = bf16[2048,2048]{1,0:T(8,128)(2,1)} async-done(((bf16[256,2048]{1,0:T(8,128)(2,1)}), bf16[2048,2048]{1,0:T(8,128)(2,1)}) %all-gather.23.cloned.1.call-update) | async-done | bytes 8388624 | tf_op jit(solution)/shard_map/all_gather | solution.py:137
  471.6 88.4 %all-gather.21.cloned.1.call-done = bf16[2048,2048]{1,0:T(8,128)(2,1)} async-done(((bf16[512,2048]{1,0:T(8,128)(2,1)}), bf16[2048,2048]{1,0:T(8,128)(2,1)}) %all-gather.21.cloned.1.call-update) | async-done | bytes 8388624 | tf_op jit(solution)/shard_map/all_gather | solution.py:140
  560.0 24.2 %fusion.64 = f32[2048,2048]{1,0:T(8,128)} fusion(bf16[2048,2048]{1,0:T(8,128)(2,1)} %all-gather.21.cloned.1.call-done, bf16[2048,2048]{1,0:T(8,128)(2,1)} %all-gather.23.cloned.1.call-done), kind=kOutput, calls=%fused_computation.124 | convolution fusion | flops 17179869184 | bytes 33554432 | tf_op jit(solution)/shard_map/dot_general | solution.py:141
  584.2 59.5 %all-gather.25.cloned.1.call-done = bf16[2048,2048]{1,0:T(8,128)(2,1)} async-done(((bf16[256,2048]{1,0:T(8,128)(2,1)}), bf16[2048,2048]{1,0:T(8,128)(2,1)}) %all-gather.25.cloned.1.call-update) | async-done | bytes 8388624 | tf_op jit(solution)/shard_map/all_gather | solution.py:138
  643.7 26.5 %convolution_convert_fusion.3 = bf16[2048,2048]{1,0:T(8,128)(2,1)} fusion(bf16[2048,2048]{1,0:T(8,128)(2,1)} %all-gather.25.cloned.1.call-done, f32[2048,2048]{1,0:T(8,128)} %fusion.64, f32[2048]{0:T(1024)S(1)} %dynamic_slice.25), kind=kOutput, calls=%fused_computation.61 | convolution fusion | flops 17226006528 | bytes 33562624 | tf_op jit(solution)/shard_map/dot_general | solution.py:22
  670.9 84.3 %reduce-scatter.13.cloned.1.call-done = bf16[512,2048]{1,0:T(8,128)(2,1)} async-done(((bf16[2048,2048]{1,0:T(8,128)(2,1)}), bf16[512,2048]{1,0:T(8,128)(2,1)}) %reduce-scatter.13.cloned.1.call-update) | async-done | bytes 2097168 | tf_op jit(solution)/shard_map/reduce_scatter | solution.py:144
  768.3 87.2 %all-gather.27.cloned.1.call-done = bf16[2048,2048]{1,0:T(8,128)(2,1)} async-done(((bf16[512,2048]{1,0:T(8,128)(2,1)}), bf16[2048,2048]{1,0:T(8,128)(2,1)}) %all-gather.27.cloned.1.call-update) | async-done | bytes 8388624 | tf_op jit(solution)/shard_map/all_gather | solution.py:157
  855.5 33.6 %convert_reduce_fusion = (f32[2048]{0:T(1024)S(1)}, bf16[2048,2048]{1,0:T(8,128)(2,1)S(1)}) fusion(f32[2048,2048]{1,0:T(8,128)} %fusion.64, f32[2048]{0:T(1024)S(1)} %dynamic_slice.25, bf16[2048,2048]{1,0:T(8,128)(2,1)} %all-gather.27.cloned.1.call-done, bf16[2048,2048]{1,0:T(8,128)(2,1)} %all-gather.25.cloned.1.call-done), kind=kOutput, calls=%fused_computation.55 | convolution fusion | flops 17276336128 | bytes 41959424 | tf_op jit(solution)/shard_map/dot_general | solution.py:158
  892.3 22.2 %convolution_convert_fusion.2 = bf16[2048,2048]{1,0:T(8,128)(2,1)} fusion(bf16[2048,2048]{1,0:T(8,128)(2,1)S(1)} %get-tuple-element.324, bf16[2048,2048]{1,0:T(8,128)(2,1)} %all-gather.23.cloned.1.call-done), kind=kOutput, calls=%fused_computation.60 | convolution fusion | flops 17184063488 | bytes 25165824 | tf_op jit(solution)/shard_map/dot_general | solution.py:22
  914.8 86.2 %reduce-scatter.15.cloned.1.call-done = bf16[512,2048]{1,0:T(8,128)(2,1)} async-done(((bf16[2048,2048]{1,0:T(8,128)(2,1)}), bf16[512,2048]{1,0:T(8,128)(2,1)}) %reduce-scatter.15.cloned.1.call-update) | async-done | bytes 2097168 | tf_op jit(solution)/shard_map/reduce_scatter | solution.py:165
  1014.8 25.1 %convolution_convert_fusion = bf16[2048,2048]{1,0:T(8,128)(2,1)} fusion(bf16[2048,2048]{1,0:T(8,128)(2,1)} %all-gather.27.cloned.1.call-done, f32[2048,2048]{1,0:T(8,128)} %fusion.64, f32[2048]{0:T(1024)S(1)} %dynamic_slice.25), kind=kOutput, calls=%fused_computation.58 | convolution fusion | flops 17226006528 | bytes 33562624 | tf_op jit(solution)/shard_map/dot_general | solution.py:16
  1042.1 23.8 %convolution_convert_fusion.1 = bf16[2048,2048]{1,0:T(8,128)(2,1)} fusion(bf16[2048,2048]{1,0:T(8,128)(2,1)} %all-gather.21.cloned.1.call-done, bf16[2048,2048]{1,0:T(8,128)(2,1)} %copy-done.27), kind=kOutput, calls=%fused_computation.59 | convolution fusion | flops 17184063488 | bytes 25165824 | tf_op jit(solution)/shard_map/dot_general | solution.py:16
  1065.9 36.4 %all-gather.29.cloned.1.call-done = bf16[2048,2048]{1,0:T(8,128)(2,1)} async-done(((bf16[512,2048]{1,0:T(8,128)(2,1)}), bf16[2048,2048]{1,0:T(8,128)(2,1)}) %all-gather.29.cloned.1.call-update) | async-done | bytes 8388624 | tf_op jit(solution)/shard_map/all_gather | solution.py:175
  1115.6 208.4 %while.29 = (s32[]{:T(128)}, f32[2048,4,128]{0,2,1:T(8,128)}, f32[2048,4,128]{0,2,1:T(8,128)}, bf16[4,512,4,128]{3,1,2,0:T(8,128)(2,1)}, bf16[4,512,4,128]{3,1,2...) while((s32[]{:T(128)}, f32[2048,4,128]{0,2,1:T(8,128)}, ...), condition=%wide.region_17.18_spmd.clone, body=%wide.region_15.17_spmd.clone.sunk | while | flops 5437390848 | bytes 253296880 | solution.py:209
  1145.6 12.4 multiply_convert_fusion.6
  1197.9 12.9 multiply_convert_fusion.6
  1238.6 12.3 multiply_reduce_fusion.9
  1250.8 12.3 multiply_convert_fusion.6
  1375.6 12.7 fusion.65
  1396.6 17.1 %add_convert_fusion = bf16[2048,2048]{1,0:T(8,128)(2,1)} fusion(f32[2048,2048]{1,0:T(8,128)} %fusion.50, f32[2048,2048]{1,0:T(8,128)} %fusion.65, bf16[2048,512]{0,1:T(8,128)(2,1)S(1)} %bitcast.138, bf16[2048,512]{1,0:T(8,128)(2,1)} %all-gather.17.cloned.1.call-done), kind=kOutput, calls=%fused_computation.56 | convolution fusion | flops 4307550208 | bytes 46137344 | tf_op jit(solution)/shard_map/dot_general | solution.py:22
  1419.4 37.2 %all-reduce.12.cloned.1.call-done = (f32[2048]{0:T(1024)}, f32[2048]{0:T(1024)}, f32[2048]{0:T(1024)}, f32[2048]{0:T(1024)}, f32[2048]{0:T(1024)}, /*index=5*/f3...) async-done(((f32[2048]{0:T(1024)}, f32[2048]{0:T(1024)}, f32[2048]{0:T(1024)}, f32[2048]{0:T(1024)}, f32[2048]{0:T(1024)}, /*index=5*/f32[8192]{0:T(1024)}, ...) | async-done | bytes 98320
  1468.0 27.9 %reduce-scatter.25.cloned.1.call-done = bf16[256,512]{1,0:T(8,128)(2,1)} async-done(((bf16[2048,512]{1,0:T(8,128)(2,1)}), bf16[256,512]{1,0:T(8,128)(2,1)}) %reduce-scatter.25.cloned.1.call-update) | async-done | bytes 262160 | tf_op jit(solution)/shard_map/reduce_scatter | solution.py:241
  1497.7 35.6 %reduce-scatter.19.cloned.1.call-done = bf16[256,512]{0,1:T(8,128)(2,1)} async-done(((bf16[2048,512]{0,1:T(8,128)(2,1)}), bf16[256,512]{0,1:T(8,128)(2,1)}) %reduce-scatter.19.cloned.1.call-update) | async-done | bytes 262160 | tf_op jit(solution)/shard_map/reduce_scatter | solution.py:232
  1535.2 35.1 %reduce-scatter.21.cloned.1.call-done = bf16[256,512]{0,1:T(8,128)(2,1)} async-done(((bf16[2048,512]{0,1:T(8,128)(2,1)}), bf16[256,512]{0,1:T(8,128)(2,1)}) %reduce-scatter.21.cloned.1.call-update) | async-done | bytes 262160 | tf_op jit(solution)/shard_map/reduce_scatter | solution.py:235
  1572.2 34.9 %reduce-scatter.23.cloned.1.call-done = bf16[256,512]{0,1:T(8,128)(2,1)} async-done(((bf16[2048,512]{0,1:T(8,128)(2,1)}), bf16[256,512]{0,1:T(8,128)(2,1)}) %reduce-scatter.23.cloned.1.call-update) | async-done | bytes 262160 | tf_op jit(solution)/shard_map/reduce_scatter | solution.py:238
  1609.0 86.2 %reduce-scatter.17.cloned.1.call-done = bf16[512,2048]{1,0:T(8,128)(2,1)} async-done(((bf16[2048,2048]{1,0:T(8,128)(2,1)}), bf16[512,2048]{1,0:T(8,128)(2,1)}) %reduce-scatter.17.cloned.1.call-update) | async-done | bytes 2097168 | tf_op jit(solution)/shard_map/reduce_scatter | solution.py:224
  (254 shorter events, 441.8 us)
Async XLA Ops:
  7.2 34.3 %all-gather.17.cloned.1.call-start = ((), (), s32[]{:S(2)}) async-start(), calls=%async_computation.13 | async-start | bytes 2359296 | tf_op jit(solution)/shard_map/all_gather | solution.py:91
  7.9 122.3 %all-gather.11.cloned.1.call-start = ((), (), s32[]{:S(2)}) async-start(), calls=%async_computation.10 | async-start | bytes 10485760 | tf_op jit(solution)/shard_map/all_gather | solution.py:94
  8.7 152.4 %all-gather.13.cloned.1.call-start = ((), (), s32[]{:S(2)}) async-start(), calls=%async_computation.11 | async-start | bytes 2359296 | tf_op jit(solution)/shard_map/all_gather | solution.py:89
  9.4 181.7 %all-gather.15.cloned.1.call-start = ((), (), s32[]{:S(2)}) async-start(), calls=%async_computation.12 | async-start | bytes 2359296 | tf_op jit(solution)/shard_map/all_gather | solution.py:90
  10.0 281.2 %all-gather.19.cloned.1.call-start = ((), (), s32[]{:S(2)}) async-start(), calls=%async_computation.14 | async-start | bytes 2359296 | tf_op jit(solution)/shard_map/all_gather | solution.py:92
  10.6 377.3 %reduce-scatter.11.cloned.1.call-start = ((), (), s32[]{:S(2)}) async-start(), calls=%async_computation.15 | async-start | bytes 10485760 | tf_op jit(solution)/shard_map/reduce_scatter | solution.py:126
  208.8 7.0 copy-start.4
  291.2 10.8 copy-start.2
  302.0 85.9 %copy-start.7 = (bf16[512,2048]{1,0:T(8,128)(2,1)S(1)}, bf16[512,2048]{1,0:T(8,128)(2,1)}, u32[]{:S(2)}) copy-start(bf16[512,2048]{1,0:T(8,128)(2,1)} %param.22) | copy-start | bytes 6291460
  302.0 85.9 %copy-start.17 = (f32[2048]{0:T(1024)S(1)}, f32[2048]{0:T(1024)}, u32[]{:S(2)}) copy-start(f32[2048]{0:T(1024)} %param.33) | copy-start | bytes 24580
  302.0 169.6 %all-gather.23.cloned.1.call-start = ((), (), s32[]{:S(2)}) async-start(), calls=%async_computation.17 | async-start | bytes 9437184 | tf_op jit(solution)/shard_map/all_gather | solution.py:137
  302.8 88.7 %copy-start.18 = (f32[2048]{0:T(1024)S(1)}, f32[2048]{0:T(1024)}, u32[]{:S(2)}) copy-start(f32[2048]{0:T(1024)} %param.34) | copy-start | bytes 24580
  302.8 88.7 %copy-start.22 = (f32[2048]{0:T(1024)S(1)}, f32[2048]{0:T(1024)}, u32[]{:S(2)}) copy-start(f32[2048]{0:T(1024)} %param.35) | copy-start | bytes 24580
  302.8 257.2 %all-gather.21.cloned.1.call-start = ((), (), s32[]{:S(2)}) async-start(), calls=%async_computation.16 | async-start | bytes 10485760 | tf_op jit(solution)/shard_map/all_gather | solution.py:140
  394.1 249.6 %all-gather.25.cloned.1.call-start = ((), (), s32[]{:S(2)}) async-start(), calls=%async_computation.18 | async-start | bytes 9437184 | tf_op jit(solution)/shard_map/all_gather | solution.py:138
  394.8 360.4 %reduce-scatter.13.cloned.1.call-start = ((), (), s32[]{:S(2)}) async-start(), calls=%async_computation.19 | async-start | bytes 10485760 | tf_op jit(solution)/shard_map/reduce_scatter | solution.py:144
  670.2 85.0 %copy-start.24 = (f32[2048]{0:T(1024)S(1)}, f32[2048]{0:T(1024)}, u32[]{:S(2)}) copy-start(f32[2048]{0:T(1024)} %param.37) | copy-start | bytes 24580
  670.2 185.2 %all-gather.27.cloned.1.call-start = ((), (), s32[]{:S(2)}) async-start(), calls=%async_computation.20 | async-start | bytes 10485760 | tf_op jit(solution)/shard_map/all_gather | solution.py:157
  767.8 233.2 %reduce-scatter.15.cloned.1.call-start = ((), (), s32[]{:S(2)}) async-start(), calls=%async_computation.21 | async-start | bytes 10485760 | tf_op jit(solution)/shard_map/reduce_scatter | solution.py:165
  914.5 187.8 %all-gather.29.cloned.1.call-start = ((), (), s32[]{:S(2)}) async-start(), calls=%async_computation.22 | async-start | bytes 10485760 | tf_op jit(solution)/shard_map/all_gather | solution.py:175
  1001.0 7.0 copy-start.12
  1014.7 399.0 %reduce-scatter.29.cloned.1.call-start = ((), (), s32[]{:S(2)}) async-start(), calls=%async_computation.29 | async-start | bytes 9437184 | tf_op jit(solution)/shard_map/reduce_scatter | solution.py:247
  1039.9 376.7 %reduce-scatter.27.cloned.1.call-start = ((), (), s32[]{:S(2)}) async-start(), calls=%async_computation.28 | async-start | bytes 9437184 | tf_op jit(solution)/shard_map/reduce_scatter | solution.py:244
  1065.8 36.5 %copy-start.26 = (bf16[2048,512]{1,0:T(8,128)(2,1)S(1)}, bf16[2048,512]{1,0:T(8,128)(2,1)}, u32[]{:S(2)}) copy-start(bf16[2048,512]{1,0:T(8,128)(2,1)} %all-gather.19.cloned.1.call-done) | copy-start | bytes 6291460
  1065.9 390.7 %all-reduce.12.cloned.1.call-start = ((), (), s32[]{:S(2)}) async-start(), calls=%async_computation.30 | async-start | bytes 196608
  1329.2 166.7 %reduce-scatter.25.cloned.1.call-start = ((), (), s32[]{:S(2)}) async-start(), calls=%async_computation.27 | async-start | bytes 2359296 | tf_op jit(solution)/shard_map/reduce_scatter | solution.py:241
  1339.2 194.2 %reduce-scatter.19.cloned.1.call-start = ((), (), s32[]{:S(2)}) async-start(), calls=%async_computation.24 | async-start | bytes 2359296 | tf_op jit(solution)/shard_map/reduce_scatter | solution.py:232
  1353.0 217.3 %reduce-scatter.21.cloned.1.call-start = ((), (), s32[]{:S(2)}) async-start(), calls=%async_computation.25 | async-start | bytes 2359296 | tf_op jit(solution)/shard_map/reduce_scatter | solution.py:235
  1366.1 241.0 %reduce-scatter.23.cloned.1.call-start = ((), (), s32[]{:S(2)}) async-start(), calls=%async_computation.26 | async-start | bytes 2359296 | tf_op jit(solution)/shard_map/reduce_scatter | solution.py:238
  1375.5 319.7 %reduce-scatter.17.cloned.1.call-start = ((), (), s32[]{:S(2)}) async-start(), calls=%async_computation.23 | async-start | bytes 10485760 | tf_op jit(solution)/shard_map/reduce_scatter | solution.py:224
  1375.6 12.7 copy-start.16
  1375.6 12.7 copy-start.25
  (32 other events, 128.3 us)
Sparse Core Ops, SparseCore 0:
  9.6 31.8 all-gather.16
  43.3 86.8 all-gather.10
  131.9 29.1 all-gather.12
  162.5 28.5 all-gather.14
  192.5 28.5 all-gather.18
  302.1 85.7 reduce-scatter.10
  389.5 82.0 all-gather.22
  474.0 85.9 all-gather.20
  561.6 82.0 all-gather.24
  670.3 84.7 reduce-scatter.12
  768.0 87.4 all-gather.26
  914.7 86.3 reduce-scatter.14
  1014.8 87.4 all-gather.28
  1104.5 89.5 reduce-scatter.28
  1196.2 87.9 reduce-scatter.26
  1329.4 127.2 all-reduce.11
  1458.7 37.1 reduce-scatter.24
  1498.6 34.6 reduce-scatter.18
  1535.6 34.6 reduce-scatter.20
  1572.5 34.5 reduce-scatter.22
  1610.2 84.9 reduce-scatter.16
where the time goes:
time: 1710 us
  waiting for transfers between devices  1020 us (60%)
  matrix products  448 us (26%)
  other arithmetic  121 us (7%)
  local copies, waits for them, and re-layouts  102 us (6%)
    dot_general x6, matrix products, contract_cols(): lax.dot_general(left, right, (((1,), (1,)), ((), ())), preferred_element_...  97.6 us
    all_gather x1, waiting for transfers between devices, per_device(): piece = lax.all_gather(tokens, 'tensor', axis=0, tiled=True)  88.7 us
    all_gather x1, waiting for transfers between devices, per_device(): piece = lax.all_gather(mid_low, 'tensor', axis=0, tiled=True)  88.4 us
    all_gather x1, waiting for transfers between devices, per_device(): lax.all_gather(grad_sum2.astype(jnp.bfloat16), 'tensor', axis=0, tiled=True)  87.2 us
    dot_general x6, matrix products, contract_rows(): lax.dot_general(left, right, (((0,), (0,)), ((), ())), preferred_element_...  86.5 us
    reduce_scatter x1, waiting for transfers between devices, per_device(): lax.psum_scatter(contract_cols(grad_pre, up_full).astype(jnp.bfloat16), '...  86.2 us
    reduce_scatter x1, waiting for transfers between devices, per_device(): lax.psum_scatter((total + contract_cols(grad_values, value_full)).astype(...  86.2 us
    reduce_scatter x1, waiting for transfers between devices, per_device(): lax.psum_scatter(contract_cols(context, out_full).astype(jnp.bfloat16), '...  84.9 us
  transfers between devices with their start and end apart: 21, of which 18 were waited for; matrix products, arithmetic and copies ran while one was open for 29% of the time, Pallas kernels for 0%

commit v1 on v0

v1 whole, which is shorter than its diff:
```python
import jax
import jax.numpy as jnp
from jax import lax
from jax.experimental import pallas as pl
from jax.experimental.pallas import tpu as pltpu
from jax.sharding import PartitionSpec as P

HEADS = 16
HEAD_DIM = 128
FF = 8192
CHUNKS = 2

norm_eps = 1e-06
masked_score = -1e30
log2_e = 1.4426950408889634
score_scale = HEAD_DIM ** (-0.5)


def nt(left, right):
    return lax.dot_general(
        left, right, (((1,), (1,)), ((), ())), preferred_element_type=jnp.float32
    )


def nn(left, right):
    return lax.dot_general(
        left, right, (((1,), (0,)), ((), ())), preferred_element_type=jnp.float32
    )


def tn(left, right):
    return lax.dot_general(
        left, right, (((0,), (0,)), ((), ())), preferred_element_type=jnp.float32
    )


def low(value):
    return value.astype(jnp.bfloat16)


def wide(value):
    return value.astype(jnp.float32)


def swap(value, bits):
    size = lax.axis_size("tensor")
    return lax.ppermute(value, "tensor", [(i, i ^ bits) for i in range(size)])


def gather_rows(own):
    size = lax.axis_size("tensor")
    if size != 4:
        return jnp.concatenate([own] + [swap(own, p) for p in range(1, size)], axis=0)
    half = own.shape[0] // 2
    first, second = swap(own, 1), swap(own, 2)
    return jnp.concatenate(
        [own, first, second, swap(first[:half], 2), swap(second[half:], 1)], axis=0
    )


def scatter_sum(terms):
    size = lax.axis_size("tensor")
    rows = terms.shape[0] // size
    block = [terms[p * rows : (p + 1) * rows] for p in range(size)]
    if size != 4:
        total = wide(block[0])
        for p in range(1, size):
            total = total + wide(swap(block[p], p))
        return total
    half = rows // 2
    upper = [b[:half] for b in block]
    lower = [b[half:] for b in block]
    relay_upper = swap(upper[3], 1)
    relay_lower = swap(lower[3], 2)
    direct_upper = swap(upper[1], 1)
    direct_lower = swap(lower[2], 2)
    sum_upper = swap(low(wide(relay_upper) + wide(upper[2])), 2)
    sum_lower = swap(low(wide(relay_lower) + wide(lower[1])), 1)
    return jnp.concatenate(
        [
            wide(upper[0]) + wide(direct_upper) + wide(sum_upper),
            wide(lower[0]) + wide(direct_lower) + wide(sum_lower),
        ],
        axis=0,
    )


def all_live(limits, run, count):
    full = limits[0] >= run
    for b in range(1, count):
        full = jnp.logical_and(full, limits[b] >= run)
    return full


def mask_dead(limits, run, count, ref, filler):
    for b in range(count):

        @pl.when(limits[b] < run)
        def _():
            rows = pl.ds(b * run, run)
            row = lax.broadcasted_iota(jnp.int32, (run, ref.shape[1]), 0)
            ref[rows, :] = jnp.where(row < limits[b], ref[rows, :], filler)


def attend(chunk, projected, limits, run):
    part = projected[0].shape[0]
    chunks = len(projected)
    cols = projected[0].shape[1] // 3
    heads = cols // HEAD_DIM
    keys_n = part * chunks
    count = keys_n // run
    block = min(1024, part)
    factor = score_scale * log2_e

    def kernel(lim, q_ref, *rest):
        k_refs, v_refs = rest[:chunks], rest[chunks : 2 * chunks]
        out_ref, lse_ref, s_ref = rest[2 * chunks :]
        q = q_ref[...]
        for c in range(chunks):
            s_ref[pl.ds(c * part, part), :] = nt(k_refs[c][...], q)

        @pl.when(jnp.logical_not(all_live(lim, run, count)))
        def _():
            mask_dead(lim, run, count, s_ref, masked_score)

        s = s_ref[...]
        top = jnp.max(s, axis=0, keepdims=True) * factor
        p = jnp.exp2(s * factor - top)
        total = jnp.sum(p, axis=0, keepdims=True)
        p = low(p)
        out = tn(v_refs[0][...], p[:part])
        for c in range(1, chunks):
            out = out + tn(v_refs[c][...], p[c * part : (c + 1) * part])
        out_ref[...] = low(jnp.transpose(out / total))
        lse_ref[0] = top + jnp.log2(total)

    key_spec = pl.BlockSpec((part, HEAD_DIM), lambda h, i, lim: (0, heads + h))
    value_spec = pl.BlockSpec((part, HEAD_DIM), lambda h, i, lim: (0, 2 * heads + h))
    row_spec = pl.BlockSpec((block, HEAD_DIM), lambda h, i, lim: (i, h))
    return pl.pallas_call(
        kernel,
        out_shape=(
            jax.ShapeDtypeStruct((part, cols), jnp.bfloat16),
            jax.ShapeDtypeStruct((heads, 1, part), jnp.float32),
        ),
        grid_spec=pltpu.PrefetchScalarGridSpec(
            num_scalar_prefetch=1,
            grid=(heads, part // block),
            in_specs=[row_spec] + [key_spec] * chunks + [value_spec] * chunks,
            out_specs=[row_spec, pl.BlockSpec((1, 1, block), lambda h, i, lim: (h, 0, i))],
            scratch_shapes=[pltpu.VMEM((keys_n, block), jnp.float32)],
        ),
        compiler_params=pltpu.CompilerParams(
            dimension_semantics=("arbitrary", "arbitrary"), vmem_limit_bytes=56 * 2**20
        ),
        cost_estimate=pl.CostEstimate(
            flops=8 * keys_n * part * cols,
            transcendentals=keys_n * part * heads,
            bytes_accessed=keys_n * cols * 4 + part * cols * 4,
        ),
        name="attend",
    )(limits, projected[chunk], *projected, *projected)


def attend_back(chunk, projected, context, grad, lse, limits, run, carry):
    part = projected[0].shape[0]
    chunks = len(projected)
    cols = projected[0].shape[1] // 3
    heads = cols // HEAD_DIM
    keys_n = part * chunks
    count = keys_n // run
    block = min(1024, part)
    steps = part // block
    factor = score_scale * log2_e
    last = chunk == chunks - 1

    def kernel(lim, q_ref, o_ref, do_ref, lse_ref, *rest):
        k_refs, v_refs = rest[:chunks], rest[chunks : 2 * chunks]
        rest = rest[2 * chunks :]
        if carry is not None:
            key_in, value_in = rest[:2]
            rest = rest[2:]
        dq_ref, dk_ref, dv_ref, p_ref, key_acc, value_acc = rest
        step = pl.program_id(1)

        @pl.when(step == 0)
        def _():
            if carry is None:
                key_acc[...] = jnp.zeros_like(key_acc)
                value_acc[...] = jnp.zeros_like(value_acc)
            else:
                key_acc[...] = key_in[...]
                value_acc[...] = value_in[...]

        q = q_ref[...]
        do = do_ref[...]
        lse = lse_ref[0]
        for c in range(chunks):
            p_ref[pl.ds(c * part, part), :] = jnp.exp2(nt(k_refs[c][...], q) * factor - lse)

        @pl.when(jnp.logical_not(all_live(lim, run, count)))
        def _():
            mask_dead(lim, run, count, p_ref, 0.0)

        inner = jnp.sum(jnp.transpose(wide(do) * wide(o_ref[...])), axis=0, keepdims=True)
        dq = None
        for c in range(chunks):
            rows = pl.ds(c * part, part)
            p = p_ref[rows, :]
            ds = low(p * (nt(v_refs[c][...], do) - inner))
            value_acc[rows, :] += nn(low(p), do)
            key_acc[rows, :] += nn(ds, q)
            term = tn(k_refs[c][...], ds)
            dq = term if dq is None else dq + term
        dq_ref[...] = low(jnp.transpose(dq * score_scale))

        @pl.when(step == steps - 1)
        def _():
            if last:
                dk_ref[...] = low(key_acc[...] * score_scale)
                dv_ref[...] = low(value_acc[...])
            else:
                dk_ref[...] = key_acc[...]
                dv_ref[...] = value_acc[...]

    key_spec = pl.BlockSpec((part, HEAD_DIM), lambda h, i, lim: (0, heads + h))
    value_spec = pl.BlockSpec((part, HEAD_DIM), lambda h, i, lim: (0, 2 * heads + h))
    row_spec = pl.BlockSpec((block, HEAD_DIM), lambda h, i, lim: (i, h))
    acc_spec = pl.BlockSpec((keys_n, HEAD_DIM), lambda h, i, lim: (0, h))
    acc_type = jnp.bfloat16 if last else jnp.float32
    acc_shape = jax.ShapeDtypeStruct((keys_n, cols), acc_type)
    return pl.pallas_call(
        kernel,
        out_shape=(jax.ShapeDtypeStruct((part, cols), jnp.bfloat16), acc_shape, acc_shape),
        grid_spec=pltpu.PrefetchScalarGridSpec(
            num_scalar_prefetch=1,
            grid=(heads, steps),
            in_specs=[
                row_spec,
                row_spec,
                row_spec,
                pl.BlockSpec((1, 1, block), lambda h, i, lim: (h, 0, i)),
            ]
            + [key_spec] * chunks
            + [value_spec] * chunks
            + ([] if carry is None else [acc_spec] * 2),
            out_specs=[row_spec, acc_spec, acc_spec],
            scratch_shapes=[
                pltpu.VMEM((keys_n, block), jnp.float32),
                pltpu.VMEM((keys_n, HEAD_DIM), jnp.float32),
                pltpu.VMEM((keys_n, HEAD_DIM), jnp.float32),
            ],
        ),
        compiler_params=pltpu.CompilerParams(
            dimension_semantics=("arbitrary", "arbitrary"), vmem_limit_bytes=56 * 2**20
        ),
        cost_estimate=pl.CostEstimate(
            flops=20 * keys_n * part * cols,
            transcendentals=keys_n * part * heads,
            bytes_accessed=keys_n * cols * 16 + part * cols * 8,
        ),
        name="attend_back",
    )(
        limits,
        projected[chunk],
        context,
        grad,
        lse,
        *projected,
        *projected,
        *(() if carry is None else carry),
    )


def norm_rows(value, gain, shift):
    centred = value - jnp.mean(value, axis=-1, keepdims=True)
    inverse = lax.rsqrt(jnp.mean(centred * centred, axis=-1, keepdims=True) + norm_eps)
    unit = centred * inverse
    return (unit * gain + shift, unit, inverse)


def norm_back(grad_out, unit, inverse, gain):
    grad_unit = grad_out * gain
    inner = jnp.mean(grad_unit * unit, axis=-1, keepdims=True)
    grad_in = inverse * (grad_unit - jnp.mean(grad_unit, axis=-1, keepdims=True) - unit * inner)
    return (grad_in, jnp.sum(grad_out * unit, axis=0), jnp.sum(grad_out, axis=0))


def gate_and_slope(pre):
    ratio = (2.0 / jnp.pi) ** 0.5
    square = pre * pre
    bent = jnp.tanh(ratio * (pre + 0.044715 * square * pre))
    half = 0.5 * (1.0 + bent)
    slope = half + 0.5 * pre * (1.0 - bent * bent) * (ratio * (1.0 + 3 * 0.044715 * square))
    return low(pre * half), low(slope)


def placed(part, start, total):
    return lax.dynamic_update_slice_in_dim(jnp.zeros((total,), jnp.float32), part, start, 0)


def total_of(vectors):
    devices = lax.axis_size("dp") * lax.axis_size("tensor")
    packed = jnp.concatenate([v.reshape(devices, -1) for v in vectors], axis=1)
    packed = lax.psum_scatter(packed, ("dp", "tensor"), scatter_dimension=0, tiled=True)[0]
    sizes = [v.shape[0] // devices for v in vectors]
    parts, at = [], 0
    for size in sizes:
        parts.append(packed[at : at + size])
        at += size
    return parts


def gather_weight(weight):
    return lax.all_gather(weight, "dp", axis=0, tiled=True)


def scatter_weight(grad):
    return wide(lax.psum_scatter(low(grad), "dp", scatter_dimension=0, tiled=True))


def add_up(terms):
    total = terms[0]
    for term in terms[1:]:
        total = total + term
    return total


def per_device(
    tokens,
    cotangent,
    lengths,
    query_weight,
    key_weight,
    value_weight,
    out_weight,
    up_weight,
    down_weight,
    query_bias,
    value_bias,
    out_bias,
    norm1_gain,
    norm1_shift,
    up_bias,
    down_bias,
    norm2_gain,
    norm2_shift,
):
    rows, width = tokens.shape
    groups = lax.axis_size("tensor")
    position = lax.axis_index("tensor")
    head_cols = width // groups
    hidden_cols = FF // groups
    slot_len = lengths[0]
    col_start = position * head_cols
    hid_start = position * hidden_cols
    part = rows // CHUNKS
    cut = [slice(c * part, (c + 1) * part) for c in range(CHUNKS)]
    every = range(CHUNKS)
    limits = jnp.stack(
        [
            slot_len - ((position ^ p) * rows + c * part)
            for c in range(CHUNKS)
            for p in range(groups)
        ]
    ).astype(jnp.int32)
    row_live = (position * rows + jnp.arange(rows, dtype=jnp.int32) < slot_len).astype(jnp.float32)[
        :, None
    ]
    bias_query = lax.dynamic_slice_in_dim(query_bias, col_start, head_cols)
    bias_value = lax.dynamic_slice_in_dim(value_bias, col_start, head_cols)
    bias_up = lax.dynamic_slice_in_dim(up_bias, hid_start, hidden_cols)
    bias_proj = jnp.concatenate([bias_query, jnp.zeros_like(bias_query), bias_value])

    proj_full = gather_weight(jnp.concatenate([query_weight, key_weight, value_weight], axis=1))
    out_full = gather_weight(out_weight)
    up_full = gather_weight(up_weight)
    down_full = gather_weight(down_weight)

    seq_tokens = [gather_rows(tokens[cut[c]]) for c in every]
    projected = [low(nn(seq_tokens[c], proj_full) + bias_proj) for c in every]
    context, lse, mid, unit1, inverse1, mid_low = ([None] * CHUNKS for _ in range(6))
    for c in every:
        context[c], lse[c] = attend(c, projected, limits, part)
    for c in every:
        attn_sum = scatter_sum(low(nt(context[c], out_full)))
        mid[c], unit1[c], inverse1[c] = norm_rows(
            wide(tokens[cut[c]]) + attn_sum + out_bias, norm1_gain, norm1_shift
        )
    mid_seq = [gather_rows(low(mid[c])) for c in every]
    activ, slope = ([None] * CHUNKS for _ in range(2))
    ffn_sum = [None] * CHUNKS
    for c in every:
        activ[c], slope[c] = gate_and_slope(nn(mid_seq[c], up_full) + bias_up)
        ffn_sum[c] = scatter_sum(low(nt(activ[c], down_full)))
    layer_out, grad_sum2, vec2 = ([None] * CHUNKS for _ in range(3))
    for c in every:
        final, unit2, inverse2 = norm_rows(mid[c] + ffn_sum[c] + down_bias, norm2_gain, norm2_shift)
        layer_out[c] = low(final * row_live[cut[c]])
        grad_final = wide(cotangent[cut[c]]) * row_live[cut[c]]
        grad_sum2[c], gain_part, shift_part = norm_back(grad_final, unit2, inverse2, norm2_gain)
        vec2[c] = (gain_part, shift_part, jnp.sum(grad_sum2[c], axis=0))
    grad_ffn = [gather_rows(low(grad_sum2[c])) for c in every]
    grad_pre = [low(nn(grad_ffn[c], down_full) * wide(slope[c])) for c in every]
    mid_sum = [scatter_sum(low(nt(grad_pre[c], up_full))) for c in every]
    grad_sum1, vec1 = ([None] * CHUNKS for _ in range(2))
    for c in every:
        grad_sum1[c], gain_part, shift_part = norm_back(
            grad_sum2[c] + mid_sum[c], unit1[c], inverse1[c], norm1_gain
        )
        vec1[c] = (gain_part, shift_part, jnp.sum(grad_sum1[c], axis=0))
    grad_attn = [gather_rows(low(grad_sum1[c])) for c in every]

    down_part = scatter_weight(add_up([tn(grad_ffn[c], activ[c]) for c in every]))
    up_part = scatter_weight(add_up([tn(mid_seq[c], grad_pre[c]) for c in every]))
    out_part = scatter_weight(add_up([tn(grad_attn[c], context[c]) for c in every]))
    up_bias_part = add_up([jnp.sum(wide(grad_pre[c]), axis=0) for c in every])

    grad_query, carry = [None] * CHUNKS, None
    for c in every:
        grad_context = low(nn(grad_attn[c], out_full))
        grad_query[c], *carry = attend_back(
            c, projected, context[c], grad_context, lse[c], limits, part, carry
        )
    size = part * groups
    grad_proj = [
        jnp.concatenate([grad_query[c]] + [a[c * size : (c + 1) * size] for a in carry], axis=1)
        for c in every
    ]
    proj_part = scatter_weight(add_up([tn(seq_tokens[c], grad_proj[c]) for c in every]))
    tokens_grad = [
        low(grad_sum1[c] + scatter_sum(low(nt(grad_proj[c], proj_full)))) for c in every
    ]
    proj_bias = add_up([jnp.sum(wide(grad_proj[c]), axis=0) for c in every])
    (
        norm2_gain_grad,
        norm2_shift_grad,
        down_bias_grad,
        norm1_gain_grad,
        norm1_shift_grad,
        out_bias_grad,
        up_bias_grad,
    ) = total_of(
        [add_up([vec2[c][i] for c in every]) for i in range(3)]
        + [add_up([vec1[c][i] for c in every]) for i in range(3)]
        + [placed(up_bias_part, hid_start, FF)]
    )
    query_bias_grad, value_bias_grad = total_of(
        [
            placed(proj_bias[:head_cols], col_start, width),
            placed(proj_bias[2 * head_cols :], col_start, width),
        ]
    )
    return (
        jnp.concatenate(layer_out, axis=0),
        jnp.concatenate(tokens_grad, axis=0),
        proj_part[:, :head_cols],
        proj_part[:, head_cols : 2 * head_cols],
        proj_part[:, 2 * head_cols :],
        out_part,
        up_part,
        down_part,
        query_bias_grad,
        value_bias_grad,
        out_bias_grad,
        norm1_gain_grad,
        norm1_shift_grad,
        up_bias_grad,
        down_bias_grad,
        norm2_gain_grad,
        norm2_shift_grad,
    )


def solution(mesh):
    row = P(("dp", "tensor"), None)
    block = P("dp", "tensor")
    share = P(("dp", "tensor"))
    return jax.shard_map(
        per_device,
        mesh=mesh,
        in_specs=(row, row, P("dp")) + (block,) * 6 + (P(),) * 9,
        out_specs=(row, row) + (block,) * 6 + (share,) * 9,
        check_vma=False,
    )
```

time: 1710 us -> 1110 us (0.65)
  waiting for transfers between devices: 1020 us -> 430 us
  matrix products: 448 us -> 282 us
  Pallas kernels: 0 us -> 95.4 us
  starting transfers between devices: 1.61 us -> 91.4 us
  blocking collectives: 0 us -> 87.4 us
  other arithmetic: 121 us -> 48.1 us
  local copies, waits for them, and re-layouts: 102 us -> 54.7 us
    all_gather x10 -> x4, waiting for transfers between devices: 501 us -> 0.01 us  [gather_weight(): return lax.all_gather(weight, 'dp', axis=0, tiled=True)]
    reduce_scatter x10 -> x4, waiting for transfers between devices: 475 us -> 45.2 us  [scatter_weight(): lax.psum_scatter(low(grad), 'dp', scatter_dimension=0, tiled=True)]
    ppermute x0 -> x80, waiting for transfers between devices: none -> 383 us  [swap(): return lax.ppermute(value, 'tensor', [(i, i ^ bits) for i in range(size)])]
    dot_general x46 -> x24, matrix products: 448 us -> 282 us  [the longest x8 99.8 us: tn(): lax.dot_general(left, right, (((0,), (0,)), ((), ())), preferred_element_...]
    pallas_call x0 -> x4, Pallas kernels: none -> 95.4 us  [the longest x2 55 us: attend_back(): pl.pallas_call(kernel, out_shape=(jax.ShapeDtypeStruct((part, cols), jnp....]
    ppermute x0 -> x80, starting transfers between devices: none -> 91 us  [swap(): return lax.ppermute(value, 'tensor', [(i, i ^ bits) for i in range(size)])]
    unnamed x0 -> x1, blocking collectives: none -> 87.4 us
    convert_element_type x12 -> x13, other arithmetic: 72.9 us -> 11.2 us  [the longest x3 7.41 us: wide(): return value.astype(jnp.float32)]
  transfers between devices with their start and end apart: 21 -> 89, of which waited for: 18 -> 36; matrix products, arithmetic and copies ran while one was open for 29% -> 31% of each run, Pallas kernels for 0% -> 9%
where the time goes in v1:
time: 1110 us
  waiting for transfers between devices  430 us (39%)
  matrix products  282 us (25%)
  Pallas kernels  95.4 us (9%)
  starting transfers between devices  91.4 us (8%)
  blocking collectives  87.4 us (8%)
  local copies, waits for them, and re-layouts  54.7 us (5%)
  other arithmetic  48.1 us (4%)
  between operations  16.3 us (1%)
    ppermute x80, waiting for transfers between devices, swap(): return lax.ppermute(value, 'tensor', [(i, i ^ bits) for i in range(size)])  383 us
    dot_general x8, matrix products, tn(): lax.dot_general(left, right, (((0,), (0,)), ((), ())), preferred_element_...  99.8 us
    dot_general x8, matrix products, nn(): lax.dot_general(left, right, (((1,), (0,)), ((), ())), preferred_element_...  98.4 us
    ppermute x80, starting transfers between devices, swap(): return lax.ppermute(value, 'tensor', [(i, i ^ bits) for i in range(size)])  91 us
    unnamed x1, blocking collectives  87.4 us
    dot_general x8, matrix products, nt(): lax.dot_general(left, right, (((1,), (1,)), ((), ())), preferred_element_...  83.9 us
    pallas_call x2, Pallas kernels, attend_back(): pl.pallas_call(kernel, out_shape=(jax.ShapeDtypeStruct((part, cols), jnp....  55 us
    reduce_scatter x4, waiting for transfers between devices, scatter_weight(): lax.psum_scatter(low(grad), 'dp', scatter_dimension=0, tiled=True)  45.2 us
  transfers between devices with their start and end apart: 89, of which 36 were waited for; matrix products, arithmetic and copies ran while one was open for 31% of the time, Pallas kernels for 9%

profile of v1, /device:TPU:0, one launch (start us, length us, event | category | flops | bytes accessed | tf_op | source)
XLA Modules:
  0.0 1105.0 jit_solution(6906119682886368048)
XLA Ops:
  21.2 19.3 %collective-permute-done = bf16[256,2048]{1,0:T(8,128)(2,1)S(1)} collective-permute-done((bf16[256,2048]{1,0:T(8,128)(2,1)}, bf16[256,2048]{1,0:T(8,128)(2,1)S(1)}, u32[]{:S(2)}, u32[]{:S(2)}) %collective-permute-start) | collective-permute-done | bytes 1048608 | tf_op jit(solution)/shard_map/ppermute | solution.py:47
  44.3 18.7 %collective-permute-done.4 = bf16[256,2048]{1,0:T(8,128)(2,1)S(1)} collective-permute-done((bf16[256,2048]{1,0:T(8,128)(2,1)}, bf16[256,2048]{1,0:T(8,128)(2,1)S(1)}, u32[]{:S(2)}, u32[]{:S(2)}) %collective-permute-start.4) | collective-permute-done | bytes 1048608 | tf_op jit(solution)/shard_map/ppermute | solution.py:47
  108.7 20.0 %attend.2 = (bf16[1024,512]{1,0:T(8,128)(2,1)}, f32[4,1,1024]{2,1,0:T(1,128)}) custom-call(s32[8]{0:T(128)} %stack.35.lim, bf16[1024,1536]{1,0:T(8,128)(2,1)} %add_convert_fusion.6.q_ref.rest_0_.rest_2_, bf16[1024,1536]{1,0:T(8,128)(2,1)} %add_convert_fusion.6.q_ref.rest_0_.rest_2_, bf16[1024,1536]{1,0:T(8,128)(2,1)} %add_convert_fusion.5.rest_1_.rest_3_.q_ref, ...), custom_call_target="tpu_custom_call" | custom-call | flops 8589934592 | bytes 6291456 | tf_op jit(solution)/shard_map/attend/pallas_call | solution.py:140
  133.7 20.3 %attend.3 = (bf16[1024,512]{1,0:T(8,128)(2,1)}, f32[4,1,1024]{2,1,0:T(1,128)}) custom-call(s32[8]{0:T(128)} %stack.35.lim, bf16[1024,1536]{1,0:T(8,128)(2,1)} %add_convert_fusion.5.rest_1_.rest_3_.q_ref, bf16[1024,1536]{1,0:T(8,128)(2,1)} %add_convert_fusion.6.q_ref.rest_0_.rest_2_, bf16[1024,1536]{1,0:T(8,128)(2,1)} %add_convert_fusion.5.rest_1_.rest_3_.q_ref, ...), custom_call_target="tpu_custom_call" | custom-call | flops 8589934592 | bytes 6291456 | tf_op jit(solution)/shard_map/attend/pallas_call | solution.py:140
  194.7 14.4 %collective-permute-done.28 = bf16[128,2048]{1,0:T(8,128)(2,1)S(1)} collective-permute-done((bf16[128,2048]{1,0:T(8,128)(2,1)S(1)}, bf16[128,2048]{1,0:T(8,128)(2,1)S(1)}, u32[]{:S(2)}, u32[]{:S(2)}) %collective-permute-start.28) | collective-permute-done | bytes 524320 | tf_op jit(solution)/shard_map/ppermute | solution.py:47
  209.1 16.9 %collective-permute-done.26 = bf16[128,2048]{1,0:T(8,128)(2,1)S(1)} collective-permute-done((bf16[128,2048]{1,0:T(8,128)(2,1)S(1)}, bf16[128,2048]{1,0:T(8,128)(2,1)S(1)}, u32[]{:S(2)}, u32[]{:S(2)}) %collective-permute-start.26) | collective-permute-done | bytes 524320 | tf_op jit(solution)/shard_map/ppermute | solution.py:47
  244.9 21.5 %collective-permute-done.14 = bf16[256,2048]{1,0:T(8,128)(2,1)S(1)} collective-permute-done((bf16[256,2048]{1,0:T(8,128)(2,1)}, bf16[256,2048]{1,0:T(8,128)(2,1)S(1)}, u32[]{:S(2)}, u32[]{:S(2)}) %collective-permute-start.14) | collective-permute-done | bytes 1048608 | tf_op jit(solution)/shard_map/ppermute | solution.py:47
  270.5 18.5 %collective-permute-done.30 = bf16[256,2048]{1,0:T(8,128)(2,1)} collective-permute-done((bf16[256,2048]{1,0:T(8,128)(2,1)}, bf16[256,2048]{1,0:T(8,128)(2,1)}, u32[]{:S(2)}, u32[]{:S(2)}) %collective-permute-start.30) | collective-permute-done | bytes 1048608 | tf_op jit(solution)/shard_map/ppermute | solution.py:47
  306.6 14.6 %fusion.48 = f32[1024,2048]{1,0:T(8,128)} fusion(bf16[1024,2048]{1,0:T(8,128)(2,1)} %constant_dynamic-update-slice_fusion.10, bf16[2048,2048]{1,0:T(8,128)(2,1)} %all-gather.9.cloned.1.call-done), kind=kOutput, calls=%fused_computation.216 | convolution fusion | flops 8589934592 | bytes 20971520 | tf_op jit(solution)/shard_map/dot_general | solution.py:26
  321.1 15.6 %convolution_convert_fusion.6 = bf16[1024,2048]{1,0:T(8,128)(2,1)S(1)} fusion(bf16[2048,2048]{1,0:T(8,128)(2,1)} %all-gather.11.cloned.1.call-done, f32[1024,2048]{1,0:T(8,128)} %fusion.48, f32[2048]{0:T(1024)S(1)} %dynamic_slice.11), kind=kOutput, calls=%fused_computation.30 | convolution fusion | flops 8613003264 | bytes 20979712 | tf_op jit(solution)/shard_map/dot_general | solution.py:20
  340.7 14.5 %fusion.49 = f32[1024,2048]{1,0:T(8,128)} fusion(bf16[1024,2048]{1,0:T(8,128)(2,1)} %constant_dynamic-update-slice_fusion.15, bf16[2048,2048]{1,0:T(8,128)(2,1)} %all-gather.9.cloned.1.call-done), kind=kOutput, calls=%fused_computation.217 | convolution fusion | flops 8589934592 | bytes 20971520 | tf_op jit(solution)/shard_map/dot_general | solution.py:26
  355.2 15.7 %convolution_convert_fusion.4 = bf16[1024,2048]{1,0:T(8,128)(2,1)S(1)} fusion(bf16[2048,2048]{1,0:T(8,128)(2,1)} %all-gather.11.cloned.1.call-done, f32[1024,2048]{1,0:T(8,128)} %fusion.49, f32[2048]{0:T(1024)S(1)} %dynamic_slice.11), kind=kOutput, calls=%fused_computation.28 | convolution fusion | flops 8613003264 | bytes 20979712 | tf_op jit(solution)/shard_map/dot_general | solution.py:20
  409.3 12.8 %collective-permute-done.36 = bf16[128,2048]{1,0:T(8,128)(2,1)S(1)} collective-permute-done((bf16[128,2048]{1,0:T(8,128)(2,1)S(1)}, bf16[128,2048]{1,0:T(8,128)(2,1)S(1)}, u32[]{:S(2)}, u32[]{:S(2)}) %collective-permute-start.36) | collective-permute-done | bytes 524320 | tf_op jit(solution)/shard_map/ppermute | solution.py:47
  446.7 20.7 %collective-permute-done.40 = bf16[256,2048]{1,0:T(8,128)(2,1)S(1)} collective-permute-done((bf16[256,2048]{1,0:T(8,128)(2,1)S(1)}, bf16[256,2048]{1,0:T(8,128)(2,1)S(1)}, u32[]{:S(2)}, u32[]{:S(2)}) %collective-permute-start.40) | collective-permute-done | bytes 1048608 | tf_op jit(solution)/shard_map/ppermute | solution.py:47
  469.6 20.2 %collective-permute-done.54 = bf16[256,2048]{1,0:T(8,128)(2,1)S(1)} collective-permute-done((bf16[256,2048]{1,0:T(8,128)(2,1)S(1)}, bf16[256,2048]{1,0:T(8,128)(2,1)S(1)}, u32[]{:S(2)}, u32[]{:S(2)}) %collective-permute-start.54) | collective-permute-done | bytes 1048608 | tf_op jit(solution)/shard_map/ppermute | solution.py:47
  496.4 19.9 %convert_reduce_fusion.1 = (f32[2048]{0:T(1024)S(1)}, bf16[1024,2048]{1,0:T(8,128)(2,1)}) fusion(f32[1024,2048]{1,0:T(8,128)} %fusion.48, f32[2048]{0:T(1024)S(1)} %dynamic_slice.11, bf16[1024,2048]{1,0:T(8,128)(2,1)S(1)} %constant_dynamic-update-slice_fusion.20, bf16[2048,2048]{1,0:T(8,128)(2,1)} %all-gather.11.cloned.1.call-done), kind=kOutput, calls=%fused_computation.10 | convolution fusion | flops 8638167040 | bytes 25182208 | tf_op jit(solution)/shard_map/dot_general | solution.py:26
  516.4 12.6 %convolution_convert_fusion.3 = bf16[1024,2048]{1,0:T(8,128)(2,1)S(1)} fusion(bf16[1024,2048]{1,0:T(8,128)(2,1)} %get-tuple-element.172, bf16[2048,2048]{1,0:T(8,128)(2,1)} %all-gather.9.cloned.1.call-done), kind=kOutput, calls=%fused_computation.27 | convolution fusion | flops 8592031744 | bytes 16777216 | tf_op jit(solution)/shard_map/dot_general | solution.py:20
  531.9 19.6 %convert_reduce_fusion = (f32[2048]{0:T(1024)S(1)}, bf16[1024,2048]{1,0:T(8,128)(2,1)}) fusion(f32[1024,2048]{1,0:T(8,128)} %fusion.49, f32[2048]{0:T(1024)S(1)} %dynamic_slice.11, bf16[1024,2048]{1,0:T(8,128)(2,1)} %constant_dynamic-update-slice_fusion.30, bf16[2048,2048]{1,0:T(8,128)(2,1)} %all-gather.11.cloned.1.call-done), kind=kOutput, calls=%fused_computation.9 | convolution fusion | flops 8638167040 | bytes 25182208 | tf_op jit(solution)/shard_map/dot_general | solution.py:26
  551.5 12.7 %convolution_convert_fusion.2 = bf16[1024,2048]{1,0:T(8,128)(2,1)S(1)} fusion(bf16[1024,2048]{1,0:T(8,128)(2,1)} %get-tuple-element.174, bf16[2048,2048]{1,0:T(8,128)(2,1)} %all-gather.9.cloned.1.call-done), kind=kOutput, calls=%fused_computation.26 | convolution fusion | flops 8592031744 | bytes 16777216 | tf_op jit(solution)/shard_map/dot_general | solution.py:20
  607.5 12.7 %collective-permute-done.60 = bf16[128,2048]{1,0:T(8,128)(2,1)S(1)} collective-permute-done((bf16[128,2048]{1,0:T(8,128)(2,1)S(1)}, bf16[128,2048]{1,0:T(8,128)(2,1)S(1)}, u32[]{:S(2)}, u32[]{:S(2)}) %collective-permute-start.60) | collective-permute-done | bytes 524320 | tf_op jit(solution)/shard_map/ppermute | solution.py:47
  622.1 13.4 %collective-permute-done.63 = bf16[128,2048]{1,0:T(8,128)(2,1)S(1)} collective-permute-done((bf16[128,2048]{1,0:T(8,128)(2,1)S(1)}, bf16[128,2048]{1,0:T(8,128)(2,1)S(1)}, u32[]{:S(2)}, u32[]{:S(2)}) %collective-permute-start.63) | collective-permute-done | bytes 524320 | tf_op jit(solution)/shard_map/ppermute | solution.py:47
  647.3 19.3 %collective-permute-done.64 = bf16[256,2048]{1,0:T(8,128)(2,1)S(1)} collective-permute-done((bf16[256,2048]{1,0:T(8,128)(2,1)}, bf16[256,2048]{1,0:T(8,128)(2,1)S(1)}, u32[]{:S(2)}, u32[]{:S(2)}) %collective-permute-start.64) | collective-permute-done | bytes 1048608 | tf_op jit(solution)/shard_map/ppermute | solution.py:47
  696.3 27.2 %attend_back.2 = (bf16[1024,512]{1,0:T(8,128)(2,1)}, f32[2048,512]{1,0:T(8,128)}, f32[2048,512]{1,0:T(8,128)}) custom-call(s32[8]{0:T(128)} %stack.35.lim, bf16[1024,1536]{1,0:T(8,128)(2,1)} %add_convert_fusion.6.q_ref.rest_0_.rest_2_, bf16[1024,512]{1,0:T(8,128)(2,1)} %get-tuple-element.27.o_ref, bf16[1024,512]{1,0:T(8,128)(2,1)} %convolution_convert_fusion.9.do_ref, ...), custom_call_target="tpu_custom_call" | custom-call | flops 21474836480 | bytes 20971520 | tf_op jit(solution)/shard_map/attend_back/pallas_call | solution.py:232
  735.0 27.8 %attend_back.3 = (bf16[1024,512]{1,0:T(8,128)(2,1)}, bf16[2048,512]{1,0:T(8,128)(2,1)}, bf16[2048,512]{1,0:T(8,128)(2,1)}) custom-call(s32[8]{0:T(128)} %stack.35.lim, bf16[1024,1536]{1,0:T(8,128)(2,1)} %add_convert_fusion.5.rest_1_.rest_3_.q_ref, bf16[1024,512]{1,0:T(8,128)(2,1)} %get-tuple-element.28.o_ref, ...), custom_call_target="tpu_custom_call" | custom-call | flops 21474836480 | bytes 20971520 | tf_op jit(solution)/shard_map/attend_back/pallas_call | solution.py:232
  777.9 12.5 %add_convert_fusion.2 = bf16[2048,1536]{1,0:T(8,128)(2,1)} fusion(f32[2048,1536]{1,0:T(8,128)} %fusion.19, bf16[1024,2048]{1,0:T(8,128)(2,1)S(1)} %copy-done.24, bf16[1024,512]{1,0:T(8,128)(2,1)S(1)} %get-tuple-element.143, bf16[1024,512]{1,0:T(8,128)(2,1)S(1)} %get-tuple-element.141, bf16[1024,512]{1,0:T(8,128)(2,1)S(1)} %copy-done.20), kind=kOutput, calls=%fused_computation.2 | convolution fusion | flops 6458179584 | bytes 26214400 | tf_op jit(solution)/shard_map/dot_general | solution.py:32
  790.5 15.5 %fusion.51 = f32[2048,2048]{1,0:T(8,128)} fusion(bf16[1024,2048]{1,0:T(8,128)(2,1)} %constant_dynamic-update-slice_fusion.15, bf16[1024,2048]{1,0:T(8,128)(2,1)} %get-tuple-element.174), kind=kOutput, calls=%fused_computation.219 | convolution fusion | flops 8589934592 | bytes 25165824 | tf_op jit(solution)/shard_map/dot_general | solution.py:32
  806.0 14.7 %add_convert_fusion.1 = bf16[2048,2048]{1,0:T(8,128)(2,1)} fusion(f32[2048,2048]{1,0:T(8,128)} %fusion.51, bf16[1024,2048]{1,0:T(8,128)(2,1)S(1)} %copy-done.29, bf16[1024,2048]{1,0:T(8,128)(2,1)S(1)} %copy-done.42), kind=kOutput, calls=%fused_computation.1 | convolution fusion | flops 8598323200 | bytes 33554432 | tf_op jit(solution)/shard_map/dot_general | solution.py:32
  821.3 16.5 %fusion.20 = f32[2048,2048]{1,0:T(8,128)} fusion(bf16[1024,2048]{1,0:T(8,128)(2,1)} %constant_dynamic-update-slice_fusion.30, f32[1024,2048]{1,0:T(8,128)} %fusion.49, f32[2048]{0:T(1024)S(1)} %copy-done.36), kind=kOutput, calls=%fused_computation.194 | convolution fusion | flops 8610906112 | bytes 29368320 | tf_op jit(solution)/shard_map/dot_general | solution.py:32
  837.8 17.7 %add_convert_fusion = bf16[2048,2048]{1,0:T(8,128)(2,1)} fusion(f32[2048,2048]{1,0:T(8,128)} %fusion.20, bf16[1024,2048]{1,0:T(8,128)(2,1)} %copy-done.28, f32[1024,2048]{1,0:T(8,128)} %fusion.48, f32[2048]{0:T(1024)S(1)} %copy-done.36), kind=kOutput, calls=%fused_computation | convolution fusion | flops 8619294720 | bytes 37756928 | tf_op jit(solution)/shard_map/dot_general | solution.py:32
  889.2 87.4 %all-reduce = f32[32,128]{1,0:T(8,128)S(1)} all-reduce(f32[32,128]{1,0:T(8,128)S(1)} %pad_maximum_fusion.5), channel_id=6, replica_groups=mesh['dp'=8,'tensor'=4] {'dp','tensor'}, use_global_device_ids=true, to_apply=%region_22.0.clone | all-reduce | flops 4096 | bytes 32768
  1004.2 21.1 %collective-permute-done.70 = bf16[128,2048]{1,0:T(8,128)(2,1)S(1)} collective-permute-done((bf16[128,2048]{1,0:T(8,128)(2,1)S(1)}, bf16[128,2048]{1,0:T(8,128)(2,1)S(1)}, u32[]{:S(2)}, u32[]{:S(2)}) %collective-permute-start.70) | collective-permute-done | bytes 524320 | tf_op jit(solution)/shard_map/ppermute | solution.py:47
  1050.1 45.2 %reduce-scatter.11.cloned.1.call-done = bf16[256,2048]{1,0:T(8,128)(2,1)} async-done(((bf16[2048,2048]{1,0:T(8,128)(2,1)}), bf16[256,2048]{1,0:T(8,128)(2,1)}) %reduce-scatter.11.cloned.1.call-update) | async-done | bytes 1048592 | tf_op jit(solution)/shard_map/reduce_scatter | solution.py:319
  (431 shorter events, 429.2 us)
Async XLA Ops:
  7.2 80.5 %all-gather.5.cloned.1.call-start = ((), (), s32[]{:S(2)}) async-start(), calls=%async_computation.4 | async-start | bytes 7077888 | tf_op jit(solution)/shard_map/all_gather | solution.py:315
  9.5 119.2 %all-gather.7.cloned.1.call-start = ((), (), s32[]{:S(2)}) async-start(), calls=%async_computation.5 | async-start | bytes 2359296 | tf_op jit(solution)/shard_map/all_gather | solution.py:315
  10.2 296.4 %all-gather.9.cloned.1.call-start = ((), (), s32[]{:S(2)}) async-start(), calls=%async_computation.6 | async-start | bytes 9437184 | tf_op jit(solution)/shard_map/all_gather | solution.py:315
  10.9 310.2 %all-gather.11.cloned.1.call-start = ((), (), s32[]{:S(2)}) async-start(), calls=%async_computation.7 | async-start | bytes 9437184 | tf_op jit(solution)/shard_map/all_gather | solution.py:315
  17.8 45.2 %collective-permute-start.4 = (bf16[256,2048]{1,0:T(8,128)(2,1)}, bf16[256,2048]{1,0:T(8,128)(2,1)S(1)}, u32[]{:S(2)}, u32[]{:S(2)}) collective-permute-start(bf16[256,2048]{1,0:T(8,128)(2,1)} %get-tuple-element.148), channel_id=1, source_target_pairs={{0,1},{1,0},{2,3},{3,2},{4,5},{5,4},{6,7},{7,6},{8,9},{9,8},{10,11... | collective-permute-start | bytes 3145736 | tf_op jit(solution)/shard_map/ppermute | solution.py:47
  18.3 46.8 %collective-permute-start.5 = (bf16[256,2048]{1,0:T(8,128)(2,1)}, bf16[256,2048]{1,0:T(8,128)(2,1)}, u32[]{:S(2)}, u32[]{:S(2)}) collective-permute-start(bf16[256,2048]{1,0:T(8,128)(2,1)} %get-tuple-element.148), channel_id=1, source_target_pairs={{0,2},{1,3},{2,0},{3,1},{4,6},{5,7},{6,4},{7,5},{8,10},{9,11},{10,... | collective-permute-start | bytes 3145736 | tf_op jit(solution)/shard_map/ppermute | solution.py:47
  18.3 840.2 %all-reduce.4.cloned.1.call-start = ((), (), s32[]{:S(2)}) async-start(), calls=%async_computation.12 | async-start | bytes 163840
  162.8 65.0 %collective-permute-start.11 = (bf16[128,2048]{1,0:T(8,128)(2,1)S(1)}, bf16[128,2048]{1,0:T(8,128)(2,1)S(1)}, u32[]{:S(2)}, u32[]{:S(2)}) collective-permute-start(bf16[128,2048]{1,0:T(8,128)(2,1)S(1)} %get-tuple-element.120), channel_id=1, source_target_pairs={{0,2},{1,3},{2,0},{3,1},{4,6},{5,7},{6,4},{7,5},{8,10},{9,11},{10,... | collective-permute-start | bytes 1572872 | tf_op jit(solution)/shard_map/ppermute | solution.py:47
  186.4 41.7 %collective-permute-start.27 = (bf16[128,2048]{1,0:T(8,128)(2,1)S(1)}, bf16[128,2048]{1,0:T(8,128)(2,1)S(1)}, u32[]{:S(2)}, u32[]{:S(2)}) collective-permute-start(bf16[128,2048]{1,0:T(8,128)(2,1)S(1)} %get-tuple-element.132), channel_id=1, source_target_pairs={{0,2},{1,3},{2,0},{3,1},{4,6},{5,7},{6,4},{7,5},{8,10},{9,11},{10,... | collective-permute-start | bytes 1572872 | tf_op jit(solution)/shard_map/ppermute | solution.py:47
  186.6 39.4 %collective-permute-start.26 = (bf16[128,2048]{1,0:T(8,128)(2,1)S(1)}, bf16[128,2048]{1,0:T(8,128)(2,1)S(1)}, u32[]{:S(2)}, u32[]{:S(2)}) collective-permute-start(bf16[128,2048]{1,0:T(8,128)(2,1)S(1)} %add_convert_fusion.19), channel_id=1, source_target_pairs={{0,2},{1,3},{2,0},{3,1},{4,6},{5,7},{6,4},{7,5},{8,10},{9,11},{10,... | collective-permute-start | bytes 1572872 | tf_op jit(solution)/shard_map/ppermute | solution.py:47
  243.0 46.0 %collective-permute-start.30 = (bf16[256,2048]{1,0:T(8,128)(2,1)}, bf16[256,2048]{1,0:T(8,128)(2,1)}, u32[]{:S(2)}, u32[]{:S(2)}) collective-permute-start(bf16[256,2048]{1,0:T(8,128)(2,1)} %get-tuple-element.161), channel_id=1, source_target_pairs={{0,1},{1,0},{2,3},{3,2},{4,5},{5,4},{6,7},{7,6},{8,9},{9,8},{10,11... | collective-permute-start | bytes 3145736 | tf_op jit(solution)/shard_map/ppermute | solution.py:47
  243.6 47.9 %collective-permute-start.31 = (bf16[256,2048]{1,0:T(8,128)(2,1)}, bf16[256,2048]{1,0:T(8,128)(2,1)}, u32[]{:S(2)}, u32[]{:S(2)}) collective-permute-start(bf16[256,2048]{1,0:T(8,128)(2,1)} %get-tuple-element.161), channel_id=1, source_target_pairs={{0,2},{1,3},{2,0},{3,1},{4,6},{5,7},{6,4},{7,5},{8,10},{9,11},{10,... | collective-permute-start | bytes 3145736 | tf_op jit(solution)/shard_map/ppermute | solution.py:47
  338.2 47.2 %collective-permute-start.18 = (bf16[128,2048]{1,0:T(8,128)(2,1)S(1)}, bf16[128,2048]{1,0:T(8,128)(2,1)S(1)}, u32[]{:S(2)}, u32[]{:S(2)}) collective-permute-start(bf16[128,2048]{1,0:T(8,128)(2,1)S(1)} %get-tuple-element.112), channel_id=1, source_target_pairs={{0,1},{1,0},{2,3},{3,2},{4,5},{5,4},{6,7},{7,6},{8,9},{9,8},{10,11... | collective-permute-start | bytes 1572872 | tf_op jit(solution)/shard_map/ppermute | solution.py:47
  339.1 47.7 %collective-permute-start.22 = (bf16[128,2048]{1,0:T(8,128)(2,1)S(1)}, bf16[128,2048]{1,0:T(8,128)(2,1)S(1)}, u32[]{:S(2)}, u32[]{:S(2)}) collective-permute-start(bf16[128,2048]{1,0:T(8,128)(2,1)S(1)} %get-tuple-element.113), channel_id=1, source_target_pairs={{0,2},{1,3},{2,0},{3,1},{4,6},{5,7},{6,4},{7,5},{8,10},{9,11},{10,... | collective-permute-start | bytes 1572872 | tf_op jit(solution)/shard_map/ppermute | solution.py:47
  373.0 50.9 %collective-permute-start.21 = (bf16[128,2048]{1,0:T(8,128)(2,1)S(1)}, bf16[128,2048]{1,0:T(8,128)(2,1)S(1)}, u32[]{:S(2)}, u32[]{:S(2)}) collective-permute-start(bf16[128,2048]{1,0:T(8,128)(2,1)S(1)} %get-tuple-element.114), channel_id=1, source_target_pairs={{0,2},{1,3},{2,0},{3,1},{4,6},{5,7},{6,4},{7,5},{8,10},{9,11},{10,... | collective-permute-start | bytes 1572872 | tf_op jit(solution)/shard_map/ppermute | solution.py:47
  386.8 37.4 %collective-permute-start.37 = (bf16[128,2048]{1,0:T(8,128)(2,1)S(1)}, bf16[128,2048]{1,0:T(8,128)(2,1)S(1)}, u32[]{:S(2)}, u32[]{:S(2)}) collective-permute-start(bf16[128,2048]{1,0:T(8,128)(2,1)S(1)} %get-tuple-element.126), channel_id=1, source_target_pairs={{0,2},{1,3},{2,0},{3,1},{4,6},{5,7},{6,4},{7,5},{8,10},{9,11},{10,... | collective-permute-start | bytes 1572872 | tf_op jit(solution)/shard_map/ppermute | solution.py:47
  444.4 45.4 %collective-permute-start.54 = (bf16[256,2048]{1,0:T(8,128)(2,1)S(1)}, bf16[256,2048]{1,0:T(8,128)(2,1)S(1)}, u32[]{:S(2)}, u32[]{:S(2)}) collective-permute-start(bf16[256,2048]{1,0:T(8,128)(2,1)S(1)} %get-tuple-element.73), channel_id=1, source_target_pairs={{0,1},{1,0},{2,3},{3,2},{4,5},{5,4},{6,7},{7,6},{8,9},{9,8},{10,11... | collective-permute-start | bytes 3145736 | tf_op jit(solution)/shard_map/ppermute | solution.py:47
  445.9 45.4 %collective-permute-start.55 = (bf16[256,2048]{1,0:T(8,128)(2,1)S(1)}, bf16[256,2048]{1,0:T(8,128)(2,1)S(1)}, u32[]{:S(2)}, u32[]{:S(2)}) collective-permute-start(bf16[256,2048]{1,0:T(8,128)(2,1)S(1)} %get-tuple-element.73), channel_id=1, source_target_pairs={{0,2},{1,3},{2,0},{3,1},{4,6},{5,7},{6,4},{7,5},{8,10},{9,11},{10,... | collective-permute-start | bytes 3145736 | tf_op jit(solution)/shard_map/ppermute | solution.py:47
  489.8 40.3 %collective-permute-start.56 = (bf16[128,2048]{1,0:T(8,128)(2,1)S(1)}, bf16[128,2048]{1,0:T(8,128)(2,1)S(1)}, u32[]{:S(2)}, u32[]{:S(2)}) collective-permute-start(bf16[128,2048]{1,0:T(8,128)(2,1)S(1)} %slice.606), channel_id=1, source_target_pairs={{0,2},{1,3},{2,0},{3,1},{4,6},{5,7},{6,4},{7,5},{8,10},{9,11},{10,... | collective-permute-start | bytes 1572872 | tf_op jit(solution)/shard_map/ppermute | solution.py:47
  491.3 39.7 %collective-permute-start.57 = (bf16[128,2048]{1,0:T(8,128)(2,1)S(1)}, bf16[128,2048]{1,0:T(8,128)(2,1)S(1)}, u32[]{:S(2)}, u32[]{:S(2)}) collective-permute-start(bf16[128,2048]{1,0:T(8,128)(2,1)S(1)} %slice.607), channel_id=1, source_target_pairs={{0,1},{1,0},{2,3},{3,2},{4,5},{5,4},{6,7},{7,6},{8,9},{9,8},{10,11... | collective-permute-start | bytes 1572872 | tf_op jit(solution)/shard_map/ppermute | solution.py:47
  529.2 38.9 %collective-permute-start.45 = (bf16[128,2048]{1,0:T(8,128)(2,1)S(1)}, bf16[128,2048]{1,0:T(8,128)(2,1)S(1)}, u32[]{:S(2)}, u32[]{:S(2)}) collective-permute-start(bf16[128,2048]{1,0:T(8,128)(2,1)S(1)} %get-tuple-element.103), channel_id=1, source_target_pairs={{0,1},{1,0},{2,3},{3,2},{4,5},{5,4},{6,7},{7,6},{8,9},{9,8},{10,11... | collective-permute-start | bytes 1572872 | tf_op jit(solution)/shard_map/ppermute | solution.py:47
  568.8 52.1 %collective-permute-start.47 = (bf16[128,2048]{1,0:T(8,128)(2,1)S(1)}, bf16[128,2048]{1,0:T(8,128)(2,1)S(1)}, u32[]{:S(2)}, u32[]{:S(2)}) collective-permute-start(bf16[128,2048]{1,0:T(8,128)(2,1)S(1)} %get-tuple-element.102), channel_id=1, source_target_pairs={{0,2},{1,3},{2,0},{3,1},{4,6},{5,7},{6,4},{7,5},{8,10},{9,11},{10,... | collective-permute-start | bytes 1572872 | tf_op jit(solution)/shard_map/ppermute | solution.py:47
  647.2 395.9 %reduce-scatter.7.cloned.1.call-start = ((), (), s32[]{:S(2)}) async-start(), calls=%async_computation.9 | async-start | bytes 2359296 | tf_op jit(solution)/shard_map/reduce_scatter | solution.py:319
  729.4 315.5 %reduce-scatter.5.cloned.1.call-start = ((), (), s32[]{:S(2)}) async-start(), calls=%async_computation.8 | async-start | bytes 7077888 | tf_op jit(solution)/shard_map/reduce_scatter | solution.py:319
  790.4 256.8 %reduce-scatter.9.cloned.1.call-start = ((), (), s32[]{:S(2)}) async-start(), calls=%async_computation.10 | async-start | bytes 9437184 | tf_op jit(solution)/shard_map/reduce_scatter | solution.py:319
  820.6 274.6 %reduce-scatter.11.cloned.1.call-start = ((), (), s32[]{:S(2)}) async-start(), calls=%async_computation.11 | async-start | bytes 9437184 | tf_op jit(solution)/shard_map/reduce_scatter | solution.py:319
  872.3 104.4 %collective-permute-start.75 = (bf16[128,2048]{1,0:T(8,128)(2,1)}, bf16[128,2048]{1,0:T(8,128)(2,1)S(1)}, u32[]{:S(2)}, u32[]{:S(2)}) collective-permute-start(bf16[128,2048]{1,0:T(8,128)(2,1)} %get-tuple-element.97), channel_id=1, source_target_pairs={{0,1},{1,0},{2,3},{3,2},{4,5},{5,4},{6,7},{7,6},{8,9},{9,8},{10,11... | collective-permute-start | bytes 1572872 | tf_op jit(solution)/shard_map/ppermute | solution.py:47
  872.5 109.5 %collective-permute-start.74 = (bf16[128,2048]{1,0:T(8,128)(2,1)}, bf16[128,2048]{1,0:T(8,128)(2,1)}, u32[]{:S(2)}, u32[]{:S(2)}) collective-permute-start(bf16[128,2048]{1,0:T(8,128)(2,1)} %get-tuple-element.94), channel_id=1, source_target_pairs={{0,1},{1,0},{2,3},{3,2},{4,5},{5,4},{6,7},{7,6},{8,9},{9,8},{10,11... | collective-permute-start | bytes 1572872 | tf_op jit(solution)/shard_map/ppermute | solution.py:47
  874.3 109.3 %collective-permute-start.78 = (bf16[128,2048]{1,0:T(8,128)(2,1)}, bf16[128,2048]{1,0:T(8,128)(2,1)}, u32[]{:S(2)}, u32[]{:S(2)}) collective-permute-start(bf16[128,2048]{1,0:T(8,128)(2,1)} %get-tuple-element.95), channel_id=1, source_target_pairs={{0,2},{1,3},{2,0},{3,1},{4,6},{5,7},{6,4},{7,5},{8,10},{9,11},{10,... | collective-permute-start | bytes 1572872 | tf_op jit(solution)/shard_map/ppermute | solution.py:47
  875.5 152.6 %collective-permute-start.77 = (bf16[128,2048]{1,0:T(8,128)(2,1)S(1)}, bf16[128,2048]{1,0:T(8,128)(2,1)S(1)}, u32[]{:S(2)}, u32[]{:S(2)}) collective-permute-start(bf16[128,2048]{1,0:T(8,128)(2,1)S(1)} %get-tuple-element.96), channel_id=1, source_target_pairs={{0,2},{1,3},{2,0},{3,1},{4,6},{5,7},{6,4},{7,5},{8,10},{9,11},{10,... | collective-permute-start | bytes 1572872 | tf_op jit(solution)/shard_map/ppermute | solution.py:47
  886.5 93.7 %collective-permute-start.69 = (bf16[128,2048]{1,0:T(8,128)(2,1)}, bf16[128,2048]{1,0:T(8,128)(2,1)S(1)}, u32[]{:S(2)}, u32[]{:S(2)}) collective-permute-start(bf16[128,2048]{1,0:T(8,128)(2,1)} %get-tuple-element.91), channel_id=1, source_target_pairs={{0,1},{1,0},{2,3},{3,2},{4,5},{5,4},{6,7},{7,6},{8,9},{9,8},{10,11... | collective-permute-start | bytes 1572872 | tf_op jit(solution)/shard_map/ppermute | solution.py:47
  983.5 45.8 %collective-permute-start.71 = (bf16[128,2048]{1,0:T(8,128)(2,1)}, bf16[128,2048]{1,0:T(8,128)(2,1)S(1)}, u32[]{:S(2)}, u32[]{:S(2)}) collective-permute-start(bf16[128,2048]{1,0:T(8,128)(2,1)} %get-tuple-element.90), channel_id=1, source_target_pairs={{0,2},{1,3},{2,0},{3,1},{4,6},{5,7},{6,4},{7,5},{8,10},{9,11},{10,... | collective-permute-start | bytes 1572872 | tf_op jit(solution)/shard_map/ppermute | solution.py:47
  (100 other events, 2144.2 us)
Sparse Core Ops, SparseCore 0:
  10.2 67.4 all-gather.4
  79.3 27.7 all-gather.6
  108.7 81.4 all-gather.8
  191.6 80.5 all-gather.10
  647.3 155.1 all-reduce.3
  804.7 38.1 reduce-scatter.6
  845.2 68.2 reduce-scatter.4
  915.8 89.0 reduce-scatter.8
  1007.2 87.9 reduce-scatter.10

commit v2 on v1

--- a/solution.py
+++ b/solution.py
@@ -47,39 +47,53 @@
     return lax.ppermute(value, "tensor", [(i, i ^ bits) for i in range(size)])
 
 
-def gather_rows(own):
+def after(value, *others):
+    return lax.optimization_barrier((value, *others))[0]
+
+
+def gather_near(own):
     size = lax.axis_size("tensor")
     if size != 4:
-        return jnp.concatenate([own] + [swap(own, p) for p in range(1, size)], axis=0)
-    half = own.shape[0] // 2
-    first, second = swap(own, 1), swap(own, 2)
-    return jnp.concatenate(
-        [own, first, second, swap(first[:half], 2), swap(second[half:], 1)], axis=0
-    )
-
-
-def scatter_sum(terms):
+        return [own] + [swap(own, p) for p in range(1, size)]
+    return [own, swap(own, 1), swap(own, 2)]
+
+
+def gather_far(near, *others):
+    if lax.axis_size("tensor") != 4:
+        return jnp.concatenate(near, axis=0)
+    half = near[0].shape[0] // 2
+    upper, lower = after(near[1][:half], *others), after(near[2][half:], *others)
+    return jnp.concatenate(near + [swap(upper, 2), swap(lower, 1)], axis=0)
+
+
+def scatter_near(terms):
     size = lax.axis_size("tensor")
     rows = terms.shape[0] // size
     block = [terms[p * rows : (p + 1) * rows] for p in range(size)]
     if size != 4:
-        total = wide(block[0])
-        for p in range(1, size):
-            total = total + wide(swap(block[p], p))
-        return total
+        return block, [swap(block[p], p) for p in range(1, size)]
     half = rows // 2
-    upper = [b[:half] for b in block]
-    lower = [b[half:] for b in block]
-    relay_upper = swap(upper[3], 1)
-    relay_lower = swap(lower[3], 2)
-    direct_upper = swap(upper[1], 1)
-    direct_lower = swap(lower[2], 2)
-    sum_upper = swap(low(wide(relay_upper) + wide(upper[2])), 2)
-    sum_lower = swap(low(wide(relay_lower) + wide(lower[1])), 1)
+    return block, [
+        swap(block[3][:half], 1),
+        swap(block[3][half:], 2),
+        swap(block[1][:half], 1),
+        swap(block[2][half:], 2),
+    ]
+
+
+def scatter_far(near, *others):
+    block, came = near
+    if lax.axis_size("tensor") != 4:
+        return add_up([wide(block[0])] + [wide(c) for c in came])
+    half = block[0].shape[0] // 2
+    upper = low(wide(came[0]) + wide(block[2][:half]))
+    lower = low(wide(came[1]) + wide(block[1][half:]))
+    sum_upper = swap(after(upper, *others), 2)
+    sum_lower = swap(after(lower, *others), 1)
     return jnp.concatenate(
         [
-            wide(upper[0]) + wide(direct_upper) + wide(sum_upper),
-            wide(lower[0]) + wide(direct_lower) + wide(sum_lower),
+            wide(block[0][:half]) + wide(came[2]) + wide(sum_upper),
+            wide(block[0][half:]) + wide(came[3]) + wide(sum_lower),
         ],
         axis=0,
     )
@@ -300,13 +314,29 @@
 
 
 def total_of(vectors):
-    devices = lax.axis_size("dp") * lax.axis_size("tensor")
-    packed = jnp.concatenate([v.reshape(devices, -1) for v in vectors], axis=1)
-    packed = lax.psum_scatter(packed, ("dp", "tensor"), scatter_dimension=0, tiled=True)[0]
-    sizes = [v.shape[0] // devices for v in vectors]
+    slots, groups = lax.axis_size("dp"), lax.axis_size("tensor")
+    slot, position = lax.axis_index("dp"), lax.axis_index("tensor")
+    packed = jnp.concatenate([v.reshape(slots, groups, -1) for v in vectors], axis=2)
+
+    def share(p):
+        return lax.dynamic_index_in_dim(packed, position ^ p, 1, keepdims=False)
+
+    total = add_up([share(0)] + [swap(share(p), p) for p in range(1, groups)])
+
+    def ahead(step):
+        return lax.dynamic_index_in_dim(total, (slot + step) % slots, 0, keepdims=False)
+
+    total = add_up(
+        [ahead(0)]
+        + [
+            lax.ppermute(ahead(step), "dp", [(i, (i + step) % slots) for i in range(slots)])
+            for step in range(1, slots)
+        ]
+    )
     parts, at = [], 0
-    for size in sizes:
-        parts.append(packed[at : at + size])
+    for v in vectors:
+        size = v.shape[0] // (slots * groups)
+        parts.append(total[at : at + size])
         at += size
     return parts
 
@@ -316,7 +346,7 @@
 
 
 def scatter_weight(grad):
-    return wide(lax.psum_scatter(low(grad), "dp", scatter_dimension=0, tiled=True))
+    return lax.psum_scatter(grad, "dp", scatter_dimension=0, tiled=True)
 
 
 def add_up(terms):
@@ -377,60 +407,109 @@
     up_full = gather_weight(up_weight)
     down_full = gather_weight(down_weight)
 
-    seq_tokens = [gather_rows(tokens[cut[c]]) for c in every]
-    projected = [low(nn(seq_tokens[c], proj_full) + bias_proj) for c in every]
-    context, lse, mid, unit1, inverse1, mid_low = ([None] * CHUNKS for _ in range(6))
-    for c in every:
-        context[c], lse[c] = attend(c, projected, limits, part)
-    for c in every:
-        attn_sum = scatter_sum(low(nt(context[c], out_full)))
+    def lists(count):
+        return ([None] * CHUNKS for _ in range(count))
+
+    near, seq_tokens, projected = lists(3)
+    for c in every:
+        near[c] = gather_near(after(tokens[cut[c]], *(near[c - 1] if c else ())))
+    for c in every:
+        seq_tokens[c] = gather_far(near[c])
+        projected[c] = low(nn(seq_tokens[c], proj_full) + bias_proj)
+    context, lse, attn_low = lists(3)
+    for c in every:
+        queries = projected if c == 0 else [after(p, attn_low[c - 1]) for p in projected]
+        context[c], lse[c] = attend(c, queries, limits, part)
+        attn_low[c] = low(nt(context[c], out_full))
+        near[c] = scatter_near(attn_low[c])
+    mid, mid_out, unit1, inverse1, mid_near = lists(5)
+    before = attn_low[-1]
+    for c in every:
+        attn_sum = scatter_far(near[c], before)
         mid[c], unit1[c], inverse1[c] = norm_rows(
             wide(tokens[cut[c]]) + attn_sum + out_bias, norm1_gain, norm1_shift
         )
-    mid_seq = [gather_rows(low(mid[c])) for c in every]
-    activ, slope = ([None] * CHUNKS for _ in range(2))
-    ffn_sum = [None] * CHUNKS
-    for c in every:
-        activ[c], slope[c] = gate_and_slope(nn(mid_seq[c], up_full) + bias_up)
-        ffn_sum[c] = scatter_sum(low(nt(activ[c], down_full)))
-    layer_out, grad_sum2, vec2 = ([None] * CHUNKS for _ in range(3))
-    for c in every:
-        final, unit2, inverse2 = norm_rows(mid[c] + ffn_sum[c] + down_bias, norm2_gain, norm2_shift)
+        before = mid_out[c] = low(mid[c])
+    for c in every:
+        mid_near[c] = gather_near(after(mid_out[c], *(mid_near[c - 1] if c else ())))
+    mid_seq, activ, slope, ffn_low, ffn_near = lists(5)
+    before = mid_out[-1]
+    for c in every:
+        mid_seq[c] = gather_far(mid_near[c], before)
+        source = mid_seq[c] if c == 0 else after(mid_seq[c], ffn_low[c - 1])
+        activ[c], slope[c] = gate_and_slope(nn(source, up_full) + bias_up)
+        ffn_low[c] = low(nt(activ[c], down_full))
+        ffn_near[c] = scatter_near(ffn_low[c])
+        before = activ[c]
+    layer_out, grad_sum2, grad_out2, vec2, grad_near = lists(5)
+    before = ffn_low[-1]
+    for c in every:
+        ffn_sum = scatter_far(ffn_near[c], before)
+        final, unit2, inverse2 = norm_rows(mid[c] + ffn_sum + down_bias, norm2_gain, norm2_shift)
         layer_out[c] = low(final * row_live[cut[c]])
         grad_final = wide(cotangent[cut[c]]) * row_live[cut[c]]
         grad_sum2[c], gain_part, shift_part = norm_back(grad_final, unit2, inverse2, norm2_gain)
         vec2[c] = (gain_part, shift_part, jnp.sum(grad_sum2[c], axis=0))
-    grad_ffn = [gather_rows(low(grad_sum2[c])) for c in every]
-    grad_pre = [low(nn(grad_ffn[c], down_full) * wide(slope[c])) for c in every]
-    mid_sum = [scatter_sum(low(nt(grad_pre[c], up_full))) for c in every]
-    grad_sum1, vec1 = ([None] * CHUNKS for _ in range(2))
-    for c in every:
+        before = grad_out2[c] = low(grad_sum2[c])
+    for c in every:
+        grad_near[c] = gather_near(after(grad_out2[c], *(grad_near[c - 1] if c else ())))
+    grad_ffn, grad_pre, mid_low, mid_back = lists(4)
+    before = grad_out2[-1]
+    for c in every:
+        grad_ffn[c] = gather_far(grad_near[c], before)
+        source = grad_ffn[c] if c == 0 else after(grad_ffn[c], mid_low[c - 1])
+        grad_pre[c] = low(nn(source, down_full) * wide(slope[c]))
+        mid_low[c] = low(nt(grad_pre[c], up_full))
+        mid_back[c] = scatter_near(mid_low[c])
+        before = grad_pre[c]
+    early = (mid_low[-1], *mid_back[0][1])
+    down_grad = low(add_up([tn(after(grad_ffn[c], *early), activ[c]) for c in every]))
+    down_part = scatter_weight(down_grad)
+    up_bias_part = add_up([jnp.sum(wide(grad_pre[c]), axis=0) for c in every])
+
+    grad_sum1, grad_out1, vec1, attn_near = lists(4)
+    before = (mid_low[-1],)
+    for c in every:
+        mid_sum = scatter_far(mid_back[c], *before)
         grad_sum1[c], gain_part, shift_part = norm_back(
-            grad_sum2[c] + mid_sum[c], unit1[c], inverse1[c], norm1_gain
+            grad_sum2[c] + mid_sum, unit1[c], inverse1[c], norm1_gain
         )
         vec1[c] = (gain_part, shift_part, jnp.sum(grad_sum1[c], axis=0))
-    grad_attn = [gather_rows(low(grad_sum1[c])) for c in every]
-
-    down_part = scatter_weight(add_up([tn(grad_ffn[c], activ[c]) for c in every]))
-    up_part = scatter_weight(add_up([tn(mid_seq[c], grad_pre[c]) for c in every]))
-    out_part = scatter_weight(add_up([tn(grad_attn[c], context[c]) for c in every]))
-    up_bias_part = add_up([jnp.sum(wide(grad_pre[c]), axis=0) for c in every])
-
-    grad_query, carry = [None] * CHUNKS, None
-    for c in every:
-        grad_context = low(nn(grad_attn[c], out_full))
+        grad_out1[c] = low(grad_sum1[c])
+        before = (grad_out1[c], down_grad)
+    up_grad = low(add_up([tn(after(mid_seq[c], grad_out1[0]), grad_pre[c]) for c in every]))
+    up_part = scatter_weight(up_grad)
+    for c in every:
+        attn_near[c] = gather_near(after(grad_out1[c], *(attn_near[c - 1] if c else ())))
+    grad_attn, grad_query = lists(2)
+    carry = None
+    before = (grad_out1[-1],)
+    for c in every:
+        grad_attn[c] = gather_far(attn_near[c], *before)
+        source = after(grad_attn[c], grad_query[c - 1] if c else up_grad)
+        grad_context = low(nn(source, out_full))
         grad_query[c], *carry = attend_back(
             c, projected, context[c], grad_context, lse[c], limits, part, carry
         )
+        before = (grad_query[c], down_part)
+    out_grad = low(add_up([tn(grad_attn[c], context[c]) for c in every]))
+    out_part = scatter_weight(out_grad)
     size = part * groups
     grad_proj = [
         jnp.concatenate([grad_query[c]] + [a[c * size : (c + 1) * size] for a in carry], axis=1)
         for c in every
     ]
-    proj_part = scatter_weight(add_up([tn(seq_tokens[c], grad_proj[c]) for c in every]))
-    tokens_grad = [
-        low(grad_sum1[c] + scatter_sum(low(nt(grad_proj[c], proj_full)))) for c in every
-    ]
+    proj_grad = low(add_up([tn(seq_tokens[c], grad_proj[c]) for c in every]))
+    proj_part = scatter_weight(proj_grad)
+    tokens_low, tokens_near, tokens_grad = lists(3)
+    for c in every:
+        tokens_low[c] = low(nt(after(grad_proj[c], proj_grad, up_part), proj_full))
+        tokens_near[c] = scatter_near(tokens_low[c])
+    before = (tokens_low[-1],)
+    for c in every:
+        tokens_grad[c] = low(grad_sum1[c] + scatter_far(tokens_near[c], *before))
+        before = (out_part,)
+    proj_part, out_part, up_part, down_part = map(wide, (proj_part, out_part, up_part, down_part))
     proj_bias = add_up([jnp.sum(wide(grad_proj[c]), axis=0) for c in every])
     (
         norm2_gain_grad,
@@ -440,13 +519,13 @@
         norm1_shift_grad,
         out_bias_grad,
         up_bias_grad,
+        query_bias_grad,
+        value_bias_grad,
     ) = total_of(
         [add_up([vec2[c][i] for c in every]) for i in range(3)]
         + [add_up([vec1[c][i] for c in every]) for i in range(3)]
-        + [placed(up_bias_part, hid_start, FF)]
-    )
-    query_bias_grad, value_bias_grad = total_of(
-        [
+        + [
+            placed(up_bias_part, hid_start, FF),
             placed(proj_bias[:head_cols], col_start, width),
             placed(proj_bias[2 * head_cols :], col_start, width),
         ]

time: 1110 us -> 985 us (0.89)
  blocking collectives: 87.4 us -> 0 us
  waiting for transfers between devices: 430 us -> 368 us
  starting transfers between devices: 91.4 us -> 124 us
  matrix products: 282 us -> 261 us
    unnamed x1 -> x0, blocking collectives: 87.4 us -> none
    reduce_scatter x4, waiting for transfers between devices: 45.2 us -> 0.01 us  [scatter_weight(): return lax.psum_scatter(grad, 'dp', scatter_dimension=0, tiled=True)]
    ppermute x0 -> x7, starting transfers between devices: none -> 30 us  [total_of(): lax.ppermute(ahead(step), 'dp', [(i, (i + step) % slots) for i in range(s...]
    ppermute x80 -> x83, waiting for transfers between devices: 383 us -> 365 us  [swap(): return lax.ppermute(value, 'tensor', [(i, i ^ bits) for i in range(size)])]
    unnamed x111 -> x187, local copies, waits for them, and re-layouts: 26.5 us -> 32.3 us
    ppermute x80 -> x83, starting transfers between devices: 91 us -> 92.6 us  [swap(): return lax.ppermute(value, 'tensor', [(i, i ^ bits) for i in range(size)])]
  transfers between devices with their start and end apart: 89 -> 98, of which waited for: 36 -> 51; matrix products, arithmetic and copies ran while one was open for 31% -> 33% of each run, Pallas kernels for 9% -> 10%
where the time goes in v2:
time: 985 us; the launch traced here: 978 us
  waiting for transfers between devices  368 us (37%)
  matrix products  261 us (26%)
  starting transfers between devices  124 us (13%)
  Pallas kernels  93.8 us (10%)
  local copies, waits for them, and re-layouts  58.7 us (6%)
  other arithmetic  56.1 us (6%)
  between operations  16.8 us (2%)
    ppermute x83, waiting for transfers between devices, swap(): return lax.ppermute(value, 'tensor', [(i, i ^ bits) for i in range(size)])  365 us
    ppermute x83, starting transfers between devices, swap(): return lax.ppermute(value, 'tensor', [(i, i ^ bits) for i in range(size)])  92.6 us
    dot_general x8, matrix products, nn(): lax.dot_general(left, right, (((1,), (0,)), ((), ())), preferred_element_...  91.8 us
    dot_general x8, matrix products, tn(): lax.dot_general(left, right, (((0,), (0,)), ((), ())), preferred_element_...  90.3 us
    dot_general x8, matrix products, nt(): lax.dot_general(left, right, (((1,), (1,)), ((), ())), preferred_element_...  79.2 us
    pallas_call x2, Pallas kernels, attend_back(): pl.pallas_call(kernel, out_shape=(jax.ShapeDtypeStruct((part, cols), jnp....  54 us
    pallas_call x2, Pallas kernels, attend(): pl.pallas_call(kernel, out_shape=(jax.ShapeDtypeStruct((part, cols), jnp....  39.8 us
    unnamed x187, local copies, waits for them, and re-layouts  32.3 us
  transfers between devices with their start and end apart: 98, of which 51 were waited for; matrix products, arithmetic and copies ran while one was open for 33% of the time, Pallas kernels for 10%

profile of v2, /device:TPU:0, one launch (start us, length us, event | category | flops | bytes accessed | tf_op | source)
XLA Modules:
  0.0 978.1 jit_solution(606078038673838098)
XLA Ops:
  20.9 17.7 %collective-permute-done.1 = bf16[256,2048]{1,0:T(8,128)(2,1)} collective-permute-done((bf16[256,2048]{1,0:T(8,128)(2,1)}, bf16[256,2048]{1,0:T(8,128)(2,1)}, u32[]{:S(2)}, u32[]{:S(2)}) %collective-permute-start.1) | collective-permute-done | bytes 1048608 | tf_op jit(solution)/shard_map/ppermute | solution.py:47
  50.2 26.2 %collective-permute-done.2 = bf16[128,2048]{1,0:T(8,128)(2,1)S(1)} collective-permute-done((bf16[128,2048]{1,0:T(8,128)(2,1)S(1)}, bf16[128,2048]{1,0:T(8,128)(2,1)S(1)}, u32[]{:S(2)}, u32[]{:S(2)}) %collective-permute-start.2) | collective-permute-done | bytes 524320 | tf_op jit(solution)/shard_map/ppermute | solution.py:47
  89.8 11.4 %add_convert_fusion.5.rest_1_.rest_3_.q_ref = bf16[1024,1536]{1,0:T(8,128)(2,1)} fusion(bf16[1024,2048]{1,0:T(8,128)(2,1)} %constant_dynamic-update-slice_fusion.5, bf16[2048,1536]{1,0:T(8,128)(2,1)} %all-gather.5.cloned.1.call-done, f32[1536]{0:T(1024)S(1)} %pad_maximum_fusion.5), kind=kOutput, calls=%fused_computation.21 | convolution fusion | flops 6445596672 | bytes 13637632 | tf_op jit(solution)/shard_map/dot_general | solution.py:26
  109.2 19.7 %attend.2 = (bf16[1024,512]{1,0:T(8,128)(2,1)}, f32[4,1,1024]{2,1,0:T(1,128)}) custom-call(s32[8]{0:T(128)} %stack.35.lim, bf16[1024,1536]{1,0:T(8,128)(2,1)} %add_convert_fusion.6.q_ref.rest_0_.rest_2_, bf16[1024,1536]{1,0:T(8,128)(2,1)} %add_convert_fusion.6.q_ref.rest_0_.rest_2_, bf16[1024,1536]{1,0:T(8,128)(2,1)} %add_convert_fusion.5.rest_1_.rest_3_.q_ref, ...), custom_call_target="tpu_custom_call" | custom-call | flops 8589934592 | bytes 6291456 | tf_op jit(solution)/shard_map/attend/pallas_call | solution.py:154
  137.6 20.1 %attend.3 = (bf16[1024,512]{1,0:T(8,128)(2,1)}, f32[4,1,1024]{2,1,0:T(1,128)}) custom-call(s32[8]{0:T(128)} %stack.35.lim, bf16[1024,1536]{1,0:T(8,128)(2,1)} %add_convert_fusion.5.rest_1_.rest_3_.q_ref, bf16[1024,1536]{1,0:T(8,128)(2,1)} %add_convert_fusion.6.q_ref.rest_0_.rest_2_, bf16[1024,1536]{1,0:T(8,128)(2,1)} %add_convert_fusion.5.rest_1_.rest_3_.q_ref, ...), custom_call_target="tpu_custom_call" | custom-call | flops 8589934592 | bytes 6291456 | tf_op jit(solution)/shard_map/attend/pallas_call | solution.py:154
  165.6 11.3 %collective-permute-done.10 = bf16[128,2048]{1,0:T(8,128)(2,1)S(1)} collective-permute-done((bf16[128,2048]{1,0:T(8,128)(2,1)S(1)}, bf16[128,2048]{1,0:T(8,128)(2,1)S(1)}, u32[]{:S(2)}, u32[]{:S(2)}) %collective-permute-start.10) | collective-permute-done | bytes 524320 | tf_op jit(solution)/shard_map/ppermute | solution.py:47
  199.4 11.2 %collective-permute-done.18 = bf16[128,2048]{1,0:T(8,128)(2,1)S(1)} collective-permute-done((bf16[128,2048]{1,0:T(8,128)(2,1)S(1)}, bf16[128,2048]{1,0:T(8,128)(2,1)S(1)}, u32[]{:S(2)}, u32[]{:S(2)}) %collective-permute-start.18) | collective-permute-done | bytes 524320 | tf_op jit(solution)/shard_map/ppermute | solution.py:47
  256.5 10.7 %collective-permute-done.23 = bf16[128,2048]{1,0:T(8,128)(2,1)S(1)} collective-permute-done((bf16[128,2048]{1,0:T(8,128)(2,1)S(1)}, bf16[128,2048]{1,0:T(8,128)(2,1)S(1)}, u32[]{:S(2)}, u32[]{:S(2)}) %collective-permute-start.23) | collective-permute-done | bytes 524320 | tf_op jit(solution)/shard_map/ppermute | solution.py:47
  268.0 16.9 %multiply_convert_fusion.3 = (bf16[1024,2048]{1,0:T(8,128)(2,1)}, f32[1024,2048]{1,0:T(8,128)}) fusion(f32[2048]{0:T(1024)S(1)} %dynamic_slice.49, bf16[1024,2048]{1,0:T(8,128)(2,1)} %constant_dynamic-update-slice_fusion.10, bf16[2048,2048]{1,0:T(8,128)(2,1)} %all-gather.9.cloned.1.call-done), kind=kOutput, calls=%fused_computation.17 | convolution fusion | flops 8610906112 | bytes 25174016 | tf_op jit(solution)/shard_map/dot_general | solution.py:26
  284.9 12.6 %convolution_convert_fusion.5 = bf16[1024,2048]{1,0:T(8,128)(2,1)S(1)} fusion(bf16[1024,2048]{1,0:T(8,128)(2,1)} %get-tuple-element.244, bf16[2048,2048]{1,0:T(8,128)(2,1)} %all-gather.11.cloned.1.call-done), kind=kOutput, calls=%fused_computation.29 | convolution fusion | flops 8592031744 | bytes 16777216 | tf_op jit(solution)/shard_map/dot_general | solution.py:20
  323.6 11.1 %fusion.48 = f32[1024,2048]{1,0:T(8,128)} fusion(bf16[1024,2048]{1,0:T(8,128)(2,1)S(1)} %constant_dynamic-update-slice_fusion.15, bf16[2048,2048]{1,0:T(8,128)(2,1)S(1)} %bitcast.83), kind=kOutput, calls=%fused_computation.225 | convolution fusion | flops 8589934592 | bytes 20971520 | tf_op jit(solution)/shard_map/dot_general | solution.py:26
  334.7 15.7 %convolution_convert_fusion.4 = bf16[1024,2048]{1,0:T(8,128)(2,1)S(1)} fusion(bf16[2048,2048]{1,0:T(8,128)(2,1)} %all-gather.11.cloned.1.call-done, f32[1024,2048]{1,0:T(8,128)} %fusion.48, f32[2048]{0:T(1024)S(1)} %dynamic_slice.49), kind=kOutput, calls=%fused_computation.28 | convolution fusion | flops 8613003264 | bytes 20979712 | tf_op jit(solution)/shard_map/dot_general | solution.py:20
  384.0 11.2 %collective-permute-done.36 = bf16[128,2048]{1,0:T(8,128)(2,1)S(1)} collective-permute-done((bf16[128,2048]{1,0:T(8,128)(2,1)S(1)}, bf16[128,2048]{1,0:T(8,128)(2,1)S(1)}, u32[]{:S(2)}, u32[]{:S(2)}) %collective-permute-start.36) | collective-permute-done | bytes 524320 | tf_op jit(solution)/shard_map/ppermute | solution.py:47
  412.2 14.0 %collective-permute-done.41 = bf16[256,2048]{1,0:T(8,128)(2,1)S(1)} collective-permute-done((bf16[256,2048]{1,0:T(8,128)(2,1)S(1)}, bf16[256,2048]{1,0:T(8,128)(2,1)S(1)}, u32[]{:S(2)}, u32[]{:S(2)}) %collective-permute-start.41) | collective-permute-done | bytes 1048608 | tf_op jit(solution)/shard_map/ppermute | solution.py:47
  430.8 21.4 %collective-permute-done.42 = bf16[128,2048]{1,0:T(8,128)(2,1)S(1)} collective-permute-done((bf16[128,2048]{1,0:T(8,128)(2,1)S(1)}, bf16[128,2048]{1,0:T(8,128)(2,1)S(1)}, u32[]{:S(2)}, u32[]{:S(2)}) %collective-permute-start.42) | collective-permute-done | bytes 524320 | tf_op jit(solution)/shard_map/ppermute | solution.py:47
  454.2 20.3 %convert_reduce_fusion.1 = (f32[2048]{0:T(1024)}, bf16[1024,2048]{1,0:T(8,128)(2,1)}) fusion(f32[1024,2048]{1,0:T(8,128)} %get-tuple-element.245, f32[2048]{0:T(1024)S(1)} %dynamic_slice.49, bf16[1024,2048]{1,0:T(8,128)(2,1)} %copy-done.31, bf16[2048,2048]{1,0:T(8,128)(2,1)} %all-gather.11.cloned.1.call-done), kind=kOutput, calls=%fused_computation.10 | convolution fusion | flops 8638167040 | bytes 25182208 | tf_op jit(solution)/shard_map/dot_general | solution.py:26
  474.5 10.7 %convolution_convert_fusion.3 = bf16[1024,2048]{1,0:T(8,128)(2,1)S(1)} fusion(bf16[1024,2048]{1,0:T(8,128)(2,1)} %get-tuple-element.247, bf16[2048,2048]{1,0:T(8,128)(2,1)S(1)} %bitcast.85), kind=kOutput, calls=%fused_computation.27 | convolution fusion | flops 8592031744 | bytes 16777216 | tf_op jit(solution)/shard_map/dot_general | solution.py:20
  506.6 17.4 %convert_reduce_fusion = (f32[2048]{0:T(1024)}, bf16[1024,2048]{1,0:T(8,128)(2,1)S(1)}) fusion(f32[1024,2048]{1,0:T(8,128)} %fusion.48, f32[2048]{0:T(1024)S(1)} %dynamic_slice.49, bf16[1024,2048]{1,0:T(8,128)(2,1)S(1)} %constant_dynamic-update-slice_fusion.25, bf16[2048,2048]{1,0:T(8,128)(2,1)} %all-gather.11.cloned.1.call-done), kind=kOutput, calls=%fused_computation.9 | convolution fusion | flops 8638167040 | bytes 25182208 | tf_op jit(solution)/shard_map/dot_general | solution.py:26
  525.9 12.6 %convolution_convert_fusion.2 = bf16[1024,2048]{1,0:T(8,128)(2,1)} fusion(bf16[1024,2048]{1,0:T(8,128)(2,1)S(1)} %get-tuple-element.249, bf16[2048,2048]{1,0:T(8,128)(2,1)} %all-gather.9.cloned.1.call-done), kind=kOutput, calls=%fused_computation.26 | convolution fusion | flops 8592031744 | bytes 16777216 | tf_op jit(solution)/shard_map/dot_general | solution.py:20
  539.5 16.0 %fusion.21 = f32[2048,2048]{1,0:T(8,128)} fusion(bf16[1024,2048]{1,0:T(8,128)(2,1)S(1)} %constant_dynamic-update-slice_fusion.25, f32[1024,2048]{1,0:T(8,128)} %fusion.48, f32[2048]{0:T(1024)S(1)} %dynamic_slice.49), kind=kOutput, calls=%fused_computation.202 | convolution fusion | flops 8610906112 | bytes 29368320 | tf_op jit(solution)/shard_map/dot_general | solution.py:32
  555.5 15.8 %add_convert_fusion.1 = bf16[2048,2048]{1,0:T(8,128)(2,1)} fusion(f32[2048,2048]{1,0:T(8,128)} %fusion.21, bf16[1024,2048]{1,0:T(8,128)(2,1)S(1)} %copy-done.32, bf16[1024,2048]{1,0:T(8,128)(2,1)} %get-tuple-element.244), kind=kOutput, calls=%fused_computation.1 | convolution fusion | flops 8598323200 | bytes 33554432 | tf_op jit(solution)/shard_map/dot_general | solution.py:32
  600.9 11.8 %fusion.49 = f32[2048,2048]{1,0:T(8,128)} fusion(bf16[1024,2048]{1,0:T(8,128)(2,1)S(1)} %copy-done.37, bf16[1024,2048]{1,0:T(8,128)(2,1)S(1)} %copy-done.70), kind=kOutput, calls=%fused_computation.226 | convolution fusion | flops 8589934592 | bytes 25165824 | tf_op jit(solution)/shard_map/dot_general | solution.py:32
  612.8 15.9 %add_convert_fusion = bf16[2048,2048]{1,0:T(8,128)(2,1)} fusion(f32[2048,2048]{1,0:T(8,128)} %fusion.49, bf16[1024,2048]{1,0:T(8,128)(2,1)} %constant_dynamic-update-slice_fusion.10, bf16[1024,2048]{1,0:T(8,128)(2,1)S(1)} %copy-done.71), kind=kOutput, calls=%fused_computation | convolution fusion | flops 8598323200 | bytes 33554432 | tf_op jit(solution)/shard_map/dot_general | solution.py:32
  633.6 12.3 %collective-permute-done.57 = bf16[128,2048]{1,0:T(8,128)(2,1)S(1)} collective-permute-done((bf16[128,2048]{1,0:T(8,128)(2,1)S(1)}, bf16[128,2048]{1,0:T(8,128)(2,1)S(1)}, u32[]{:S(2)}, u32[]{:S(2)}) %collective-permute-start.57) | collective-permute-done | bytes 524320 | tf_op jit(solution)/shard_map/ppermute | solution.py:47
  672.2 19.2 %collective-permute-done.54 = bf16[256,2048]{1,0:T(8,128)(2,1)S(1)} collective-permute-done((bf16[256,2048]{1,0:T(8,128)(2,1)S(1)}, bf16[256,2048]{1,0:T(8,128)(2,1)S(1)}, u32[]{:S(2)}, u32[]{:S(2)}) %collective-permute-start.54) | collective-permute-done | bytes 1048608 | tf_op jit(solution)/shard_map/ppermute | solution.py:47
  700.8 13.6 %collective-permute-done.63 = bf16[128,2048]{1,0:T(8,128)(2,1)S(1)} collective-permute-done((bf16[128,2048]{1,0:T(8,128)(2,1)S(1)}, bf16[128,2048]{1,0:T(8,128)(2,1)S(1)}, u32[]{:S(2)}, u32[]{:S(2)}) %collective-permute-start.63) | collective-permute-done | bytes 524320 | tf_op jit(solution)/shard_map/ppermute | solution.py:47
  717.7 26.7 %attend_back.2 = (bf16[1024,512]{1,0:T(8,128)(2,1)}, f32[2048,512]{1,0:T(8,128)}, f32[2048,512]{1,0:T(8,128)}) custom-call(s32[8]{0:T(128)} %stack.35.lim, bf16[1024,1536]{1,0:T(8,128)(2,1)} %add_convert_fusion.6.q_ref.rest_0_.rest_2_, bf16[1024,512]{1,0:T(8,128)(2,1)} %get-tuple-element.72.o_ref, bf16[1024,512]{1,0:T(8,128)(2,1)} %convolution_convert_fusion.9.do_ref, ...), custom_call_target="tpu_custom_call" | custom-call | flops 21474836480 | bytes 20971520 | tf_op jit(solution)/shard_map/attend_back/pallas_call | solution.py:246
  760.9 27.3 %attend_back.3 = (bf16[1024,512]{1,0:T(8,128)(2,1)}, bf16[2048,512]{1,0:T(8,128)(2,1)}, bf16[2048,512]{1,0:T(8,128)(2,1)}) custom-call(s32[8]{0:T(128)} %stack.35.lim, bf16[1024,1536]{1,0:T(8,128)(2,1)} %add_convert_fusion.5.rest_1_.rest_3_.q_ref, bf16[1024,512]{1,0:T(8,128)(2,1)} %get-tuple-element.75.o_ref, ...), custom_call_target="tpu_custom_call" | custom-call | flops 21474836480 | bytes 20971520 | tf_op jit(solution)/shard_map/attend_back/pallas_call | solution.py:246
  802.1 13.1 %fusion.50 = f32[2048,1536]{1,0:T(8,128)} fusion(bf16[1024,2048]{1,0:T(8,128)(2,1)} %constant_dynamic-update-slice_fusion.5, bf16[1024,1536]{1,0:T(8,128)(2,1)S(1)} %get-tuple-element.120), kind=kOutput, calls=%fused_computation.227 | convolution fusion | flops 6442450944 | bytes 19922944 | tf_op jit(solution)/shard_map/dot_general | solution.py:32
  815.2 11.6 %add_convert_fusion.2 = bf16[2048,1536]{1,0:T(8,128)(2,1)} fusion(f32[2048,1536]{1,0:T(8,128)} %fusion.50, bf16[1024,2048]{1,0:T(8,128)(2,1)S(1)} %copy-done.35, bf16[1024,1536]{1,0:T(8,128)(2,1)S(1)} %get-tuple-element.119), kind=kOutput, calls=%fused_computation.2 | convolution fusion | flops 6448742400 | bytes 26214400 | tf_op jit(solution)/shard_map/dot_general | solution.py:32
  842.6 21.2 %collective-permute-start.88 = (f32[768]{0:T(1024)S(1)}, f32[768]{0:T(1024)S(1)}, u32[]{:S(2)}, u32[]{:S(2)}) collective-permute-start(f32[768]{0:T(1024)S(1)} %get-tuple-element.143), channel_id=1, source_target_pairs={{0,24},{4,28},{8,0},{12,4},{16,8},{20,12},{24,16},{28,20},{1,25},{... | collective-permute-start | bytes 9224 | tf_op jit(solution)/shard_map/ppermute | solution.py:332
  940.2 11.1 %collective-permute-done.76 = bf16[128,2048]{1,0:T(8,128)(2,1)S(1)} collective-permute-done((bf16[128,2048]{1,0:T(8,128)(2,1)}, bf16[128,2048]{1,0:T(8,128)(2,1)S(1)}, u32[]{:S(2)}, u32[]{:S(2)}) %collective-permute-start.76) | collective-permute-done | bytes 524320 | tf_op jit(solution)/shard_map/ppermute | solution.py:47
  (533 shorter events, 453.4 us)
Async XLA Ops:
  7.2 82.6 %all-gather.5.cloned.1.call-start = ((), (), s32[]{:S(2)}) async-start(), calls=%async_computation.4 | async-start | bytes 7077888 | tf_op jit(solution)/shard_map/all_gather | solution.py:345
  9.4 119.5 %all-gather.7.cloned.1.call-start = ((), (), s32[]{:S(2)}) async-start(), calls=%async_computation.5 | async-start | bytes 2359296 | tf_op jit(solution)/shard_map/all_gather | solution.py:345
  10.2 257.8 %all-gather.9.cloned.1.call-start = ((), (), s32[]{:S(2)}) async-start(), calls=%async_computation.6 | async-start | bytes 9437184 | tf_op jit(solution)/shard_map/all_gather | solution.py:345
  10.9 274.0 %all-gather.11.cloned.1.call-start = ((), (), s32[]{:S(2)}) async-start(), calls=%async_computation.7 | async-start | bytes 9437184 | tf_op jit(solution)/shard_map/all_gather | solution.py:345
  16.7 729.5 %reduce-scatter.5.cloned.1.call-start = ((), (), s32[]{:S(2)}) async-start(), calls=%async_computation.8 | async-start | bytes 9437184 | tf_op jit(solution)/shard_map/reduce_scatter | solution.py:349
  40.1 36.3 %collective-permute-start.4 = (bf16[256,2048]{1,0:T(8,128)(2,1)S(1)}, bf16[256,2048]{1,0:T(8,128)(2,1)S(1)}, u32[]{:S(2)}, u32[]{:S(2)}) collective-permute-start(bf16[256,2048]{1,0:T(8,128)(2,1)S(1)} %get-tuple-element.71), channel_id=1, source_target_pairs={{0,1},{1,0},{2,3},{3,2},{4,5},{5,4},{6,7},{7,6},{8,9},{9,8},{10,11... | collective-permute-start | bytes 3145736 | tf_op jit(solution)/shard_map/ppermute | solution.py:47
  41.6 35.6 %collective-permute-start.5 = (bf16[256,2048]{1,0:T(8,128)(2,1)S(1)}, bf16[256,2048]{1,0:T(8,128)(2,1)S(1)}, u32[]{:S(2)}, u32[]{:S(2)}) collective-permute-start(bf16[256,2048]{1,0:T(8,128)(2,1)S(1)} %get-tuple-element.71), channel_id=1, source_target_pairs={{0,2},{1,3},{2,0},{3,1},{4,6},{5,7},{6,4},{7,5},{8,10},{9,11},{10,... | collective-permute-start | bytes 3145736 | tf_op jit(solution)/shard_map/ppermute | solution.py:47
  43.2 33.1 %collective-permute-start.2 = (bf16[128,2048]{1,0:T(8,128)(2,1)S(1)}, bf16[128,2048]{1,0:T(8,128)(2,1)S(1)}, u32[]{:S(2)}, u32[]{:S(2)}) collective-permute-start(bf16[128,2048]{1,0:T(8,128)(2,1)S(1)} %slice.518), channel_id=1, source_target_pairs={{0,2},{1,3},{2,0},{3,1},{4,6},{5,7},{6,4},{7,5},{8,10},{9,11},{10,... | collective-permute-start | bytes 1572872 | tf_op jit(solution)/shard_map/ppermute | solution.py:47
  134.4 31.2 %collective-permute-start.8 = (bf16[128,2048]{1,0:T(8,128)(2,1)}, bf16[128,2048]{1,0:T(8,128)(2,1)S(1)}, u32[]{:S(2)}, u32[]{:S(2)}) collective-permute-start(bf16[128,2048]{1,0:T(8,128)(2,1)} %get-tuple-element.215), channel_id=1, source_target_pairs={{0,1},{1,0},{2,3},{3,2},{4,5},{5,4},{6,7},{7,6},{8,9},{9,8},{10,11... | collective-permute-start | bytes 1572872 | tf_op jit(solution)/shard_map/ppermute | solution.py:47
  244.4 58.2 %collective-permute-start.27 = (bf16[256,2048]{1,0:T(8,128)(2,1)}, bf16[256,2048]{1,0:T(8,128)(2,1)S(1)}, u32[]{:S(2)}, u32[]{:S(2)}) collective-permute-start(bf16[256,2048]{1,0:T(8,128)(2,1)} %fusion.17), channel_id=1, source_target_pairs={{0,2},{1,3},{2,0},{3,1},{4,6},{5,7},{6,4},{7,5},{8,10},{9,11},{10,... | collective-permute-start | bytes 3145736 | tf_op jit(solution)/shard_map/ppermute | solution.py:47
  245.2 57.4 %collective-permute-start.26 = (bf16[256,2048]{1,0:T(8,128)(2,1)}, bf16[256,2048]{1,0:T(8,128)(2,1)}, u32[]{:S(2)}, u32[]{:S(2)}) collective-permute-start(bf16[256,2048]{1,0:T(8,128)(2,1)} %fusion.17), channel_id=1, source_target_pairs={{0,1},{1,0},{2,3},{3,2},{4,5},{5,4},{6,7},{7,6},{8,9},{9,8},{10,11... | collective-permute-start | bytes 3145736 | tf_op jit(solution)/shard_map/ppermute | solution.py:47
  300.5 53.8 %collective-permute-start.24 = (bf16[128,2048]{1,0:T(8,128)(2,1)S(1)}, bf16[128,2048]{1,0:T(8,128)(2,1)S(1)}, u32[]{:S(2)}, u32[]{:S(2)}) collective-permute-start(bf16[128,2048]{1,0:T(8,128)(2,1)S(1)} %get-tuple-element.203), channel_id=1, source_target_pairs={{0,1},{1,0},{2,3},{3,2},{4,5},{5,4},{6,7},{7,6},{8,9},{9,8},{10,11... | collective-permute-start | bytes 1572872 | tf_op jit(solution)/shard_map/ppermute | solution.py:47
  301.5 52.8 %collective-permute-start.32 = (bf16[128,2048]{1,0:T(8,128)(2,1)S(1)}, bf16[128,2048]{1,0:T(8,128)(2,1)S(1)}, u32[]{:S(2)}, u32[]{:S(2)}) collective-permute-start(bf16[128,2048]{1,0:T(8,128)(2,1)S(1)} %get-tuple-element.204), channel_id=1, source_target_pairs={{0,2},{1,3},{2,0},{3,1},{4,6},{5,7},{6,4},{7,5},{8,10},{9,11},{10,... | collective-permute-start | bytes 1572872 | tf_op jit(solution)/shard_map/ppermute | solution.py:47
  426.2 65.0 %collective-permute-start.47 = (bf16[256,2048]{1,0:T(8,128)(2,1)S(1)}, bf16[256,2048]{1,0:T(8,128)(2,1)S(1)}, u32[]{:S(2)}, u32[]{:S(2)}) collective-permute-start(bf16[256,2048]{1,0:T(8,128)(2,1)S(1)} %convert_element_type.495), channel_id=1, source_target_pairs={{0,2},{1,3},{2,0},{3,1},{4,6},{5,7},{6,4},{7,5},{8,10},{9,11},{10,... | collective-permute-start | bytes 3145736 | tf_op jit(solution)/shard_map/ppermute | solution.py:47
  427.6 57.6 %collective-permute-start.46 = (bf16[256,2048]{1,0:T(8,128)(2,1)S(1)}, bf16[256,2048]{1,0:T(8,128)(2,1)S(1)}, u32[]{:S(2)}, u32[]{:S(2)}) collective-permute-start(bf16[256,2048]{1,0:T(8,128)(2,1)S(1)} %convert_element_type.495), channel_id=1, source_target_pairs={{0,1},{1,0},{2,3},{3,2},{4,5},{5,4},{6,7},{7,6},{8,9},{9,8},{10,11... | collective-permute-start | bytes 3145736 | tf_op jit(solution)/shard_map/ppermute | solution.py:47
  487.1 51.4 %collective-permute-start.44 = (bf16[128,2048]{1,0:T(8,128)(2,1)S(1)}, bf16[128,2048]{1,0:T(8,128)(2,1)S(1)}, u32[]{:S(2)}, u32[]{:S(2)}) collective-permute-start(bf16[128,2048]{1,0:T(8,128)(2,1)S(1)} %get-tuple-element.191), channel_id=1, source_target_pairs={{0,1},{1,0},{2,3},{3,2},{4,5},{5,4},{6,7},{7,6},{8,9},{9,8},{10,11... | collective-permute-start | bytes 1572872 | tf_op jit(solution)/shard_map/ppermute | solution.py:47
  489.2 49.4 %collective-permute-start.52 = (bf16[128,2048]{1,0:T(8,128)(2,1)S(1)}, bf16[128,2048]{1,0:T(8,128)(2,1)S(1)}, u32[]{:S(2)}, u32[]{:S(2)}) collective-permute-start(bf16[128,2048]{1,0:T(8,128)(2,1)S(1)} %get-tuple-element.192), channel_id=1, source_target_pairs={{0,2},{1,3},{2,0},{3,1},{4,6},{5,7},{6,4},{7,5},{8,10},{9,11},{10,... | collective-permute-start | bytes 1572872 | tf_op jit(solution)/shard_map/ppermute | solution.py:47
  489.5 49.1 %collective-permute-start.51 = (bf16[128,2048]{1,0:T(8,128)(2,1)S(1)}, bf16[128,2048]{1,0:T(8,128)(2,1)S(1)}, u32[]{:S(2)}, u32[]{:S(2)}) collective-permute-start(bf16[128,2048]{1,0:T(8,128)(2,1)S(1)} %get-tuple-element.193), channel_id=1, source_target_pairs={{0,2},{1,3},{2,0},{3,1},{4,6},{5,7},{6,4},{7,5},{8,10},{9,11},{10,... | collective-permute-start | bytes 1572872 | tf_op jit(solution)/shard_map/ppermute | solution.py:47
  499.1 39.4 %collective-permute-start.45 = (bf16[128,2048]{1,0:T(8,128)(2,1)S(1)}, bf16[128,2048]{1,0:T(8,128)(2,1)S(1)}, u32[]{:S(2)}, u32[]{:S(2)}) collective-permute-start(bf16[128,2048]{1,0:T(8,128)(2,1)S(1)} %get-tuple-element.194), channel_id=1, source_target_pairs={{0,1},{1,0},{2,3},{3,2},{4,5},{5,4},{6,7},{7,6},{8,9},{9,8},{10,11... | collective-permute-start | bytes 1572872 | tf_op jit(solution)/shard_map/ppermute | solution.py:47
  571.3 292.5 %reduce-scatter.7.cloned.1.call-start = ((), (), s32[]{:S(2)}) async-start(), calls=%async_computation.9 | async-start | bytes 9437184 | tf_op jit(solution)/shard_map/reduce_scatter | solution.py:349
  628.7 300.1 %reduce-scatter.9.cloned.1.call-start = ((), (), s32[]{:S(2)}) async-start(), calls=%async_computation.10 | async-start | bytes 2359296 | tf_op jit(solution)/shard_map/reduce_scatter | solution.py:349
  659.5 32.6 %collective-permute-start.55 = (bf16[256,2048]{1,0:T(8,128)(2,1)S(1)}, bf16[256,2048]{1,0:T(8,128)(2,1)S(1)}, u32[]{:S(2)}, u32[]{:S(2)}) collective-permute-start(bf16[256,2048]{1,0:T(8,128)(2,1)S(1)} %convert_element_type.516), channel_id=1, source_target_pairs={{0,2},{1,3},{2,0},{3,1},{4,6},{5,7},{6,4},{7,5},{8,10},{9,11},{10,... | collective-permute-start | bytes 3145736 | tf_op jit(solution)/shard_map/ppermute | solution.py:47
  660.0 31.4 %collective-permute-start.54 = (bf16[256,2048]{1,0:T(8,128)(2,1)S(1)}, bf16[256,2048]{1,0:T(8,128)(2,1)S(1)}, u32[]{:S(2)}, u32[]{:S(2)}) collective-permute-start(bf16[256,2048]{1,0:T(8,128)(2,1)S(1)} %convert_element_type.516), channel_id=1, source_target_pairs={{0,1},{1,0},{2,3},{3,2},{4,5},{5,4},{6,7},{7,6},{8,9},{9,8},{10,11... | collective-permute-start | bytes 3145736 | tf_op jit(solution)/shard_map/ppermute | solution.py:47
  692.1 56.2 %collective-permute-start.65 = (bf16[256,2048]{1,0:T(8,128)(2,1)}, bf16[256,2048]{1,0:T(8,128)(2,1)S(1)}, u32[]{:S(2)}, u32[]{:S(2)}) collective-permute-start(bf16[256,2048]{1,0:T(8,128)(2,1)} %convert_element_type.530), channel_id=1, source_target_pairs={{0,2},{1,3},{2,0},{3,1},{4,6},{5,7},{6,4},{7,5},{8,10},{9,11},{10,... | collective-permute-start | bytes 3145736 | tf_op jit(solution)/shard_map/ppermute | solution.py:47
  693.7 50.7 %collective-permute-start.64 = (bf16[256,2048]{1,0:T(8,128)(2,1)}, bf16[256,2048]{1,0:T(8,128)(2,1)S(1)}, u32[]{:S(2)}, u32[]{:S(2)}) collective-permute-start(bf16[256,2048]{1,0:T(8,128)(2,1)} %convert_element_type.530), channel_id=1, source_target_pairs={{0,1},{1,0},{2,3},{3,2},{4,5},{5,4},{6,7},{7,6},{8,9},{9,8},{10,11... | collective-permute-start | bytes 3145736 | tf_op jit(solution)/shard_map/ppermute | solution.py:47
  798.8 170.0 %reduce-scatter.11.cloned.1.call-start = ((), (), s32[]{:S(2)}) async-start(), calls=%async_computation.11 | async-start | bytes 7077888 | tf_op jit(solution)/shard_map/reduce_scatter | solution.py:349
  836.9 49.6 %collective-permute-start.83 = (f32[768]{0:T(1024)S(1)}, f32[768]{0:T(1024)S(1)}, u32[]{:S(2)}, u32[]{:S(2)}) collective-permute-start(f32[768]{0:T(1024)S(1)} %get-tuple-element.141), channel_id=1, source_target_pairs={{0,4},{4,8},{8,12},{12,16},{16,20},{20,24},{24,28},{28,0},{1,5},{5... | collective-permute-start | bytes 9224 | tf_op jit(solution)/shard_map/ppermute | solution.py:332
  837.0 51.3 %collective-permute-start.89 = (f32[768]{0:T(1024)S(1)}, f32[768]{0:T(1024)S(1)}, u32[]{:S(2)}, u32[]{:S(2)}) collective-permute-start(f32[768]{0:T(1024)S(1)} %get-tuple-element.142), channel_id=1, source_target_pairs={{0,28},{4,0},{8,4},{12,8},{16,12},{20,16},{24,20},{28,24},{1,29},{... | collective-permute-start | bytes 9224 | tf_op jit(solution)/shard_map/ppermute | solution.py:332
  842.6 47.9 %collective-permute-start.88 = (f32[768]{0:T(1024)S(1)}, f32[768]{0:T(1024)S(1)}, u32[]{:S(2)}, u32[]{:S(2)}) collective-permute-start(f32[768]{0:T(1024)S(1)} %get-tuple-element.143), channel_id=1, source_target_pairs={{0,24},{4,28},{8,0},{12,4},{16,8},{20,12},{24,16},{28,20},{1,25},{... | collective-permute-start | bytes 9224 | tf_op jit(solution)/shard_map/ppermute | solution.py:332
  894.8 38.8 %collective-permute-start.71 = (bf16[128,2048]{1,0:T(8,128)(2,1)}, bf16[128,2048]{1,0:T(8,128)(2,1)}, u32[]{:S(2)}, u32[]{:S(2)}) collective-permute-start(bf16[128,2048]{1,0:T(8,128)(2,1)} %get-tuple-element.175), channel_id=1, source_target_pairs={{0,2},{1,3},{2,0},{3,1},{4,6},{5,7},{6,4},{7,5},{8,10},{9,11},{10,... | collective-permute-start | bytes 1572872 | tf_op jit(solution)/shard_map/ppermute | solution.py:47
  897.3 42.8 %collective-permute-start.74 = (bf16[128,2048]{1,0:T(8,128)(2,1)}, bf16[128,2048]{1,0:T(8,128)(2,1)}, u32[]{:S(2)}, u32[]{:S(2)}) collective-permute-start(bf16[128,2048]{1,0:T(8,128)(2,1)} %get-tuple-element.179), channel_id=1, source_target_pairs={{0,1},{1,0},{2,3},{3,2},{4,5},{5,4},{6,7},{7,6},{8,9},{9,8},{10,11... | collective-permute-start | bytes 1572872 | tf_op jit(solution)/shard_map/ppermute | solution.py:47
  905.4 34.8 %collective-permute-start.78 = (bf16[128,2048]{1,0:T(8,128)(2,1)}, bf16[128,2048]{1,0:T(8,128)(2,1)}, u32[]{:S(2)}, u32[]{:S(2)}) collective-permute-start(bf16[128,2048]{1,0:T(8,128)(2,1)} %get-tuple-element.180), channel_id=1, source_target_pairs={{0,2},{1,3},{2,0},{3,1},{4,6},{5,7},{6,4},{7,5},{8,10},{9,11},{10,... | collective-permute-start | bytes 1572872 | tf_op jit(solution)/shard_map/ppermute | solution.py:47
  (142 other events, 2911.0 us)
Sparse Core Ops, SparseCore 0:
  10.2 67.4 all-gather.4
  79.3 27.8 all-gather.6
  108.8 81.4 all-gather.8
  191.7 80.5 all-gather.10
  571.4 110.8 reduce-scatter.4
  684.5 88.0 reduce-scatter.6
  798.9 58.2 reduce-scatter.8
  859.5 68.5 reduce-scatter.10

commit v3 on v1

--- a/solution.py
+++ b/solution.py
@@ -42,44 +42,97 @@
     return value.astype(jnp.float32)
 
 
+def half_order():
+    size = lax.axis_size("tensor")
+    if size != 4:
+        return [(p, side) for p in range(size) for side in range(2)]
+    return [(0, 0), (0, 1), (1, 1), (2, 0), (3, 0), (1, 0), (3, 1), (2, 1)]
+
+
 def swap(value, bits):
     size = lax.axis_size("tensor")
     return lax.ppermute(value, "tensor", [(i, i ^ bits) for i in range(size)])
 
 
-def gather_rows(own):
+def after(value, *others):
+    return lax.optimization_barrier((value, *others))[0]
+
+
+def together(values, *others):
+    values = tuple(values)
+    return lax.optimization_barrier((*values, *others))[: len(values)]
+
+
+def gather_near(own, *others):
     size = lax.axis_size("tensor")
-    if size != 4:
-        return jnp.concatenate([own] + [swap(own, p) for p in range(1, size)], axis=0)
+    own = after(own, *others)
+    return [swap(own, p) for p in range(1, 3 if size == 4 else size)]
+
+
+def gather_far(near, *others):
+    if lax.axis_size("tensor") != 4:
+        return []
+    half = near[0].shape[0] // 2
+    near = together(near, *others)
+    return [swap(near[0][:half], 2), swap(near[1][half:], 1)]
+
+
+def gathered(own, near, far):
+    if not far:
+        return jnp.concatenate([own] + near, axis=0)
     half = own.shape[0] // 2
-    first, second = swap(own, 1), swap(own, 2)
+    first, second = near
     return jnp.concatenate(
-        [own, first, second, swap(first[:half], 2), swap(second[half:], 1)], axis=0
-    )
-
-
-def scatter_sum(terms):
+        [own, first[half:], second[:half], far[0], first[:half], far[1], second[half:]], axis=0
+    )
+
+
+def scatter_near(terms, *others):
     size = lax.axis_size("tensor")
     rows = terms.shape[0] // size
-    block = [terms[p * rows : (p + 1) * rows] for p in range(size)]
+    terms = after(terms, *others)
     if size != 4:
-        total = wide(block[0])
-        for p in range(1, size):
-            total = total + wide(swap(block[p], p))
-        return total
-    half = rows // 2
-    upper = [b[:half] for b in block]
-    lower = [b[half:] for b in block]
-    relay_upper = swap(upper[3], 1)
-    relay_lower = swap(lower[3], 2)
-    direct_upper = swap(upper[1], 1)
-    direct_lower = swap(lower[2], 2)
-    sum_upper = swap(low(wide(relay_upper) + wide(upper[2])), 2)
-    sum_lower = swap(low(wide(relay_lower) + wide(lower[1])), 1)
+        return terms[:rows], [swap(terms[p * rows : (p + 1) * rows], p) for p in range(1, size)]
+    return terms[: 2 * rows], [
+        swap(terms[2 * rows : 3 * rows], 1),
+        swap(terms[3 * rows :], 2),
+    ]
+
+
+def scatter_sums(near, *others):
+    if lax.axis_size("tensor") != 4:
+        return []
+    kept, came = near
+    first, second = together(came, *others)
+    half = kept.shape[0] // 4
+    lower = low(wide(second[:half]) + wide(kept[2 * half : 3 * half]))
+    upper = low(wide(first[:half]) + wide(kept[3 * half :]))
+    return together((lower, upper))
+
+
+def scatter_far(near, *others):
+    return [swap(value, p) for p, value in enumerate(scatter_sums(near, *others), 1)]
+
+
+def scatter_far_gather_near(near, own, *others):
+    sums = scatter_sums(near, *others)
+    if not sums:
+        return [], gather_near(own, *near[1], *others)
+    half = sums[0].shape[0]
+    pieces = together([jnp.concatenate([value, own], axis=0) for value in sums])
+    came = [swap(value, p) for p, value in enumerate(pieces, 1)]
+    return [c[:half] for c in came], [c[half:] for c in came]
+
+
+def scattered(near, far):
+    kept, came = near
+    if not far:
+        return add_up([wide(kept)] + [wide(c) for c in came])
+    half = kept.shape[0] // 4
     return jnp.concatenate(
         [
-            wide(upper[0]) + wide(direct_upper) + wide(sum_upper),
-            wide(lower[0]) + wide(direct_lower) + wide(sum_lower),
+            wide(kept[:half]) + wide(came[0][half:]) + wide(far[1]),
+            wide(kept[half : 2 * half]) + wide(came[1][half:]) + wide(far[0]),
         ],
         axis=0,
     )
@@ -300,13 +353,29 @@
 
 
 def total_of(vectors):
-    devices = lax.axis_size("dp") * lax.axis_size("tensor")
-    packed = jnp.concatenate([v.reshape(devices, -1) for v in vectors], axis=1)
-    packed = lax.psum_scatter(packed, ("dp", "tensor"), scatter_dimension=0, tiled=True)[0]
-    sizes = [v.shape[0] // devices for v in vectors]
+    slots, groups = lax.axis_size("dp"), lax.axis_size("tensor")
+    slot, position = lax.axis_index("dp"), lax.axis_index("tensor")
+    packed = jnp.concatenate([v.reshape(slots, groups, -1) for v in vectors], axis=2)
+
+    def share(p):
+        return lax.dynamic_index_in_dim(packed, position ^ p, 1, keepdims=False)
+
+    total = add_up([share(0)] + [swap(share(p), p) for p in range(1, groups)])
+
+    def ahead(step):
+        return lax.dynamic_index_in_dim(total, (slot + step) % slots, 0, keepdims=False)
+
+    total = add_up(
+        [ahead(0)]
+        + [
+            lax.ppermute(ahead(step), "dp", [(i, (i + step) % slots) for i in range(slots)])
+            for step in range(1, slots)
+        ]
+    )
     parts, at = [], 0
-    for size in sizes:
-        parts.append(packed[at : at + size])
+    for v in vectors:
+        size = v.shape[0] // (slots * groups)
+        parts.append(total[at : at + size])
         at += size
     return parts
 
@@ -316,7 +385,34 @@
 
 
 def scatter_weight(grad):
-    return wide(lax.psum_scatter(low(grad), "dp", scatter_dimension=0, tiled=True))
+    return lax.psum_scatter(grad, "dp", scatter_dimension=0, tiled=True)
+
+
+def pair_exchange(grad):
+    slots = lax.axis_size("dp")
+    side = lax.axis_index("dp") % 2
+    blocks = grad.reshape(slots // 2, 2, grad.shape[0] // slots, grad.shape[1])
+    give = lax.dynamic_index_in_dim(blocks, 1 - side, 1, keepdims=False)
+    kept = lax.dynamic_index_in_dim(blocks, side, 1, keepdims=False)
+    return kept, lax.ppermute(give, "dp", [(i, i ^ 1) for i in range(slots)])
+
+
+def pair_scatter(pair, *others):
+    slots = lax.axis_size("dp")
+    pairs = slots // 2
+    own = lax.axis_index("dp") // 2
+    kept, came = pair
+    total = low(wide(kept) + wide(after(came, *others)))
+    ahead = together(
+        [
+            lax.dynamic_index_in_dim(total, (own + step) % pairs, 0, keepdims=False)
+            for step in range(pairs)
+        ]
+    )
+    return [ahead[0]] + [
+        lax.ppermute(ahead[step], "dp", [(i, (i + 2 * step) % slots) for i in range(slots)])
+        for step in range(1, pairs)
+    ]
 
 
 def add_up(terms):
@@ -357,11 +453,12 @@
     part = rows // CHUNKS
     cut = [slice(c * part, (c + 1) * part) for c in range(CHUNKS)]
     every = range(CHUNKS)
+    run = part // 2
     limits = jnp.stack(
         [
-            slot_len - ((position ^ p) * rows + c * part)
+            slot_len - ((position ^ p) * rows + c * part + side * run)
             for c in range(CHUNKS)
-            for p in range(groups)
+            for p, side in half_order()
         ]
     ).astype(jnp.int32)
     row_live = (position * rows + jnp.arange(rows, dtype=jnp.int32) < slot_len).astype(jnp.float32)[
@@ -377,60 +474,156 @@
     up_full = gather_weight(up_weight)
     down_full = gather_weight(down_weight)
 
-    seq_tokens = [gather_rows(tokens[cut[c]]) for c in every]
-    projected = [low(nn(seq_tokens[c], proj_full) + bias_proj) for c in every]
-    context, lse, mid, unit1, inverse1, mid_low = ([None] * CHUNKS for _ in range(6))
+
+    def lists(count):
+        return ([None] * CHUNKS for _ in range(count))
+
+    near, far, seq_tokens, projected = lists(4)
+    before = ()
     for c in every:
-        context[c], lse[c] = attend(c, projected, limits, part)
-    for c in every:
-        attn_sum = scatter_sum(low(nt(context[c], out_full)))
-        mid[c], unit1[c], inverse1[c] = norm_rows(
-            wide(tokens[cut[c]]) + attn_sum + out_bias, norm1_gain, norm1_shift
+        near[c] = gather_near(tokens[cut[c]], *before)
+        far[c] = gather_far(near[c])
+        before = far[c] or near[c]
+        seq_tokens[c] = gathered(
+            tokens[cut[c]], near[c], together(far[c], *projected[:c]) if far[c] else []
         )
-    mid_seq = [gather_rows(low(mid[c])) for c in every]
-    activ, slope = ([None] * CHUNKS for _ in range(2))
-    ffn_sum = [None] * CHUNKS
-    for c in every:
-        activ[c], slope[c] = gate_and_slope(nn(mid_seq[c], up_full) + bias_up)
-        ffn_sum[c] = scatter_sum(low(nt(activ[c], down_full)))
-    layer_out, grad_sum2, vec2 = ([None] * CHUNKS for _ in range(3))
-    for c in every:
-        final, unit2, inverse2 = norm_rows(mid[c] + ffn_sum[c] + down_bias, norm2_gain, norm2_shift)
-        layer_out[c] = low(final * row_live[cut[c]])
+        projected[c] = low(nn(seq_tokens[c], proj_full) + bias_proj)
+
+    down_terms, up_terms = [], []
+    context, lse, attn_low = lists(3)
+    context[0], lse[0] = attend(0, projected, limits, run)
+    attn_low[0] = low(nt(context[0], out_full))
+    near[0] = scatter_near(attn_low[0])
+    context[1], lse[1] = attend(1, [after(p, attn_low[0]) for p in projected], limits, run)
+    far[0] = scatter_far(near[0], context[1])
+    attn_low[1] = low(nt(after(context[1], *near[0][1]), out_full))
+
+    def first_norm(c):
+        attn_sum = scattered(near[c], far[c])
+        result = norm_rows(wide(tokens[cut[c]]) + attn_sum + out_bias, norm1_gain, norm1_shift)
+        return (*result, low(result[0]))
+
+    def second_norm(c):
+        ffn_sum = scattered(near[c], far[c])
+        final, unit2, inverse2 = norm_rows(mid[c] + ffn_sum + down_bias, norm2_gain, norm2_shift)
         grad_final = wide(cotangent[cut[c]]) * row_live[cut[c]]
-        grad_sum2[c], gain_part, shift_part = norm_back(grad_final, unit2, inverse2, norm2_gain)
-        vec2[c] = (gain_part, shift_part, jnp.sum(grad_sum2[c], axis=0))
-    grad_ffn = [gather_rows(low(grad_sum2[c])) for c in every]
-    grad_pre = [low(nn(grad_ffn[c], down_full) * wide(slope[c])) for c in every]
-    mid_sum = [scatter_sum(low(nt(grad_pre[c], up_full))) for c in every]
-    grad_sum1, vec1 = ([None] * CHUNKS for _ in range(2))
-    for c in every:
-        grad_sum1[c], gain_part, shift_part = norm_back(
-            grad_sum2[c] + mid_sum[c], unit1[c], inverse1[c], norm1_gain
+        grad_sum, gain_part, shift_part = norm_back(grad_final, unit2, inverse2, norm2_gain)
+        return (
+            low(final * row_live[cut[c]]),
+            grad_sum,
+            (gain_part, shift_part, jnp.sum(grad_sum, axis=0)),
+            low(grad_sum),
         )
-        vec1[c] = (gain_part, shift_part, jnp.sum(grad_sum1[c], axis=0))
-    grad_attn = [gather_rows(low(grad_sum1[c])) for c in every]
-
-    down_part = scatter_weight(add_up([tn(grad_ffn[c], activ[c]) for c in every]))
-    up_part = scatter_weight(add_up([tn(mid_seq[c], grad_pre[c]) for c in every]))
-    out_part = scatter_weight(add_up([tn(grad_attn[c], context[c]) for c in every]))
+
+    def first_norm_back(c):
+        mid_sum = scattered(near[c], far[c])
+        grad_sum, gain_part, shift_part = norm_back(
+            grad_sum2[c] + mid_sum, unit1[c], inverse1[c], norm1_gain
+        )
+        return (grad_sum, (gain_part, shift_part, jnp.sum(grad_sum, axis=0)), low(grad_sum))
+
+    def turn(terms, norm, filler=None):
+        near[1] = scatter_near(terms, *far[0])
+        results = [norm(0), None]
+        out = results[0][-1]
+        if filler is not None:
+            filler(0, (out,))
+        far[1], near[0] = scatter_far_gather_near(near[1], out)
+        if filler is not None:
+            filler(1, tuple(near[1][1]))
+        results[1] = norm(1)
+        far[0] = gather_far(near[0], *down_terms[1:])
+        whole = gathered(out, near[0], far[0])
+        near[1] = gather_near(results[1][-1], *(far[0] or near[0]))
+        return results, after(whole, results[1][-1])
+
+    results, source = turn(attn_low[1], first_norm)
+    mid, unit1, inverse1, mid_out = zip(*results)
+    mid_seq, activ, slope, ffn_low = lists(4)
+    mid_seq[0] = source
+    activ[0], slope[0] = gate_and_slope(nn(source, up_full) + bias_up)
+    far[1] = gather_far(near[1])
+    ffn_low[0] = low(nt(after(activ[0], *near[1]), down_full))
+    mid_seq[1] = gathered(mid_out[1], near[1], far[1])
+    near[0] = scatter_near(ffn_low[0], *(far[1] or near[1]))
+    activ[1], slope[1] = gate_and_slope(nn(after(mid_seq[1], ffn_low[0]), up_full) + bias_up)
+    far[0] = scatter_far(near[0])
+    ffn_low[1] = low(nt(after(activ[1], *near[0][1]), down_full))
+
+    results, source = turn(ffn_low[1], second_norm)
+    layer_out, grad_sum2, vec2, grad_out2 = zip(*results)
+    grad_ffn, grad_pre, mid_low = lists(3)
+    grad_ffn[0] = source
+    grad_pre[0] = low(nn(source, down_full) * wide(slope[0]))
+    far[1] = gather_far(near[1])
+    mid_low[0] = low(nt(after(grad_pre[0], *near[1]), up_full))
+    grad_ffn[1] = gathered(grad_out2[1], near[1], far[1])
+    near[0] = scatter_near(mid_low[0], *(far[1] or near[1]))
+    grad_pre[1] = low(nn(after(grad_ffn[1], mid_low[0]), down_full) * wide(slope[1]))
+    far[0] = scatter_far(near[0])
+    mid_low[1] = low(nt(after(grad_pre[1], *near[0][1]), up_full))
+
+    def down_term(c, others):
+        down_terms.append(tn(after(grad_ffn[c], *others), activ[c]))
+
+    results, source = turn(mid_low[1], first_norm_back, down_term)
+    down_grad = low(add_up(down_terms))
+    down_part = scatter_weight(down_grad)
     up_bias_part = add_up([jnp.sum(wide(grad_pre[c]), axis=0) for c in every])
-
-    grad_query, carry = [None] * CHUNKS, None
-    for c in every:
-        grad_context = low(nn(grad_attn[c], out_full))
-        grad_query[c], *carry = attend_back(
-            c, projected, context[c], grad_context, lse[c], limits, part, carry
-        )
+    grad_sum1, vec1, grad_out1 = zip(*results)
+    grad_attn, grad_query = lists(2)
+    grad_attn[0] = source
+    grad_context = low(nn(after(source, down_grad), out_full))
+    grad_query[0], *carry = attend_back(
+        0, projected, context[0], grad_context, lse[0], limits, run, None
+    )
+    far[1] = gather_far(near[1], grad_query[0])
+    up_terms.append(tn(after(mid_seq[0], grad_query[0], *near[1]), grad_pre[0]))
+    up_terms.append(tn(after(mid_seq[1], up_terms[0]), grad_pre[1]))
+    up_grad = low(add_up(up_terms))
+    up_part = scatter_weight(up_grad)
+    grad_attn[1] = gathered(
+        grad_out1[1], near[1], together(far[1], up_terms[0]) if far[1] else []
+    )
+    grad_context = low(nn(after(grad_attn[1], up_grad), out_full))
+    grad_query[1], *carry = attend_back(
+        1, projected, context[1], grad_context, lse[1], limits, run, carry
+    )
     size = part * groups
     grad_proj = [
         jnp.concatenate([grad_query[c]] + [a[c * size : (c + 1) * size] for a in carry], axis=1)
         for c in every
     ]
-    proj_part = scatter_weight(add_up([tn(seq_tokens[c], grad_proj[c]) for c in every]))
-    tokens_grad = [
-        low(grad_sum1[c] + scatter_sum(low(nt(grad_proj[c], proj_full)))) for c in every
-    ]
+    tokens_low, tokens_grad = lists(2)
+
+    def proj_term(i, *others):
+        cols = slice(i * head_cols, (i + 1) * head_cols)
+        return low(
+            add_up([tn(after(seq_tokens[c], *others), grad_proj[c][:, cols]) for c in every])
+        )
+
+    tokens_low[0] = low(nt(after(grad_proj[0], up_grad, down_part), proj_full))
+    near[0] = scatter_near(tokens_low[0])
+    proj_grad, pair, proj_came = [None] * 3, [None] * 3, [None] * 3
+    proj_grad[0] = proj_term(0, tokens_low[0])
+    pair[0] = pair_exchange(proj_grad[0])
+    proj_grad[1] = proj_term(1, proj_grad[0])
+    pair[1] = pair_exchange(proj_grad[1])
+    proj_came[0] = pair_scatter(pair[0], proj_grad[1])
+    far[0] = scatter_far(near[0], proj_grad[1])
+    tokens_low[1] = low(nt(after(grad_proj[1], pair[0][1], *near[0][1]), proj_full))
+    near[1] = scatter_near(tokens_low[1], *far[0])
+    proj_came[1] = pair_scatter(pair[1], tokens_low[1])
+    proj_grad[2] = proj_term(2, tokens_low[1], pair[1][1], *far[0])
+    pair[2] = pair_exchange(proj_grad[2])
+    out_grad = low(add_up([tn(after(grad_attn[c], proj_grad[2]), context[c]) for c in every]))
+    out_part = scatter_weight(out_grad)
+    far[1] = scatter_far(near[1], out_grad)
+    proj_came[2] = pair_scatter(pair[2], out_grad, *proj_came[0])
+    for c in every:
+        tokens_grad[c] = low(grad_sum1[c] + scattered(near[c], far[c]))
+    out_part, up_part, down_part = map(wide, (out_part, up_part, down_part))
+    proj_part = [add_up([wide(v) for v in came]) for came in proj_came]
     proj_bias = add_up([jnp.sum(wide(grad_proj[c]), axis=0) for c in every])
     (
         norm2_gain_grad,
@@ -440,13 +633,13 @@
         norm1_shift_grad,
         out_bias_grad,
         up_bias_grad,
+        query_bias_grad,
+        value_bias_grad,
     ) = total_of(
-        [add_up([vec2[c][i] for c in every]) for i in range(3)]
+        [after(add_up([vec2[c][i] for c in every]), up_part) for i in range(3)]
         + [add_up([vec1[c][i] for c in every]) for i in range(3)]
-        + [placed(up_bias_part, hid_start, FF)]
-    )
-    query_bias_grad, value_bias_grad = total_of(
-        [
+        + [
+            placed(up_bias_part, hid_start, FF),
             placed(proj_bias[:head_cols], col_start, width),
             placed(proj_bias[2 * head_cols :], col_start, width),
         ]
@@ -454,9 +647,7 @@
     return (
         jnp.concatenate(layer_out, axis=0),
         jnp.concatenate(tokens_grad, axis=0),
-        proj_part[:, :head_cols],
-        proj_part[:, head_cols : 2 * head_cols],
-        proj_part[:, 2 * head_cols :],
+        *proj_part,
         out_part,
         up_part,
         down_part,

time: 1110 us -> 891 us (0.80)
  waiting for transfers between devices: 430 us -> 265 us
  blocking collectives: 87.4 us -> 0 us
  matrix products: 282 us -> 258 us
  other arithmetic: 48.1 us -> 70.6 us
  starting transfers between devices: 91.4 us -> 110 us
  local copies, waits for them, and re-layouts: 54.7 us -> 66.7 us
    ppermute x80 -> x61, waiting for transfers between devices: 383 us -> 226 us  [swap(): return lax.ppermute(value, 'tensor', [(i, i ^ bits) for i in range(size)])]
    unnamed x1 -> x0, blocking collectives: 87.4 us -> none
    reduce_scatter x4 -> x3, waiting for transfers between devices: 45.2 us -> 0.01 us  [scatter_weight(): return lax.psum_scatter(grad, 'dp', scatter_dimension=0, tiled=True)]
    ppermute x0 -> x19, starting transfers between devices: none -> 42.7 us  [the longest x9 25.9 us: pair_scatter(): lax.ppermute(ahead[step], 'dp', [(i, (i + 2 * step) % slots) for i in ran...]
    ppermute x0 -> x19, waiting for transfers between devices: none -> 38.1 us  [the longest x9 34.5 us: pair_scatter(): lax.ppermute(ahead[step], 'dp', [(i, (i + 2 * step) % slots) for i in ran...]
    ppermute x80 -> x61, starting transfers between devices: 91 us -> 66.6 us  [swap(): return lax.ppermute(value, 'tensor', [(i, i ^ bits) for i in range(size)])]
    dot_general x8 -> x12, matrix products: 99.8 us -> 86.6 us  [tn(): lax.dot_general(left, right, (((0,), (0,)), ((), ())), preferred_element_...]
    unnamed x111 -> x217, local copies, waits for them, and re-layouts: 26.5 us -> 34.4 us
  transfers between devices with their start and end apart: 89 -> 87, of which waited for: 36 -> 45; matrix products, arithmetic and copies ran while one was open for 31% -> 40% of each run, Pallas kernels for 9% -> 10%
where the time goes in v3:
time: 891 us; the launch traced here: 878 us
  waiting for transfers between devices  265 us (30%)
  matrix products  258 us (29%)
  starting transfers between devices  110 us (12%)
  Pallas kernels  91 us (10%)
  other arithmetic  70.6 us (8%)
  local copies, waits for them, and re-layouts  66.7 us (7%)
  between operations  16.9 us (2%)
    ppermute x61, waiting for transfers between devices, swap(): return lax.ppermute(value, 'tensor', [(i, i ^ bits) for i in range(size)])  226 us
    dot_general x8, matrix products, nn(): lax.dot_general(left, right, (((1,), (0,)), ((), ())), preferred_element_...  97.4 us
    dot_general x12, matrix products, tn(): lax.dot_general(left, right, (((0,), (0,)), ((), ())), preferred_element_...  86.6 us
    dot_general x8, matrix products, nt(): lax.dot_general(left, right, (((1,), (1,)), ((), ())), preferred_element_...  73.7 us
    ppermute x61, starting transfers between devices, swap(): return lax.ppermute(value, 'tensor', [(i, i ^ bits) for i in range(size)])  66.6 us
    pallas_call x2, Pallas kernels, attend_back(): pl.pallas_call(kernel, out_shape=(jax.ShapeDtypeStruct((part, cols), jnp....  53 us
    pallas_call x2, Pallas kernels, attend(): pl.pallas_call(kernel, out_shape=(jax.ShapeDtypeStruct((part, cols), jnp....  38 us
    ppermute x9, waiting for transfers between devices, pair_scatter(): lax.ppermute(ahead[step], 'dp', [(i, (i + 2 * step) % slots) for i in ran...  34.5 us
  transfers between devices with their start and end apart: 87, of which 45 were waited for; matrix products, arithmetic and copies ran while one was open for 40% of the time, Pallas kernels for 10%

profile of v3, /device:TPU:0, one launch (start us, length us, event | category | flops | bytes accessed | tf_op | source)
XLA Modules:
  0.0 877.9 jit_solution(2229597903535405106)
XLA Ops:
  20.8 18.9 %collective-permute-done.1 = bf16[256,2048]{1,0:T(8,128)(2,1)S(1)} collective-permute-done((bf16[256,2048]{1,0:T(8,128)(2,1)}, bf16[256,2048]{1,0:T(8,128)(2,1)S(1)}, u32[]{:S(2)}, u32[]{:S(2)}) %collective-permute-start.1) | collective-permute-done | bytes 1048608 | tf_op jit(solution)/shard_map/ppermute | solution.py:54
  61.7 17.2 %collective-permute-done.5 = bf16[256,2048]{1,0:T(8,128)(2,1)S(1)} collective-permute-done((bf16[256,2048]{1,0:T(8,128)(2,1)S(1)}, bf16[256,2048]{1,0:T(8,128)(2,1)S(1)}, u32[]{:S(2)}, u32[]{:S(2)}) %collective-permute-start.5) | collective-permute-done | bytes 1048608 | tf_op jit(solution)/shard_map/ppermute | solution.py:54
  84.6 11.5 %add_convert_fusion.5.q_ref.rest_0_.rest_2_ = bf16[1024,1536]{1,0:T(8,128)(2,1)} fusion(bf16[1024,2048]{1,0:T(8,128)(2,1)} %slice_dynamic-update-slice_fusion.28, bf16[2048,1536]{1,0:T(8,128)(2,1)} %all-gather.5.cloned.1.call-done, f32[1536]{0:T(1024)S(1)} %pad_maximum_fusion.11), kind=kOutput, calls=%fused_computation.21 | convolution fusion | flops 6445596672 | bytes 13637632 | tf_op jit(solution)/shard_map/dot_general | solution.py:26
  101.7 9.6 %add_convert_fusion.4.rest_1_.rest_3_.q_ref = bf16[1024,1536]{1,0:T(8,128)(2,1)} fusion(bf16[1024,2048]{1,0:T(8,128)(2,1)} %slice_dynamic-update-slice_fusion.24, bf16[2048,1536]{1,0:T(8,128)(2,1)S(1)} %copy-done.76, f32[1536]{0:T(1024)S(1)} %pad_maximum_fusion.11), kind=kOutput, calls=%fused_computation.20 | convolution fusion | flops 6445596672 | bytes 13637632 | tf_op jit(solution)/shard_map/dot_general | solution.py:26
  111.3 18.8 %attend.2 = (bf16[1024,512]{1,0:T(8,128)(2,1)}, f32[4,1,1024]{2,1,0:T(1,128)}) custom-call(s32[16]{0:T(128)} %stack.67.lim, bf16[1024,1536]{1,0:T(8,128)(2,1)} %add_convert_fusion.5.q_ref.rest_0_.rest_2_, bf16[1024,1536]{1,0:T(8,128)(2,1)} %add_convert_fusion.5.q_ref.rest_0_.rest_2_, bf16[1024,1536]{1,0:T(8,128)(2,1)} %add_convert_fusion.4.rest_1_.rest_3_.q_ref, ...), custom_call_target="tpu_custom_call" | custom-call | flops 8589934592 | bytes 6291456 | tf_op jit(solution)/shard_map/attend/pallas_call | solution.py:193
  138.3 19.2 %attend.3 = (bf16[1024,512]{1,0:T(8,128)(2,1)}, f32[4,1,1024]{2,1,0:T(1,128)}) custom-call(s32[16]{0:T(128)} %stack.67.lim, bf16[1024,1536]{1,0:T(8,128)(2,1)} %add_convert_fusion.4.rest_1_.rest_3_.q_ref, bf16[1024,1536]{1,0:T(8,128)(2,1)} %add_convert_fusion.5.q_ref.rest_0_.rest_2_, bf16[1024,1536]{1,0:T(8,128)(2,1)} %add_convert_fusion.4.rest_1_.rest_3_.q_ref, ...), custom_call_target="tpu_custom_call" | custom-call | flops 8589934592 | bytes 6291456 | tf_op jit(solution)/shard_map/attend/pallas_call | solution.py:193
  179.0 14.4 %collective-permute-done.13 = bf16[256,2048]{1,0:T(8,128)(2,1)S(1)} collective-permute-done((bf16[256,2048]{1,0:T(8,128)(2,1)S(1)}, bf16[256,2048]{1,0:T(8,128)(2,1)S(1)}, u32[]{:S(2)}, u32[]{:S(2)}) %collective-permute-start.13) | collective-permute-done | bytes 1048608 | tf_op jit(solution)/shard_map/ppermute | solution.py:54
  200.0 31.3 %collective-permute-done.14 = bf16[384,2048]{1,0:T(8,128)(2,1)S(1)} collective-permute-done((bf16[384,2048]{1,0:T(8,128)(2,1)}, bf16[384,2048]{1,0:T(8,128)(2,1)S(1)}, u32[]{:S(2)}, u32[]{:S(2)}) %collective-permute-start.14) | collective-permute-done | bytes 1572896 | tf_op jit(solution)/shard_map/ppermute | solution.py:54
  252.9 16.9 %multiply_convert_fusion.3 = (bf16[1024,2048]{1,0:T(8,128)(2,1)}, f32[1024,2048]{1,0:T(8,128)}) fusion(f32[2048]{0:T(1024)S(1)} %dynamic_slice.105, bf16[1024,2048]{1,0:T(8,128)(2,1)} %slice_dynamic-update-slice_fusion.20, bf16[2048,2048]{1,0:T(8,128)(2,1)} %all-gather.9.cloned.1.call-done), kind=kOutput, calls=%fused_computation.16 | convolution fusion | flops 8610906112 | bytes 25174016 | tf_op jit(solution)/shard_map/dot_general | solution.py:26
  273.9 12.7 %convolution_convert_fusion.5 = bf16[1024,2048]{1,0:T(8,128)(2,1)S(1)} fusion(bf16[1024,2048]{1,0:T(8,128)(2,1)} %get-tuple-element.172, bf16[2048,2048]{1,0:T(8,128)(2,1)} %all-gather.11.cloned.1.call-done), kind=kOutput, calls=%fused_computation.31 | convolution fusion | flops 8592031744 | bytes 16777216 | tf_op jit(solution)/shard_map/dot_general | solution.py:20
  294.1 14.9 %multiply_convert_fusion.2 = (bf16[1024,2048]{1,0:T(8,128)(2,1)S(1)}, f32[1024,2048]{1,0:T(8,128)}) fusion(f32[2048]{0:T(1024)S(1)} %dynamic_slice.105, bf16[1024,2048]{1,0:T(8,128)(2,1)S(1)} %slice_dynamic-update-slice_fusion.16, bf16[2048,2048]{1,0:T(8,128)(2,1)} %all-gather.9.cloned.1.call-done), kind=kOutput, calls=%fused_computation.14 | convolution fusion | flops 8610906112 | bytes 25174016 | tf_op jit(solution)/shard_map/dot_general | solution.py:26
  318.6 11.3 %convolution_convert_fusion.4 = bf16[1024,2048]{1,0:T(8,128)(2,1)S(1)} fusion(bf16[1024,2048]{1,0:T(8,128)(2,1)S(1)} %get-tuple-element.181, bf16[2048,2048]{1,0:T(8,128)(2,1)} %all-gather.11.cloned.1.call-done), kind=kOutput, calls=%fused_computation.30 | convolution fusion | flops 8592031744 | bytes 16777216 | tf_op jit(solution)/shard_map/dot_general | solution.py:20
  339.3 15.8 %collective-permute-done.27 = bf16[256,2048]{1,0:T(8,128)(2,1)S(1)} collective-permute-done((bf16[256,2048]{1,0:T(8,128)(2,1)S(1)}, bf16[256,2048]{1,0:T(8,128)(2,1)S(1)}, u32[]{:S(2)}, u32[]{:S(2)}) %collective-permute-start.27) | collective-permute-done | bytes 1048608 | tf_op jit(solution)/shard_map/ppermute | solution.py:54
  358.2 31.1 %collective-permute-done.28 = bf16[384,2048]{1,0:T(8,128)(2,1)S(1)} collective-permute-done((bf16[384,2048]{1,0:T(8,128)(2,1)S(1)}, bf16[384,2048]{1,0:T(8,128)(2,1)S(1)}, u32[]{:S(2)}, u32[]{:S(2)}) %collective-permute-start.28) | collective-permute-done | bytes 1572896 | tf_op jit(solution)/shard_map/ppermute | solution.py:54
  410.1 17.0 %convert_reduce_fusion.1 = (f32[2048]{0:T(1024)S(1)}, bf16[1024,2048]{1,0:T(8,128)(2,1)S(1)}) fusion(f32[1024,2048]{1,0:T(8,128)} %get-tuple-element.418, f32[2048]{0:T(1024)S(1)} %dynamic_slice.105, bf16[1024,2048]{1,0:T(8,128)(2,1)S(1)} %slice_dynamic-update-slice_fusion.12, bf16[2048,2048]{1,0:T(8,128)(2,1)} %all-gather.11.cloned.1.call-done), kind=kOutput, calls=%fused_computation.9 | convolution fusion | flops 8638167040 | bytes 25182208 | tf_op jit(solution)/shard_map/dot_general | solution.py:26
  433.2 11.3 %convolution_convert_fusion.3 = bf16[1024,2048]{1,0:T(8,128)(2,1)S(1)} fusion(bf16[1024,2048]{1,0:T(8,128)(2,1)S(1)} %get-tuple-element.193, bf16[2048,2048]{1,0:T(8,128)(2,1)} %all-gather.9.cloned.1.call-done), kind=kOutput, calls=%fused_computation.29 | convolution fusion | flops 8592031744 | bytes 16777216 | tf_op jit(solution)/shard_map/dot_general | solution.py:20
  448.5 18.6 %convert_reduce_fusion = (f32[2048]{0:T(1024)S(1)}, bf16[1024,2048]{1,0:T(8,128)(2,1)}) fusion(f32[1024,2048]{1,0:T(8,128)} %get-tuple-element.420, f32[2048]{0:T(1024)S(1)} %dynamic_slice.105, bf16[1024,2048]{1,0:T(8,128)(2,1)S(1)} %slice_dynamic-update-slice_fusion.8, bf16[2048,2048]{1,0:T(8,128)(2,1)} %all-gather.11.cloned.1.call-done), kind=kOutput, calls=%fused_computation.8 | convolution fusion | flops 8638167040 | bytes 25182208 | tf_op jit(solution)/shard_map/dot_general | solution.py:26
  471.0 12.5 %convolution_convert_fusion.2 = bf16[1024,2048]{1,0:T(8,128)(2,1)S(1)} fusion(bf16[1024,2048]{1,0:T(8,128)(2,1)} %get-tuple-element.202, bf16[2048,2048]{1,0:T(8,128)(2,1)} %all-gather.9.cloned.1.call-done), kind=kOutput, calls=%fused_computation.28 | convolution fusion | flops 8592031744 | bytes 16777216 | tf_op jit(solution)/shard_map/dot_general | solution.py:20
  491.6 10.6 %collective-permute-done.41 = bf16[256,2048]{1,0:T(8,128)(2,1)S(1)} collective-permute-done((bf16[256,2048]{1,0:T(8,128)(2,1)S(1)}, bf16[256,2048]{1,0:T(8,128)(2,1)S(1)}, u32[]{:S(2)}, u32[]{:S(2)}) %collective-permute-start.41) | collective-permute-done | bytes 1048608 | tf_op jit(solution)/shard_map/ppermute | solution.py:54
  503.0 11.9 %fusion.65 = f32[2048,2048]{1,0:T(8,128)} fusion(bf16[1024,2048]{1,0:T(8,128)(2,1)S(1)} %copy-done.54, bf16[1024,2048]{1,0:T(8,128)(2,1)S(1)} %copy-done.83), kind=kOutput, calls=%fused_computation.285 | convolution fusion | flops 8589934592 | bytes 25165824 | tf_op jit(solution)/shard_map/dot_general | solution.py:32
  514.9 16.0 %add_convert_fusion.1 = bf16[2048,2048]{1,0:T(8,128)(2,1)} fusion(f32[2048,2048]{1,0:T(8,128)} %fusion.65, bf16[1024,2048]{1,0:T(8,128)(2,1)S(1)} %slice_dynamic-update-slice_fusion.12, bf16[1024,2048]{1,0:T(8,128)(2,1)} %get-tuple-element.172), kind=kOutput, calls=%fused_computation.1 | convolution fusion | flops 8598323200 | bytes 33554432 | tf_op jit(solution)/shard_map/dot_general | solution.py:32
  541.9 17.1 %collective-permute-done.42 = bf16[384,2048]{1,0:T(8,128)(2,1)} collective-permute-done((bf16[384,2048]{1,0:T(8,128)(2,1)}, bf16[384,2048]{1,0:T(8,128)(2,1)}, u32[]{:S(2)}, u32[]{:S(2)}) %collective-permute-start.42) | collective-permute-done | bytes 1572896 | tf_op jit(solution)/shard_map/ppermute | solution.py:54
  577.2 8.9 %collective-permute-done.45 = bf16[128,2048]{1,0:T(8,128)(2,1)S(1)} collective-permute-done((bf16[128,2048]{1,0:T(8,128)(2,1)S(1)}, bf16[128,2048]{1,0:T(8,128)(2,1)S(1)}, u32[]{:S(2)}, u32[]{:S(2)}) %collective-permute-start.45) | collective-permute-done | bytes 524320 | tf_op jit(solution)/shard_map/ppermute | solution.py:54
  594.1 26.4 %attend_back.2 = (bf16[1024,512]{1,0:T(8,128)(2,1)}, f32[2048,512]{1,0:T(8,128)}, f32[2048,512]{1,0:T(8,128)}) custom-call(s32[16]{0:T(128)} %stack.67.lim, bf16[1024,1536]{1,0:T(8,128)(2,1)} %add_convert_fusion.5.q_ref.rest_0_.rest_2_, bf16[1024,512]{1,0:T(8,128)(2,1)} %get-tuple-element.152.o_ref, bf16[1024,512]{1,0:T(8,128)(2,1)} %convolution_convert_fusion.9.do_ref, ...), custom_call_target="tpu_custom_call" | custom-call | flops 21474836480 | bytes 20971520 | tf_op jit(solution)/shard_map/attend_back/pallas_call | solution.py:285
  623.5 15.7 %fusion.66 = f32[2048,2048]{1,0:T(8,128)} fusion(bf16[1024,2048]{1,0:T(8,128)(2,1)} %slice_dynamic-update-slice_fusion.20, bf16[1024,2048]{1,0:T(8,128)(2,1)} %copy-done.81), kind=kOutput, calls=%fused_computation.286 | convolution fusion | flops 8589934592 | bytes 25165824 | tf_op jit(solution)/shard_map/dot_general | solution.py:32
  639.2 14.8 %add_convert_fusion = bf16[2048,2048]{1,0:T(8,128)(2,1)} fusion(f32[2048,2048]{1,0:T(8,128)} %fusion.66, bf16[1024,2048]{1,0:T(8,128)(2,1)S(1)} %copy-done.52, bf16[1024,2048]{1,0:T(8,128)(2,1)S(1)} %copy-done.84), kind=kOutput, calls=%fused_computation | convolution fusion | flops 8598323200 | bytes 33554432 | tf_op jit(solution)/shard_map/dot_general | solution.py:32
  665.8 26.6 %attend_back.3 = (bf16[1024,512]{1,0:T(8,128)(2,1)}, bf16[2048,512]{1,0:T(8,128)(2,1)}, bf16[2048,512]{1,0:T(8,128)(2,1)}) custom-call(s32[16]{0:T(128)} %stack.67.lim, bf16[1024,1536]{1,0:T(8,128)(2,1)} %add_convert_fusion.4.rest_1_.rest_3_.q_ref, bf16[1024,512]{1,0:T(8,128)(2,1)} %get-tuple-element.160.o_ref, ...), custom_call_target="tpu_custom_call" | custom-call | flops 21474836480 | bytes 20971520 | tf_op jit(solution)/shard_map/attend_back/pallas_call | solution.py:285
  697.9 10.5 %convolution_convert_fusion.1 = bf16[1024,2048]{1,0:T(8,128)(2,1)S(1)} fusion(bf16[1024,1536]{1,0:T(8,128)(2,1)} %get-tuple-element.231, bf16[2048,1536]{1,0:T(8,128)(2,1)} %all-gather.5.cloned.1.call-done), kind=kOutput, calls=%fused_computation.27 | convolution fusion | flops 6444548096 | bytes 13631488 | tf_op jit(solution)/shard_map/dot_general | solution.py:20
  744.9 11.0 %collective-permute-done.61 = bf16[256,512]{1,0:T(8,128)(2,1)S(1)} collective-permute-done((bf16[256,512]{1,0:T(8,128)(2,1)S(1)}, bf16[256,512]{1,0:T(8,128)(2,1)S(1)}, u32[]{:S(2)}, u32[]{:S(2)}) %collective-permute-start.61) | collective-permute-done | bytes 262176 | tf_op jit(solution)/shard_map/ppermute | solution.py:413
  755.9 15.7 %collective-permute-start.65 = (bf16[256,512]{1,0:T(8,128)(2,1)S(1)}, bf16[256,512]{1,0:T(8,128)(2,1)S(1)}, u32[]{:S(2)}, u32[]{:S(2)}) collective-permute-start(bf16[256,512]{1,0:T(8,128)(2,1)S(1)} %get-tuple-element.260), channel_id=1, source_target_pairs={{0,24},{4,28},{8,0},{12,4},{16,8},{20,12},{24,16},{28,20},{1,25},{... | collective-permute-start | bytes 786440 | tf_op jit(solution)/shard_map/ppermute | solution.py:413
  824.0 11.8 %collective-permute-done.68 = bf16[256,512]{1,0:T(8,128)(2,1)S(1)} collective-permute-done((bf16[256,512]{1,0:T(8,128)(2,1)S(1)}, bf16[256,512]{1,0:T(8,128)(2,1)S(1)}, u32[]{:S(2)}, u32[]{:S(2)}) %collective-permute-start.68) | collective-permute-done | bytes 262176 | tf_op jit(solution)/shard_map/ppermute | solution.py:413
  846.4 9.8 %collective-permute-start.79 = (f32[768]{0:T(1024)S(1)}, f32[768]{0:T(1024)S(1)}, u32[]{:S(2)}, u32[]{:S(2)}) collective-permute-start(f32[768]{0:T(1024)S(1)} %get-tuple-element.286), channel_id=1, source_target_pairs={{0,28},{4,0},{8,4},{12,8},{16,12},{20,16},{24,20},{28,24},{1,29},{... | collective-permute-start | bytes 9224 | tf_op jit(solution)/shard_map/ppermute | solution.py:371
  (555 shorter events, 351.1 us)
Async XLA Ops:
  7.2 77.4 %all-gather.5.cloned.1.call-start = ((), (), s32[]{:S(2)}) async-start(), calls=%async_computation.3 | async-start | bytes 7077888 | tf_op jit(solution)/shard_map/all_gather | solution.py:384
  9.4 120.6 %all-gather.7.cloned.1.call-start = ((), (), s32[]{:S(2)}) async-start(), calls=%async_computation.4 | async-start | bytes 2359296 | tf_op jit(solution)/shard_map/all_gather | solution.py:384
  10.2 242.7 %all-gather.9.cloned.1.call-start = ((), (), s32[]{:S(2)}) async-start(), calls=%async_computation.5 | async-start | bytes 9437184 | tf_op jit(solution)/shard_map/all_gather | solution.py:384
  10.9 263.0 %all-gather.11.cloned.1.call-start = ((), (), s32[]{:S(2)}) async-start(), calls=%async_computation.6 | async-start | bytes 9437184 | tf_op jit(solution)/shard_map/all_gather | solution.py:384
  13.4 26.4 %collective-permute-start.1 = (bf16[256,2048]{1,0:T(8,128)(2,1)}, bf16[256,2048]{1,0:T(8,128)(2,1)S(1)}, u32[]{:S(2)}, u32[]{:S(2)}) collective-permute-start(bf16[256,2048]{1,0:T(8,128)(2,1)} %get-tuple-element.384), channel_id=1, source_target_pairs={{0,2},{1,3},{2,0},{3,1},{4,6},{5,7},{6,4},{7,5},{8,10},{9,11},{10,... | collective-permute-start | bytes 3145736 | tf_op jit(solution)/shard_map/ppermute | solution.py:54
  16.4 24.9 %collective-permute-start = (bf16[256,2048]{1,0:T(8,128)(2,1)}, bf16[256,2048]{1,0:T(8,128)(2,1)}, u32[]{:S(2)}, u32[]{:S(2)}) collective-permute-start(bf16[256,2048]{1,0:T(8,128)(2,1)} %get-tuple-element.384), channel_id=1, source_target_pairs={{0,1},{1,0},{2,3},{3,2},{4,5},{5,4},{6,7},{7,6},{8,9},{9,8},{10,11... | collective-permute-start | bytes 3145736 | tf_op jit(solution)/shard_map/ppermute | solution.py:54
  17.9 680.0 %reduce-scatter.4.cloned.1.call-start = ((), (), s32[]{:S(2)}) async-start(), calls=%async_computation.7 | async-start | bytes 9437184 | tf_op jit(solution)/shard_map/reduce_scatter | solution.py:388
  197.1 34.2 %collective-permute-start.14 = (bf16[384,2048]{1,0:T(8,128)(2,1)}, bf16[384,2048]{1,0:T(8,128)(2,1)S(1)}, u32[]{:S(2)}, u32[]{:S(2)}) collective-permute-start(bf16[384,2048]{1,0:T(8,128)(2,1)} %get-tuple-element.166), channel_id=1, source_target_pairs={{0,1},{1,0},{2,3},{3,2},{4,5},{5,4},{6,7},{7,6},{8,9},{9,8},{10,11... | collective-permute-start | bytes 4718600 | tf_op jit(solution)/shard_map/ppermute | solution.py:54
  198.1 33.3 %collective-permute-start.15 = (bf16[384,2048]{1,0:T(8,128)(2,1)}, bf16[384,2048]{1,0:T(8,128)(2,1)S(1)}, u32[]{:S(2)}, u32[]{:S(2)}) collective-permute-start(bf16[384,2048]{1,0:T(8,128)(2,1)} %get-tuple-element.167), channel_id=1, source_target_pairs={{0,2},{1,3},{2,0},{3,1},{4,6},{5,7},{6,4},{7,5},{8,10},{9,11},{10,... | collective-permute-start | bytes 4718600 | tf_op jit(solution)/shard_map/ppermute | solution.py:54
  291.3 23.6 %collective-permute-start.23 = (bf16[256,2048]{1,0:T(8,128)(2,1)S(1)}, bf16[256,2048]{1,0:T(8,128)(2,1)S(1)}, u32[]{:S(2)}, u32[]{:S(2)}) collective-permute-start(bf16[256,2048]{1,0:T(8,128)(2,1)S(1)} %get-tuple-element.361), channel_id=1, source_target_pairs={{0,2},{1,3},{2,0},{3,1},{4,6},{5,7},{6,4},{7,5},{8,10},{9,11},{10,... | collective-permute-start | bytes 3145736 | tf_op jit(solution)/shard_map/ppermute | solution.py:54
  292.9 23.2 %collective-permute-start.22 = (bf16[256,2048]{1,0:T(8,128)(2,1)S(1)}, bf16[256,2048]{1,0:T(8,128)(2,1)S(1)}, u32[]{:S(2)}, u32[]{:S(2)}) collective-permute-start(bf16[256,2048]{1,0:T(8,128)(2,1)S(1)} %get-tuple-element.362), channel_id=1, source_target_pairs={{0,1},{1,0},{2,3},{3,2},{4,5},{5,4},{6,7},{7,6},{8,9},{9,8},{10,11... | collective-permute-start | bytes 3145736 | tf_op jit(solution)/shard_map/ppermute | solution.py:54
  357.3 32.0 %collective-permute-start.28 = (bf16[384,2048]{1,0:T(8,128)(2,1)S(1)}, bf16[384,2048]{1,0:T(8,128)(2,1)S(1)}, u32[]{:S(2)}, u32[]{:S(2)}) collective-permute-start(bf16[384,2048]{1,0:T(8,128)(2,1)S(1)} %get-tuple-element.187), channel_id=1, source_target_pairs={{0,2},{1,3},{2,0},{3,1},{4,6},{5,7},{6,4},{7,5},{8,10},{9,11},{10,... | collective-permute-start | bytes 4718600 | tf_op jit(solution)/shard_map/ppermute | solution.py:54
  357.7 32.2 %collective-permute-start.29 = (bf16[384,2048]{1,0:T(8,128)(2,1)S(1)}, bf16[384,2048]{1,0:T(8,128)(2,1)S(1)}, u32[]{:S(2)}, u32[]{:S(2)}) collective-permute-start(bf16[384,2048]{1,0:T(8,128)(2,1)S(1)} %get-tuple-element.188), channel_id=1, source_target_pairs={{0,1},{1,0},{2,3},{3,2},{4,5},{5,4},{6,7},{7,6},{8,9},{9,8},{10,11... | collective-permute-start | bytes 4718600 | tf_op jit(solution)/shard_map/ppermute | solution.py:54
  531.0 305.7 %reduce-scatter.8.cloned.1.call-start = ((), (), s32[]{:S(2)}) async-start(), calls=%async_computation.9 | async-start | bytes 9437184 | tf_op jit(solution)/shard_map/reduce_scatter | solution.py:388
  535.0 24.0 %collective-permute-start.42 = (bf16[384,2048]{1,0:T(8,128)(2,1)}, bf16[384,2048]{1,0:T(8,128)(2,1)}, u32[]{:S(2)}, u32[]{:S(2)}) collective-permute-start(bf16[384,2048]{1,0:T(8,128)(2,1)} %get-tuple-element.208), channel_id=1, source_target_pairs={{0,1},{1,0},{2,3},{3,2},{4,5},{5,4},{6,7},{7,6},{8,9},{9,8},{10,11... | collective-permute-start | bytes 4718600 | tf_op jit(solution)/shard_map/ppermute | solution.py:54
  535.3 24.6 %collective-permute-start.43 = (bf16[384,2048]{1,0:T(8,128)(2,1)}, bf16[384,2048]{1,0:T(8,128)(2,1)}, u32[]{:S(2)}, u32[]{:S(2)}) collective-permute-start(bf16[384,2048]{1,0:T(8,128)(2,1)} %get-tuple-element.209), channel_id=1, source_target_pairs={{0,2},{1,3},{2,0},{3,1},{4,6},{5,7},{6,4},{7,5},{8,10},{9,11},{10,... | collective-permute-start | bytes 4718600 | tf_op jit(solution)/shard_map/ppermute | solution.py:54
  586.6 34.0 %collective-permute-start.47 = (bf16[256,2048]{1,0:T(8,128)(2,1)S(1)}, bf16[256,2048]{1,0:T(8,128)(2,1)S(1)}, u32[]{:S(2)}, u32[]{:S(2)}) collective-permute-start(bf16[256,2048]{1,0:T(8,128)(2,1)S(1)} %get-tuple-element.218), channel_id=1, source_target_pairs={{0,2},{1,3},{2,0},{3,1},{4,6},{5,7},{6,4},{7,5},{8,10},{9,11},{10,... | collective-permute-start | bytes 3145736 | tf_op jit(solution)/shard_map/ppermute | solution.py:54
  587.7 32.8 %collective-permute-start.46 = (bf16[256,2048]{1,0:T(8,128)(2,1)S(1)}, bf16[256,2048]{1,0:T(8,128)(2,1)S(1)}, u32[]{:S(2)}, u32[]{:S(2)}) collective-permute-start(bf16[256,2048]{1,0:T(8,128)(2,1)S(1)} %get-tuple-element.218), channel_id=1, source_target_pairs={{0,1},{1,0},{2,3},{3,2},{4,5},{5,4},{6,7},{7,6},{8,9},{9,8},{10,11... | collective-permute-start | bytes 3145736 | tf_op jit(solution)/shard_map/ppermute | solution.py:54
  621.4 34.4 %collective-permute-start.49 = (bf16[128,2048]{1,0:T(8,128)(2,1)}, bf16[128,2048]{1,0:T(8,128)(2,1)S(1)}, u32[]{:S(2)}, u32[]{:S(2)}) collective-permute-start(bf16[128,2048]{1,0:T(8,128)(2,1)} %slice.666), channel_id=1, source_target_pairs={{0,1},{1,0},{2,3},{3,2},{4,5},{5,4},{6,7},{7,6},{8,9},{9,8},{10,11... | collective-permute-start | bytes 1572872 | tf_op jit(solution)/shard_map/ppermute | solution.py:54
  622.7 33.1 %collective-permute-start.48 = (bf16[128,2048]{1,0:T(8,128)(2,1)S(1)}, bf16[128,2048]{1,0:T(8,128)(2,1)}, u32[]{:S(2)}, u32[]{:S(2)}) collective-permute-start(bf16[128,2048]{1,0:T(8,128)(2,1)S(1)} %slice.665), channel_id=1, source_target_pairs={{0,2},{1,3},{2,0},{3,1},{4,6},{5,7},{6,4},{7,5},{8,10},{9,11},{10,... | collective-permute-start | bytes 1572872 | tf_op jit(solution)/shard_map/ppermute | solution.py:54
  654.0 215.0 %reduce-scatter.6.cloned.1.call-start = ((), (), s32[]{:S(2)}) async-start(), calls=%async_computation.8 | async-start | bytes 2359296 | tf_op jit(solution)/shard_map/reduce_scatter | solution.py:388
  728.3 27.6 %collective-permute-start.61 = (bf16[256,512]{1,0:T(8,128)(2,1)S(1)}, bf16[256,512]{1,0:T(8,128)(2,1)S(1)}, u32[]{:S(2)}, u32[]{:S(2)}) collective-permute-start(bf16[256,512]{1,0:T(8,128)(2,1)S(1)} %get-tuple-element.254), channel_id=1, source_target_pairs={{0,16},{4,20},{8,24},{12,28},{16,0},{20,4},{24,8},{28,12},{1,17},{... | collective-permute-start | bytes 786440 | tf_op jit(solution)/shard_map/ppermute | solution.py:413
  728.4 27.5 %collective-permute-start.62 = (bf16[256,512]{1,0:T(8,128)(2,1)S(1)}, bf16[256,512]{1,0:T(8,128)(2,1)S(1)}, u32[]{:S(2)}, u32[]{:S(2)}) collective-permute-start(bf16[256,512]{1,0:T(8,128)(2,1)S(1)} %get-tuple-element.255), channel_id=1, source_target_pairs={{0,24},{4,28},{8,0},{12,4},{16,8},{20,12},{24,16},{28,20},{1,25},{... | collective-permute-start | bytes 786440 | tf_op jit(solution)/shard_map/ppermute | solution.py:413
  732.5 50.0 %collective-permute-start.52 = (bf16[128,2048]{1,0:T(8,128)(2,1)S(1)}, bf16[128,2048]{1,0:T(8,128)(2,1)S(1)}, u32[]{:S(2)}, u32[]{:S(2)}) collective-permute-start(bf16[128,2048]{1,0:T(8,128)(2,1)S(1)} %get-tuple-element.239), channel_id=1, source_target_pairs={{0,2},{1,3},{2,0},{3,1},{4,6},{5,7},{6,4},{7,5},{8,10},{9,11},{10,... | collective-permute-start | bytes 1572872 | tf_op jit(solution)/shard_map/ppermute | solution.py:54
  740.8 41.7 %collective-permute-start.53 = (bf16[128,2048]{1,0:T(8,128)(2,1)S(1)}, bf16[128,2048]{1,0:T(8,128)(2,1)S(1)}, u32[]{:S(2)}, u32[]{:S(2)}) collective-permute-start(bf16[128,2048]{1,0:T(8,128)(2,1)S(1)} %get-tuple-element.240), channel_id=1, source_target_pairs={{0,1},{1,0},{2,3},{3,2},{4,5},{5,4},{6,7},{7,6},{8,9},{9,8},{10,11... | collective-permute-start | bytes 1572872 | tf_op jit(solution)/shard_map/ppermute | solution.py:54
  744.9 27.7 %collective-permute-start.63 = (bf16[256,512]{1,0:T(8,128)(2,1)S(1)}, bf16[256,512]{1,0:T(8,128)(2,1)S(1)}, u32[]{:S(2)}, u32[]{:S(2)}) collective-permute-start(bf16[256,512]{1,0:T(8,128)(2,1)S(1)} %get-tuple-element.258), channel_id=1, source_target_pairs={{0,8},{4,12},{8,16},{12,20},{16,24},{20,28},{24,0},{28,4},{1,9},{5... | collective-permute-start | bytes 786440 | tf_op jit(solution)/shard_map/ppermute | solution.py:413
  755.9 23.1 %collective-permute-start.64 = (bf16[256,512]{1,0:T(8,128)(2,1)S(1)}, bf16[256,512]{1,0:T(8,128)(2,1)S(1)}, u32[]{:S(2)}, u32[]{:S(2)}) collective-permute-start(bf16[256,512]{1,0:T(8,128)(2,1)S(1)} %get-tuple-element.259), channel_id=1, source_target_pairs={{0,16},{4,20},{8,24},{12,28},{16,0},{20,4},{24,8},{28,12},{1,17},{... | collective-permute-start | bytes 786440 | tf_op jit(solution)/shard_map/ppermute | solution.py:413
  755.9 25.7 %collective-permute-start.65 = (bf16[256,512]{1,0:T(8,128)(2,1)S(1)}, bf16[256,512]{1,0:T(8,128)(2,1)S(1)}, u32[]{:S(2)}, u32[]{:S(2)}) collective-permute-start(bf16[256,512]{1,0:T(8,128)(2,1)S(1)} %get-tuple-element.260), channel_id=1, source_target_pairs={{0,24},{4,28},{8,0},{12,4},{16,8},{20,12},{24,16},{28,20},{1,25},{... | collective-permute-start | bytes 786440 | tf_op jit(solution)/shard_map/ppermute | solution.py:413
  791.7 25.9 %collective-permute-start.56 = (bf16[256,2048]{1,0:T(8,128)(2,1)}, bf16[256,2048]{1,0:T(8,128)(2,1)}, u32[]{:S(2)}, u32[]{:S(2)}) collective-permute-start(bf16[256,2048]{1,0:T(8,128)(2,1)} %get-tuple-element.333), channel_id=1, source_target_pairs={{0,2},{1,3},{2,0},{3,1},{4,6},{5,7},{6,4},{7,5},{8,10},{9,11},{10,... | collective-permute-start | bytes 3145736 | tf_op jit(solution)/shard_map/ppermute | solution.py:54
  793.1 25.6 %collective-permute-start.55 = (bf16[256,2048]{1,0:T(8,128)(2,1)}, bf16[256,2048]{1,0:T(8,128)(2,1)}, u32[]{:S(2)}, u32[]{:S(2)}) collective-permute-start(bf16[256,2048]{1,0:T(8,128)(2,1)} %get-tuple-element.334), channel_id=1, source_target_pairs={{0,1},{1,0},{2,3},{3,2},{4,5},{5,4},{6,7},{7,6},{8,9},{9,8},{10,11... | collective-permute-start | bytes 3145736 | tf_op jit(solution)/shard_map/ppermute | solution.py:54
  808.4 27.3 %collective-permute-start.68 = (bf16[256,512]{1,0:T(8,128)(2,1)S(1)}, bf16[256,512]{1,0:T(8,128)(2,1)S(1)}, u32[]{:S(2)}, u32[]{:S(2)}) collective-permute-start(bf16[256,512]{1,0:T(8,128)(2,1)S(1)} %get-tuple-element.264), channel_id=1, source_target_pairs={{0,16},{4,20},{8,24},{12,28},{16,0},{20,4},{24,8},{28,12},{1,17},{... | collective-permute-start | bytes 786440 | tf_op jit(solution)/shard_map/ppermute | solution.py:413
  809.5 26.3 %collective-permute-start.69 = (bf16[256,512]{1,0:T(8,128)(2,1)S(1)}, bf16[256,512]{1,0:T(8,128)(2,1)S(1)}, u32[]{:S(2)}, u32[]{:S(2)}) collective-permute-start(bf16[256,512]{1,0:T(8,128)(2,1)S(1)} %get-tuple-element.265), channel_id=1, source_target_pairs={{0,24},{4,28},{8,0},{12,4},{16,8},{20,12},{24,16},{28,20},{1,25},{... | collective-permute-start | bytes 786440 | tf_op jit(solution)/shard_map/ppermute | solution.py:413
  (142 other events, 2295.1 us)
Sparse Core Ops, SparseCore 0:
  10.2 67.4 all-gather.4
  79.3 27.7 all-gather.6
  108.7 81.4 all-gather.8
  191.6 80.5 all-gather.10
  531.0 87.1 reduce-scatter.3
  654.2 93.2 reduce-scatter.7
  800.9 51.1 reduce-scatter.5

commit v4 on v3

--- a/solution.py
+++ b/solution.py
@@ -114,10 +114,10 @@
     return [swap(value, p) for p, value in enumerate(scatter_sums(near, *others), 1)]
 
 
-def scatter_far_gather_near(near, own, *others):
-    sums = scatter_sums(near, *others)
+def scatter_far_gather_near(near, own):
+    sums = scatter_sums(near)
     if not sums:
-        return [], gather_near(own, *near[1], *others)
+        return [], gather_near(own, *near[1])
     half = sums[0].shape[0]
     pieces = together([jnp.concatenate([value, own], axis=0) for value in sums])
     came = [swap(value, p) for p, value in enumerate(pieces, 1)]
@@ -388,33 +388,6 @@
     return lax.psum_scatter(grad, "dp", scatter_dimension=0, tiled=True)
 
 
-def pair_exchange(grad):
-    slots = lax.axis_size("dp")
-    side = lax.axis_index("dp") % 2
-    blocks = grad.reshape(slots // 2, 2, grad.shape[0] // slots, grad.shape[1])
-    give = lax.dynamic_index_in_dim(blocks, 1 - side, 1, keepdims=False)
-    kept = lax.dynamic_index_in_dim(blocks, side, 1, keepdims=False)
-    return kept, lax.ppermute(give, "dp", [(i, i ^ 1) for i in range(slots)])
-
-
-def pair_scatter(pair, *others):
-    slots = lax.axis_size("dp")
-    pairs = slots // 2
-    own = lax.axis_index("dp") // 2
-    kept, came = pair
-    total = low(wide(kept) + wide(after(came, *others)))
-    ahead = together(
-        [
-            lax.dynamic_index_in_dim(total, (own + step) % pairs, 0, keepdims=False)
-            for step in range(pairs)
-        ]
-    )
-    return [ahead[0]] + [
-        lax.ppermute(ahead[step], "dp", [(i, (i + 2 * step) % slots) for i in range(slots)])
-        for step in range(1, pairs)
-    ]
-
-
 def add_up(terms):
     total = terms[0]
     for term in terms[1:]:
@@ -489,7 +462,6 @@
         )
         projected[c] = low(nn(seq_tokens[c], proj_full) + bias_proj)
 
-    down_terms, up_terms = [], []
     context, lse, attn_low = lists(3)
     context[0], lse[0] = attend(0, projected, limits, run)
     attn_low[0] = low(nt(context[0], out_full))
@@ -522,17 +494,13 @@
         )
         return (grad_sum, (gain_part, shift_part, jnp.sum(grad_sum, axis=0)), low(grad_sum))
 
-    def turn(terms, norm, filler=None):
+    def turn(terms, norm):
         near[1] = scatter_near(terms, *far[0])
         results = [norm(0), None]
         out = results[0][-1]
-        if filler is not None:
-            filler(0, (out,))
         far[1], near[0] = scatter_far_gather_near(near[1], out)
-        if filler is not None:
-            filler(1, tuple(near[1][1]))
         results[1] = norm(1)
-        far[0] = gather_far(near[0], *down_terms[1:])
+        far[0] = gather_far(near[0])
         whole = gathered(out, near[0], far[0])
         near[1] = gather_near(results[1][-1], *(far[0] or near[0]))
         return results, after(whole, results[1][-1])
@@ -558,34 +526,43 @@
     far[1] = gather_far(near[1])
     mid_low[0] = low(nt(after(grad_pre[0], *near[1]), up_full))
     grad_ffn[1] = gathered(grad_out2[1], near[1], far[1])
+    grad_sum1, vec1, grad_out1, grad_attn, grad_query, attn_near, attn_far = lists(7)
+    down_terms, up_terms = lists(2)
     near[0] = scatter_near(mid_low[0], *(far[1] or near[1]))
-    grad_pre[1] = low(nn(after(grad_ffn[1], mid_low[0]), down_full) * wide(slope[1]))
+    down_terms[1] = tn(after(grad_ffn[1], mid_low[0]), activ[1])
     far[0] = scatter_far(near[0])
-    mid_low[1] = low(nt(after(grad_pre[1], *near[0][1]), up_full))
-
-    def down_term(c, others):
-        down_terms.append(tn(after(grad_ffn[c], *others), activ[c]))
-
-    results, source = turn(mid_low[1], first_norm_back, down_term)
-    down_grad = low(add_up(down_terms))
-    down_part = scatter_weight(down_grad)
+    down_terms[0] = tn(after(grad_ffn[0], down_terms[1], *near[0][1]), activ[0])
+    down_grad = low(add_up(down_terms[::-1]))
+    down_part = scatter_weight(after(down_grad, *far[0]))
+    grad_sum1[0], vec1[0], grad_out1[0] = first_norm_back(0)
+    attn_near[0] = gather_near(grad_out1[0], *far[0])
+    grad_pre[1] = low(
+        nn(after(grad_ffn[1], down_grad, grad_out1[0]), down_full) * wide(slope[1])
+    )
+    attn_far[0] = gather_far(attn_near[0])
+    mid_low[1] = low(nt(after(grad_pre[1], *attn_near[0]), up_full))
+    grad_attn[0] = gathered(grad_out1[0], attn_near[0], attn_far[0])
+    near[1] = scatter_near(mid_low[1], *(attn_far[0] or attn_near[0]))
+    up_terms[0] = tn(
+        after(mid_seq[0], mid_low[1], *(attn_far[0] or attn_near[0])), grad_pre[0]
+    )
+    far[1] = scatter_far(near[1])
+    up_terms[1] = tn(after(mid_seq[1], up_terms[0], *near[1][1]), grad_pre[1])
+    up_grad = low(add_up(up_terms))
+    up_part = scatter_weight(after(up_grad, *far[1]))
     up_bias_part = add_up([jnp.sum(wide(grad_pre[c]), axis=0) for c in every])
-    grad_sum1, vec1, grad_out1 = zip(*results)
-    grad_attn, grad_query = lists(2)
-    grad_attn[0] = source
-    grad_context = low(nn(after(source, down_grad), out_full))
+    grad_sum1[1], vec1[1], grad_out1[1] = first_norm_back(1)
+    attn_near[1] = gather_near(grad_out1[1], *far[1])
+    grad_context = low(nn(after(grad_attn[0], up_grad, grad_out1[1]), out_full))
     grad_query[0], *carry = attend_back(
         0, projected, context[0], grad_context, lse[0], limits, run, None
     )
-    far[1] = gather_far(near[1], grad_query[0])
-    up_terms.append(tn(after(mid_seq[0], grad_query[0], *near[1]), grad_pre[0]))
-    up_terms.append(tn(after(mid_seq[1], up_terms[0]), grad_pre[1]))
-    up_grad = low(add_up(up_terms))
-    up_part = scatter_weight(up_grad)
-    grad_attn[1] = gathered(
-        grad_out1[1], near[1], together(far[1], up_terms[0]) if far[1] else []
-    )
-    grad_context = low(nn(after(grad_attn[1], up_grad), out_full))
+    attn_far[1] = gather_far(attn_near[1])
+    out_term = tn(after(grad_attn[0], grad_query[0], *attn_near[1]), context[0])
+    grad_attn[1] = gathered(grad_out1[1], attn_near[1], attn_far[1])
+    out_grad = low(out_term + tn(grad_attn[1], context[1]))
+    out_part = scatter_weight(out_grad)
+    grad_context = low(nn(after(grad_attn[1], out_grad), out_full))
     grad_query[1], *carry = attend_back(
         1, projected, context[1], grad_context, lse[1], limits, run, carry
     )
@@ -596,34 +573,25 @@
     ]
     tokens_low, tokens_grad = lists(2)
 
-    def proj_term(i, *others):
-        cols = slice(i * head_cols, (i + 1) * head_cols)
-        return low(
-            add_up([tn(after(seq_tokens[c], *others), grad_proj[c][:, cols]) for c in every])
-        )
-
-    tokens_low[0] = low(nt(after(grad_proj[0], up_grad, down_part), proj_full))
+    proj_terms = [None] * CHUNKS
+    tokens_low[0] = low(nt(after(grad_proj[0], down_part), proj_full))
     near[0] = scatter_near(tokens_low[0])
-    proj_grad, pair, proj_came = [None] * 3, [None] * 3, [None] * 3
-    proj_grad[0] = proj_term(0, tokens_low[0])
-    pair[0] = pair_exchange(proj_grad[0])
-    proj_grad[1] = proj_term(1, proj_grad[0])
-    pair[1] = pair_exchange(proj_grad[1])
-    proj_came[0] = pair_scatter(pair[0], proj_grad[1])
-    far[0] = scatter_far(near[0], proj_grad[1])
-    tokens_low[1] = low(nt(after(grad_proj[1], pair[0][1], *near[0][1]), proj_full))
+    proj_terms[0] = tn(after(seq_tokens[0], tokens_low[0]), grad_proj[0])
+    far[0] = scatter_far(near[0])
+    tokens_low[1] = low(nt(after(grad_proj[1], proj_terms[0], *near[0][1]), proj_full))
     near[1] = scatter_near(tokens_low[1], *far[0])
-    proj_came[1] = pair_scatter(pair[1], tokens_low[1])
-    proj_grad[2] = proj_term(2, tokens_low[1], pair[1][1], *far[0])
-    pair[2] = pair_exchange(proj_grad[2])
-    out_grad = low(add_up([tn(after(grad_attn[c], proj_grad[2]), context[c]) for c in every]))
-    out_part = scatter_weight(out_grad)
-    far[1] = scatter_far(near[1], out_grad)
-    proj_came[2] = pair_scatter(pair[2], out_grad, *proj_came[0])
+    proj_terms[1] = tn(after(seq_tokens[1], tokens_low[1], *far[0]), grad_proj[1])
+    proj_grad = low(add_up(proj_terms))
+    proj_part = scatter_weight(after(proj_grad, *near[1][1]))
+    far[1] = scatter_far(near[1])
+    early = together((*(far[1] or near[1][1]), up_part))
+    if far[1]:
+        far[1] = early[:-1]
+    up_part = early[-1]
+    out_part = after(out_part, up_part)
     for c in every:
         tokens_grad[c] = low(grad_sum1[c] + scattered(near[c], far[c]))
-    out_part, up_part, down_part = map(wide, (out_part, up_part, down_part))
-    proj_part = [add_up([wide(v) for v in came]) for came in proj_came]
+    proj_part, out_part, up_part, down_part = map(wide, (proj_part, out_part, up_part, down_part))
     proj_bias = add_up([jnp.sum(wide(grad_proj[c]), axis=0) for c in every])
     (
         norm2_gain_grad,
@@ -647,7 +615,9 @@
     return (
         jnp.concatenate(layer_out, axis=0),
         jnp.concatenate(tokens_grad, axis=0),
-        *proj_part,
+        proj_part[:, :head_cols],
+        proj_part[:, head_cols : 2 * head_cols],
+        proj_part[:, 2 * head_cols :],
         out_part,
         up_part,
         down_part,

time: 891 us -> 835 us (0.937)
  starting transfers between devices: 110 us -> 71.8 us
  waiting for transfers between devices: 265 us -> 246 us
    ppermute x12 -> x0, waiting for transfers between devices: 34.6 us -> none  [the longest x9 34.5 us: pair_scatter(): lax.ppermute(ahead[step], 'dp', [(i, (i + 2 * step) % slots) for i in ran...]
    ppermute x12 -> x0, starting transfers between devices: 26.5 us -> none  [the longest x9 25.9 us: pair_scatter(): lax.ppermute(ahead[step], 'dp', [(i, (i + 2 * step) % slots) for i in ran...]
    reduce_scatter x3 -> x4, waiting for transfers between devices: 0.01 us -> 24.9 us  [scatter_weight(): return lax.psum_scatter(grad, 'dp', scatter_dimension=0, tiled=True)]
    ppermute x7, starting transfers between devices: 16.1 us -> 5.13 us  [total_of(): lax.ppermute(ahead(step), 'dp', [(i, (i + step) % slots) for i in range(s...]
    ppermute x61 -> x63, waiting for transfers between devices: 226 us -> 218 us  [swap(): return lax.ppermute(value, 'tensor', [(i, i ^ bits) for i in range(size)])]
    unnamed x217 -> x233, local copies, waits for them, and re-layouts: 34.4 us -> 40.1 us
    dot_general x12 -> x8, matrix products: 86.6 us -> 89.5 us  [tn(): lax.dot_general(left, right, (((0,), (0,)), ((), ())), preferred_element_...]
    ppermute x61 -> x63, starting transfers between devices: 66.6 us -> 66.4 us  [swap(): return lax.ppermute(value, 'tensor', [(i, i ^ bits) for i in range(size)])]
  transfers between devices with their start and end apart: 87 -> 78, of which waited for: 45 -> 45; matrix products, arithmetic and copies ran while one was open for 40% -> 46% of each run, Pallas kernels for 10% -> 11%
where the time goes in v4:
time: 835 us; the launch traced here: 824 us
  matrix products  262 us (31%)
  waiting for transfers between devices  246 us (29%)
  Pallas kernels  91.3 us (11%)
  starting transfers between devices  71.8 us (9%)
  local copies, waits for them, and re-layouts  69.2 us (8%)
  other arithmetic  66.4 us (8%)
  between operations  17.1 us (2%)
    ppermute x63, waiting for transfers between devices, swap(): return lax.ppermute(value, 'tensor', [(i, i ^ bits) for i in range(size)])  218 us
    dot_general x8, matrix products, nn(): lax.dot_general(left, right, (((1,), (0,)), ((), ())), preferred_element_...  102 us
    dot_general x8, matrix products, tn(): lax.dot_general(left, right, (((0,), (0,)), ((), ())), preferred_element_...  89.5 us
    dot_general x8, matrix products, nt(): lax.dot_general(left, right, (((1,), (1,)), ((), ())), preferred_element_...  70.3 us
    ppermute x63, starting transfers between devices, swap(): return lax.ppermute(value, 'tensor', [(i, i ^ bits) for i in range(size)])  66.4 us
    pallas_call x2, Pallas kernels, attend_back(): pl.pallas_call(kernel, out_shape=(jax.ShapeDtypeStruct((part, cols), jnp....  53.4 us
    unnamed x233, local copies, waits for them, and re-layouts  40.1 us
    pallas_call x2, Pallas kernels, attend(): pl.pallas_call(kernel, out_shape=(jax.ShapeDtypeStruct((part, cols), jnp....  37.8 us
  transfers between devices with their start and end apart: 78, of which 45 were waited for; matrix products, arithmetic and copies ran while one was open for 46% of the time, Pallas kernels for 11%

profile of v4, /device:TPU:0, one launch (start us, length us, event | category | flops | bytes accessed | tf_op | source)
XLA Modules:
  0.0 823.6 jit_solution(4557413868282706483)
XLA Ops:
  20.7 19.0 %collective-permute-done = bf16[256,2048]{1,0:T(8,128)(2,1)} collective-permute-done((bf16[256,2048]{1,0:T(8,128)(2,1)}, bf16[256,2048]{1,0:T(8,128)(2,1)}, u32[]{:S(2)}, u32[]{:S(2)}) %collective-permute-start) | collective-permute-done | bytes 1048608 | tf_op jit(solution)/shard_map/ppermute | solution.py:54
  47.1 7.7 collective-permute-done.2
  61.7 17.3 %collective-permute-done.4 = bf16[256,2048]{1,0:T(8,128)(2,1)S(1)} collective-permute-done((bf16[256,2048]{1,0:T(8,128)(2,1)S(1)}, bf16[256,2048]{1,0:T(8,128)(2,1)S(1)}, u32[]{:S(2)}, u32[]{:S(2)}) %collective-permute-start.4) | collective-permute-done | bytes 1048608 | tf_op jit(solution)/shard_map/ppermute | solution.py:54
  84.7 11.6 %add_convert_fusion.6.q_ref.rest_0_.rest_2_ = bf16[1024,1536]{1,0:T(8,128)(2,1)} fusion(bf16[1024,2048]{1,0:T(8,128)(2,1)} %slice_dynamic-update-slice_fusion.28, bf16[2048,1536]{1,0:T(8,128)(2,1)} %all-gather.5.cloned.1.call-done, f32[1536]{0:T(1024)S(1)} %pad_maximum_fusion.9), kind=kOutput, calls=%fused_computation.22 | convolution fusion | flops 6445596672 | bytes 13637632 | tf_op jit(solution)/shard_map/dot_general | solution.py:26
  101.8 9.6 %add_convert_fusion.5.rest_1_.rest_3_.q_ref = bf16[1024,1536]{1,0:T(8,128)(2,1)} fusion(bf16[1024,2048]{1,0:T(8,128)(2,1)} %slice_dynamic-update-slice_fusion.24, bf16[2048,1536]{1,0:T(8,128)(2,1)S(1)} %copy-done.79, f32[1536]{0:T(1024)S(1)} %pad_maximum_fusion.9), kind=kOutput, calls=%fused_computation.21 | convolution fusion | flops 6445596672 | bytes 13637632 | tf_op jit(solution)/shard_map/dot_general | solution.py:26
  111.4 18.8 %attend.2 = (bf16[1024,512]{1,0:T(8,128)(2,1)}, f32[4,1,1024]{2,1,0:T(1,128)}) custom-call(s32[16]{0:T(128)} %stack.67.lim, bf16[1024,1536]{1,0:T(8,128)(2,1)} %add_convert_fusion.6.q_ref.rest_0_.rest_2_, bf16[1024,1536]{1,0:T(8,128)(2,1)} %add_convert_fusion.6.q_ref.rest_0_.rest_2_, bf16[1024,1536]{1,0:T(8,128)(2,1)} %add_convert_fusion.5.rest_1_.rest_3_.q_ref, ...), custom_call_target="tpu_custom_call" | custom-call | flops 8589934592 | bytes 6291456 | tf_op jit(solution)/shard_map/attend/pallas_call | solution.py:193
  138.4 19.0 %attend.3 = (bf16[1024,512]{1,0:T(8,128)(2,1)}, f32[4,1,1024]{2,1,0:T(1,128)}) custom-call(s32[16]{0:T(128)} %stack.67.lim, bf16[1024,1536]{1,0:T(8,128)(2,1)} %add_convert_fusion.5.rest_1_.rest_3_.q_ref, bf16[1024,1536]{1,0:T(8,128)(2,1)} %add_convert_fusion.6.q_ref.rest_0_.rest_2_, bf16[1024,1536]{1,0:T(8,128)(2,1)} %add_convert_fusion.5.rest_1_.rest_3_.q_ref, ...), custom_call_target="tpu_custom_call" | custom-call | flops 8589934592 | bytes 6291456 | tf_op jit(solution)/shard_map/attend/pallas_call | solution.py:193
  179.8 14.8 %collective-permute-done.12 = bf16[256,2048]{1,0:T(8,128)(2,1)S(1)} collective-permute-done((bf16[256,2048]{1,0:T(8,128)(2,1)S(1)}, bf16[256,2048]{1,0:T(8,128)(2,1)S(1)}, u32[]{:S(2)}, u32[]{:S(2)}) %collective-permute-start.12) | collective-permute-done | bytes 1048608 | tf_op jit(solution)/shard_map/ppermute | solution.py:54
  199.8 30.5 %collective-permute-done.14 = bf16[384,2048]{1,0:T(8,128)(2,1)S(1)} collective-permute-done((bf16[384,2048]{1,0:T(8,128)(2,1)}, bf16[384,2048]{1,0:T(8,128)(2,1)S(1)}, u32[]{:S(2)}, u32[]{:S(2)}) %collective-permute-start.14) | collective-permute-done | bytes 1572896 | tf_op jit(solution)/shard_map/ppermute | solution.py:54
  253.5 17.2 %multiply_convert_fusion.3 = (bf16[1024,2048]{1,0:T(8,128)(2,1)}, f32[1024,2048]{1,0:T(8,128)}) fusion(f32[2048]{0:T(1024)S(1)} %dynamic_slice.49, bf16[1024,2048]{1,0:T(8,128)(2,1)} %slice_dynamic-update-slice_fusion.20, bf16[2048,2048]{1,0:T(8,128)(2,1)} %all-gather.9.cloned.1.call-done), kind=kOutput, calls=%fused_computation.17 | convolution fusion | flops 8610906112 | bytes 25174016 | tf_op jit(solution)/shard_map/dot_general | solution.py:26
  275.4 12.7 %convolution_convert_fusion.5 = bf16[1024,2048]{1,0:T(8,128)(2,1)S(1)} fusion(bf16[1024,2048]{1,0:T(8,128)(2,1)} %get-tuple-element.155, bf16[2048,2048]{1,0:T(8,128)(2,1)} %all-gather.11.cloned.1.call-done), kind=kOutput, calls=%fused_computation.29 | convolution fusion | flops 8592031744 | bytes 16777216 | tf_op jit(solution)/shard_map/dot_general | solution.py:20
  295.2 17.3 %multiply_convert_fusion.2 = (bf16[1024,2048]{1,0:T(8,128)(2,1)}, f32[1024,2048]{1,0:T(8,128)}) fusion(f32[2048]{0:T(1024)S(1)} %dynamic_slice.49, bf16[1024,2048]{1,0:T(8,128)(2,1)S(1)} %slice_dynamic-update-slice_fusion.16, bf16[2048,2048]{1,0:T(8,128)(2,1)} %all-gather.9.cloned.1.call-done), kind=kOutput, calls=%fused_computation.15 | convolution fusion | flops 8610906112 | bytes 25174016 | tf_op jit(solution)/shard_map/dot_general | solution.py:26
  315.5 10.9 %convolution_convert_fusion.4 = bf16[1024,2048]{1,0:T(8,128)(2,1)S(1)} fusion(bf16[1024,2048]{1,0:T(8,128)(2,1)} %get-tuple-element.164, bf16[2048,2048]{1,0:T(8,128)(2,1)S(1)} %bitcast.105), kind=kOutput, calls=%fused_computation.28 | convolution fusion | flops 8592031744 | bytes 16777216 | tf_op jit(solution)/shard_map/dot_general | solution.py:20
  336.9 13.5 %collective-permute-done.26 = bf16[256,2048]{1,0:T(8,128)(2,1)S(1)} collective-permute-done((bf16[256,2048]{1,0:T(8,128)(2,1)S(1)}, bf16[256,2048]{1,0:T(8,128)(2,1)S(1)}, u32[]{:S(2)}, u32[]{:S(2)}) %collective-permute-start.26) | collective-permute-done | bytes 1048608 | tf_op jit(solution)/shard_map/ppermute | solution.py:54
  355.1 30.1 %collective-permute-done.28 = bf16[384,2048]{1,0:T(8,128)(2,1)S(1)} collective-permute-done((bf16[384,2048]{1,0:T(8,128)(2,1)S(1)}, bf16[384,2048]{1,0:T(8,128)(2,1)S(1)}, u32[]{:S(2)}, u32[]{:S(2)}) %collective-permute-start.28) | collective-permute-done | bytes 1572896 | tf_op jit(solution)/shard_map/ppermute | solution.py:54
  393.3 7.9 collective-permute-done.30
  405.7 19.4 %convert_reduce_fusion.1 = (f32[2048]{0:T(1024)}, bf16[1024,2048]{1,0:T(8,128)(2,1)}) fusion(f32[1024,2048]{1,0:T(8,128)} %get-tuple-element.373, f32[2048]{0:T(1024)S(1)} %dynamic_slice.49, bf16[1024,2048]{1,0:T(8,128)(2,1)S(1)} %slice_dynamic-update-slice_fusion.12, bf16[2048,2048]{1,0:T(8,128)(2,1)} %all-gather.11.cloned.1.call-done), kind=kOutput, calls=%fused_computation.10 | convolution fusion | flops 8638167040 | bytes 25182208 | tf_op jit(solution)/shard_map/dot_general | solution.py:26
  428.0 10.7 %convolution_convert_fusion.3 = bf16[1024,2048]{1,0:T(8,128)(2,1)S(1)} fusion(bf16[1024,2048]{1,0:T(8,128)(2,1)} %get-tuple-element.176, bf16[2048,2048]{1,0:T(8,128)(2,1)S(1)} %bitcast.101), kind=kOutput, calls=%fused_computation.27 | convolution fusion | flops 8592031744 | bytes 16777216 | tf_op jit(solution)/shard_map/dot_general | solution.py:20
  444.1 11.7 %fusion.49 = f32[2048,2048]{1,0:T(8,128)} fusion(bf16[1024,2048]{1,0:T(8,128)(2,1)S(1)} %slice_dynamic-update-slice_fusion.4, bf16[1024,2048]{1,0:T(8,128)(2,1)S(1)} %copy-done.83), kind=kOutput, calls=%fused_computation.244 | convolution fusion | flops 8589934592 | bytes 25165824 | tf_op jit(solution)/shard_map/dot_general | solution.py:32
  455.7 7.7 collective-permute-done.36
  466.8 16.2 %add_convert_fusion.1 = bf16[2048,2048]{1,0:T(8,128)(2,1)} fusion(f32[2048,2048]{1,0:T(8,128)} %fusion.49, bf16[1024,2048]{1,0:T(8,128)(2,1)S(1)} %slice_dynamic-update-slice_fusion.12, bf16[1024,2048]{1,0:T(8,128)(2,1)} %get-tuple-element.155), kind=kOutput, calls=%fused_computation.1 | convolution fusion | flops 8598323200 | bytes 33554432 | tf_op jit(solution)/shard_map/dot_general | solution.py:32
  494.6 17.2 %convert_reduce_fusion = (f32[2048]{0:T(1024)}, bf16[1024,2048]{1,0:T(8,128)(2,1)}) fusion(f32[1024,2048]{1,0:T(8,128)} %get-tuple-element.375, f32[2048]{0:T(1024)S(1)} %dynamic_slice.49, bf16[1024,2048]{1,0:T(8,128)(2,1)S(1)} %copy-done.58, bf16[2048,2048]{1,0:T(8,128)(2,1)S(1)} %bitcast.107), kind=kOutput, calls=%fused_computation.9 | convolution fusion | flops 8638167040 | bytes 25182208 | tf_op jit(solution)/shard_map/dot_general | solution.py:26
  516.6 10.7 %convolution_convert_fusion.2 = bf16[1024,2048]{1,0:T(8,128)(2,1)S(1)} fusion(bf16[1024,2048]{1,0:T(8,128)(2,1)} %get-tuple-element.190, bf16[2048,2048]{1,0:T(8,128)(2,1)S(1)} %bitcast.103), kind=kOutput, calls=%fused_computation.26 | convolution fusion | flops 8592031744 | bytes 16777216 | tf_op jit(solution)/shard_map/dot_general | solution.py:20
  532.2 14.4 %fusion.50 = f32[2048,2048]{1,0:T(8,128)} fusion(bf16[1024,2048]{1,0:T(8,128)(2,1)} %slice_dynamic-update-slice_fusion.20, bf16[1024,2048]{1,0:T(8,128)(2,1)S(1)} %copy-done.84), kind=kOutput, calls=%fused_computation.245 | convolution fusion | flops 8589934592 | bytes 25165824 | tf_op jit(solution)/shard_map/dot_general | solution.py:32
  555.3 16.2 %add_convert_fusion = bf16[2048,2048]{1,0:T(8,128)(2,1)} fusion(f32[2048,2048]{1,0:T(8,128)} %fusion.50, bf16[1024,2048]{1,0:T(8,128)(2,1)S(1)} %copy-done.56, bf16[1024,2048]{1,0:T(8,128)(2,1)} %get-tuple-element.190), kind=kOutput, calls=%fused_computation | convolution fusion | flops 8598323200 | bytes 33554432 | tf_op jit(solution)/shard_map/dot_general | solution.py:32
  588.2 26.7 %attend_back.2 = (bf16[1024,512]{1,0:T(8,128)(2,1)}, f32[2048,512]{1,0:T(8,128)}, f32[2048,512]{1,0:T(8,128)}) custom-call(s32[16]{0:T(128)} %stack.67.lim, bf16[1024,1536]{1,0:T(8,128)(2,1)} %add_convert_fusion.6.q_ref.rest_0_.rest_2_, bf16[1024,512]{1,0:T(8,128)(2,1)} %get-tuple-element.135.o_ref, bf16[1024,512]{1,0:T(8,128)(2,1)} %convolution_convert_fusion.9.do_ref, ...), custom_call_target="tpu_custom_call" | custom-call | flops 21474836480 | bytes 20971520 | tf_op jit(solution)/shard_map/attend_back/pallas_call | solution.py:285
  642.2 26.8 %attend_back.3 = (bf16[1024,512]{1,0:T(8,128)(2,1)}, bf16[2048,512]{1,0:T(8,128)(2,1)}, bf16[2048,512]{1,0:T(8,128)(2,1)}) custom-call(s32[16]{0:T(128)} %stack.67.lim, bf16[1024,1536]{1,0:T(8,128)(2,1)} %add_convert_fusion.5.rest_1_.rest_3_.q_ref, bf16[1024,512]{1,0:T(8,128)(2,1)} %get-tuple-element.143.o_ref, ...), custom_call_target="tpu_custom_call" | custom-call | flops 21474836480 | bytes 20971520 | tf_op jit(solution)/shard_map/attend_back/pallas_call | solution.py:285
  679.0 9.9 %convolution_convert_fusion.1 = bf16[1024,2048]{1,0:T(8,128)(2,1)S(1)} fusion(bf16[1024,1536]{1,0:T(8,128)(2,1)} %get-tuple-element.212, bf16[2048,1536]{1,0:T(8,128)(2,1)} %all-gather.5.cloned.1.call-done), kind=kOutput, calls=%fused_computation.25 | convolution fusion | flops 6444548096 | bytes 13631488 | tf_op jit(solution)/shard_map/dot_general | solution.py:20
  692.4 9.6 %fusion.52 = f32[2048,1536]{1,0:T(8,128)} fusion(bf16[1024,2048]{1,0:T(8,128)(2,1)S(1)} %copy-done.51, bf16[1024,1536]{1,0:T(8,128)(2,1)S(1)} %copy-done.26), kind=kOutput, calls=%fused_computation.247 | convolution fusion | flops 6442450944 | bytes 19922944 | tf_op jit(solution)/shard_map/dot_general | solution.py:32
  701.9 8.5 %collective-permute-done.52 = bf16[256,2048]{1,0:T(8,128)(2,1)S(1)} collective-permute-done((bf16[256,2048]{1,0:T(8,128)(2,1)S(1)}, bf16[256,2048]{1,0:T(8,128)(2,1)S(1)}, u32[]{:S(2)}, u32[]{:S(2)}) %collective-permute-start.52) | collective-permute-done | bytes 1048608 | tf_op jit(solution)/shard_map/ppermute | solution.py:54
  726.6 13.1 %add_convert_fusion.2 = bf16[2048,1536]{1,0:T(8,128)(2,1)} fusion(f32[2048,1536]{1,0:T(8,128)} %fusion.52, bf16[1024,2048]{1,0:T(8,128)(2,1)} %slice_dynamic-update-slice_fusion.24, bf16[1024,1536]{1,0:T(8,128)(2,1)S(1)} %copy-done.25), kind=kOutput, calls=%fused_computation.2 | convolution fusion | flops 6448742400 | bytes 26214400 | tf_op jit(solution)/shard_map/dot_general | solution.py:32
  789.1 24.9 %reduce-scatter.9.cloned.1.call-done = bf16[256,1536]{1,0:T(8,128)(2,1)} async-done(((bf16[2048,1536]{1,0:T(8,128)(2,1)}), bf16[256,1536]{1,0:T(8,128)(2,1)}) %reduce-scatter.9.cloned.1.call-update) | async-done | bytes 786448 | tf_op jit(solution)/shard_map/reduce_scatter | solution.py:388
  (540 shorter events, 305.2 us)
Async XLA Ops:
  7.2 77.5 %all-gather.5.cloned.1.call-start = ((), (), s32[]{:S(2)}) async-start(), calls=%async_computation.4 | async-start | bytes 7077888 | tf_op jit(solution)/shard_map/all_gather | solution.py:384
  9.5 120.7 %all-gather.7.cloned.1.call-start = ((), (), s32[]{:S(2)}) async-start(), calls=%async_computation.5 | async-start | bytes 2359296 | tf_op jit(solution)/shard_map/all_gather | solution.py:384
  10.2 243.3 %all-gather.9.cloned.1.call-start = ((), (), s32[]{:S(2)}) async-start(), calls=%async_computation.6 | async-start | bytes 9437184 | tf_op jit(solution)/shard_map/all_gather | solution.py:384
  10.9 264.5 %all-gather.11.cloned.1.call-start = ((), (), s32[]{:S(2)}) async-start(), calls=%async_computation.7 | async-start | bytes 9437184 | tf_op jit(solution)/shard_map/all_gather | solution.py:384
  13.3 26.4 %collective-permute-start = (bf16[256,2048]{1,0:T(8,128)(2,1)}, bf16[256,2048]{1,0:T(8,128)(2,1)}, u32[]{:S(2)}, u32[]{:S(2)}) collective-permute-start(bf16[256,2048]{1,0:T(8,128)(2,1)} %get-tuple-element.350), channel_id=1, source_target_pairs={{0,1},{1,0},{2,3},{3,2},{4,5},{5,4},{6,7},{7,6},{8,9},{9,8},{10,11... | collective-permute-start | bytes 3145736 | tf_op jit(solution)/shard_map/ppermute | solution.py:54
  16.2 24.8 %collective-permute-start.1 = (bf16[256,2048]{1,0:T(8,128)(2,1)}, bf16[256,2048]{1,0:T(8,128)(2,1)S(1)}, u32[]{:S(2)}, u32[]{:S(2)}) collective-permute-start(bf16[256,2048]{1,0:T(8,128)(2,1)} %get-tuple-element.350), channel_id=1, source_target_pairs={{0,2},{1,3},{2,0},{3,1},{4,6},{5,7},{6,4},{7,5},{8,10},{9,11},{10,... | collective-permute-start | bytes 3145736 | tf_op jit(solution)/shard_map/ppermute | solution.py:54
  17.8 661.2 %reduce-scatter.5.cloned.1.call-start = ((), (), s32[]{:S(2)}) async-start(), calls=%async_computation.8 | async-start | bytes 9437184 | tf_op jit(solution)/shard_map/reduce_scatter | solution.py:388
  56.2 22.8 %collective-permute-start.4 = (bf16[256,2048]{1,0:T(8,128)(2,1)S(1)}, bf16[256,2048]{1,0:T(8,128)(2,1)S(1)}, u32[]{:S(2)}, u32[]{:S(2)}) collective-permute-start(bf16[256,2048]{1,0:T(8,128)(2,1)S(1)} %copy-done.41), channel_id=1, source_target_pairs={{0,1},{1,0},{2,3},{3,2},{4,5},{5,4},{6,7},{7,6},{8,9},{9,8},{10,11... | collective-permute-start | bytes 3145736 | tf_op jit(solution)/shard_map/ppermute | solution.py:54
  56.8 22.6 %collective-permute-start.5 = (bf16[256,2048]{1,0:T(8,128)(2,1)S(1)}, bf16[256,2048]{1,0:T(8,128)(2,1)S(1)}, u32[]{:S(2)}, u32[]{:S(2)}) collective-permute-start(bf16[256,2048]{1,0:T(8,128)(2,1)S(1)} %copy-done.41), channel_id=1, source_target_pairs={{0,2},{1,3},{2,0},{3,1},{4,6},{5,7},{6,4},{7,5},{8,10},{9,11},{10,... | collective-permute-start | bytes 3145736 | tf_op jit(solution)/shard_map/ppermute | solution.py:54
  136.0 22.6 %collective-permute-start.8 = (bf16[256,2048]{1,0:T(8,128)(2,1)}, bf16[256,2048]{1,0:T(8,128)(2,1)S(1)}, u32[]{:S(2)}, u32[]{:S(2)}) collective-permute-start(bf16[256,2048]{1,0:T(8,128)(2,1)} %get-tuple-element.340), channel_id=1, source_target_pairs={{0,1},{1,0},{2,3},{3,2},{4,5},{5,4},{6,7},{7,6},{8,9},{9,8},{10,11... | collective-permute-start | bytes 3145736 | tf_op jit(solution)/shard_map/ppermute | solution.py:54
  137.0 22.5 %collective-permute-start.9 = (bf16[256,2048]{1,0:T(8,128)(2,1)}, bf16[256,2048]{1,0:T(8,128)(2,1)}, u32[]{:S(2)}, u32[]{:S(2)}) collective-permute-start(bf16[256,2048]{1,0:T(8,128)(2,1)} %get-tuple-element.339), channel_id=1, source_target_pairs={{0,2},{1,3},{2,0},{3,1},{4,6},{5,7},{6,4},{7,5},{8,10},{9,11},{10,... | collective-permute-start | bytes 3145736 | tf_op jit(solution)/shard_map/ppermute | solution.py:54
  197.1 33.2 %collective-permute-start.14 = (bf16[384,2048]{1,0:T(8,128)(2,1)}, bf16[384,2048]{1,0:T(8,128)(2,1)S(1)}, u32[]{:S(2)}, u32[]{:S(2)}) collective-permute-start(bf16[384,2048]{1,0:T(8,128)(2,1)} %get-tuple-element.149), channel_id=1, source_target_pairs={{0,1},{1,0},{2,3},{3,2},{4,5},{5,4},{6,7},{7,6},{8,9},{9,8},{10,11... | collective-permute-start | bytes 4718600 | tf_op jit(solution)/shard_map/ppermute | solution.py:54
  198.5 34.4 %collective-permute-start.15 = (bf16[384,2048]{1,0:T(8,128)(2,1)}, bf16[384,2048]{1,0:T(8,128)(2,1)S(1)}, u32[]{:S(2)}, u32[]{:S(2)}) collective-permute-start(bf16[384,2048]{1,0:T(8,128)(2,1)} %get-tuple-element.150), channel_id=1, source_target_pairs={{0,2},{1,3},{2,0},{3,1},{4,6},{5,7},{6,4},{7,5},{8,10},{9,11},{10,... | collective-permute-start | bytes 4718600 | tf_op jit(solution)/shard_map/ppermute | solution.py:54
  247.6 23.1 %collective-permute-start.18 = (bf16[256,2048]{1,0:T(8,128)(2,1)}, bf16[256,2048]{1,0:T(8,128)(2,1)}, u32[]{:S(2)}, u32[]{:S(2)}) collective-permute-start(bf16[256,2048]{1,0:T(8,128)(2,1)} %get-tuple-element.154), channel_id=1, source_target_pairs={{0,1},{1,0},{2,3},{3,2},{4,5},{5,4},{6,7},{7,6},{8,9},{9,8},{10,11... | collective-permute-start | bytes 3145736 | tf_op jit(solution)/shard_map/ppermute | solution.py:54
  249.6 21.1 %collective-permute-start.19 = (bf16[256,2048]{1,0:T(8,128)(2,1)}, bf16[256,2048]{1,0:T(8,128)(2,1)S(1)}, u32[]{:S(2)}, u32[]{:S(2)}) collective-permute-start(bf16[256,2048]{1,0:T(8,128)(2,1)} %get-tuple-element.154), channel_id=1, source_target_pairs={{0,2},{1,3},{2,0},{3,1},{4,6},{5,7},{6,4},{7,5},{8,10},{9,11},{10,... | collective-permute-start | bytes 3145736 | tf_op jit(solution)/shard_map/ppermute | solution.py:54
  289.5 23.0 %collective-permute-start.22 = (bf16[256,2048]{1,0:T(8,128)(2,1)S(1)}, bf16[256,2048]{1,0:T(8,128)(2,1)S(1)}, u32[]{:S(2)}, u32[]{:S(2)}) collective-permute-start(bf16[256,2048]{1,0:T(8,128)(2,1)S(1)} %get-tuple-element.328), channel_id=1, source_target_pairs={{0,1},{1,0},{2,3},{3,2},{4,5},{5,4},{6,7},{7,6},{8,9},{9,8},{10,11... | collective-permute-start | bytes 3145736 | tf_op jit(solution)/shard_map/ppermute | solution.py:54
  291.1 21.8 %collective-permute-start.23 = (bf16[256,2048]{1,0:T(8,128)(2,1)S(1)}, bf16[256,2048]{1,0:T(8,128)(2,1)S(1)}, u32[]{:S(2)}, u32[]{:S(2)}) collective-permute-start(bf16[256,2048]{1,0:T(8,128)(2,1)S(1)} %get-tuple-element.327), channel_id=1, source_target_pairs={{0,2},{1,3},{2,0},{3,1},{4,6},{5,7},{6,4},{7,5},{8,10},{9,11},{10,... | collective-permute-start | bytes 3145736 | tf_op jit(solution)/shard_map/ppermute | solution.py:54
  329.3 21.1 %collective-permute-start.26 = (bf16[256,2048]{1,0:T(8,128)(2,1)S(1)}, bf16[256,2048]{1,0:T(8,128)(2,1)S(1)}, u32[]{:S(2)}, u32[]{:S(2)}) collective-permute-start(bf16[256,2048]{1,0:T(8,128)(2,1)S(1)} %get-tuple-element.322), channel_id=1, source_target_pairs={{0,1},{1,0},{2,3},{3,2},{4,5},{5,4},{6,7},{7,6},{8,9},{9,8},{10,11... | collective-permute-start | bytes 3145736 | tf_op jit(solution)/shard_map/ppermute | solution.py:54
  330.9 22.4 %collective-permute-start.27 = (bf16[256,2048]{1,0:T(8,128)(2,1)S(1)}, bf16[256,2048]{1,0:T(8,128)(2,1)S(1)}, u32[]{:S(2)}, u32[]{:S(2)}) collective-permute-start(bf16[256,2048]{1,0:T(8,128)(2,1)S(1)} %get-tuple-element.321), channel_id=1, source_target_pairs={{0,2},{1,3},{2,0},{3,1},{4,6},{5,7},{6,4},{7,5},{8,10},{9,11},{10,... | collective-permute-start | bytes 3145736 | tf_op jit(solution)/shard_map/ppermute | solution.py:54
  354.1 31.1 %collective-permute-start.28 = (bf16[384,2048]{1,0:T(8,128)(2,1)S(1)}, bf16[384,2048]{1,0:T(8,128)(2,1)S(1)}, u32[]{:S(2)}, u32[]{:S(2)}) collective-permute-start(bf16[384,2048]{1,0:T(8,128)(2,1)S(1)} %get-tuple-element.170), channel_id=1, source_target_pairs={{0,2},{1,3},{2,0},{3,1},{4,6},{5,7},{6,4},{7,5},{8,10},{9,11},{10,... | collective-permute-start | bytes 4718600 | tf_op jit(solution)/shard_map/ppermute | solution.py:54
  354.5 30.7 %collective-permute-start.29 = (bf16[384,2048]{1,0:T(8,128)(2,1)S(1)}, bf16[384,2048]{1,0:T(8,128)(2,1)S(1)}, u32[]{:S(2)}, u32[]{:S(2)}) collective-permute-start(bf16[384,2048]{1,0:T(8,128)(2,1)S(1)} %get-tuple-element.171), channel_id=1, source_target_pairs={{0,1},{1,0},{2,3},{3,2},{4,5},{5,4},{6,7},{7,6},{8,9},{9,8},{10,11... | collective-permute-start | bytes 4718600 | tf_op jit(solution)/shard_map/ppermute | solution.py:54
  403.3 22.6 %collective-permute-start.32 = (bf16[256,2048]{1,0:T(8,128)(2,1)S(1)}, bf16[256,2048]{1,0:T(8,128)(2,1)S(1)}, u32[]{:S(2)}, u32[]{:S(2)}) collective-permute-start(bf16[256,2048]{1,0:T(8,128)(2,1)S(1)} %get-tuple-element.175), channel_id=1, source_target_pairs={{0,1},{1,0},{2,3},{3,2},{4,5},{5,4},{6,7},{7,6},{8,9},{9,8},{10,11... | collective-permute-start | bytes 3145736 | tf_op jit(solution)/shard_map/ppermute | solution.py:54
  403.9 22.1 %collective-permute-start.33 = (bf16[256,2048]{1,0:T(8,128)(2,1)S(1)}, bf16[256,2048]{1,0:T(8,128)(2,1)S(1)}, u32[]{:S(2)}, u32[]{:S(2)}) collective-permute-start(bf16[256,2048]{1,0:T(8,128)(2,1)S(1)} %get-tuple-element.175), channel_id=1, source_target_pairs={{0,2},{1,3},{2,0},{3,1},{4,6},{5,7},{6,4},{7,5},{8,10},{9,11},{10,... | collective-permute-start | bytes 3145736 | tf_op jit(solution)/shard_map/ppermute | solution.py:54
  442.4 21.0 %collective-permute-start.36 = (bf16[256,2048]{1,0:T(8,128)(2,1)S(1)}, bf16[256,2048]{1,0:T(8,128)(2,1)S(1)}, u32[]{:S(2)}, u32[]{:S(2)}) collective-permute-start(bf16[256,2048]{1,0:T(8,128)(2,1)S(1)} %get-tuple-element.316), channel_id=1, source_target_pairs={{0,1},{1,0},{2,3},{3,2},{4,5},{5,4},{6,7},{7,6},{8,9},{9,8},{10,11... | collective-permute-start | bytes 3145736 | tf_op jit(solution)/shard_map/ppermute | solution.py:54
  484.0 283.7 %reduce-scatter.7.cloned.1.call-start = ((), (), s32[]{:S(2)}) async-start(), calls=%async_computation.9 | async-start | bytes 9437184 | tf_op jit(solution)/shard_map/reduce_scatter | solution.py:388
  571.6 213.0 %reduce-scatter.11.cloned.1.call-start = ((), (), s32[]{:S(2)}) async-start(), calls=%async_computation.11 | async-start | bytes 2359296 | tf_op jit(solution)/shard_map/reduce_scatter | solution.py:388
  583.0 31.9 %collective-permute-start.48 = (bf16[256,2048]{1,0:T(8,128)(2,1)S(1)}, bf16[256,2048]{1,0:T(8,128)(2,1)S(1)}, u32[]{:S(2)}, u32[]{:S(2)}) collective-permute-start(bf16[256,2048]{1,0:T(8,128)(2,1)S(1)} %get-tuple-element.201), channel_id=1, source_target_pairs={{0,1},{1,0},{2,3},{3,2},{4,5},{5,4},{6,7},{7,6},{8,9},{9,8},{10,11... | collective-permute-start | bytes 3145736 | tf_op jit(solution)/shard_map/ppermute | solution.py:54
  583.7 31.2 %collective-permute-start.49 = (bf16[256,2048]{1,0:T(8,128)(2,1)S(1)}, bf16[256,2048]{1,0:T(8,128)(2,1)S(1)}, u32[]{:S(2)}, u32[]{:S(2)}) collective-permute-start(bf16[256,2048]{1,0:T(8,128)(2,1)S(1)} %get-tuple-element.201), channel_id=1, source_target_pairs={{0,2},{1,3},{2,0},{3,1},{4,6},{5,7},{6,4},{7,5},{8,10},{9,11},{10,... | collective-permute-start | bytes 3145736 | tf_op jit(solution)/shard_map/ppermute | solution.py:54
  673.3 140.7 %reduce-scatter.9.cloned.1.call-start = ((), (), s32[]{:S(2)}) async-start(), calls=%async_computation.10 | async-start | bytes 7077888 | tf_op jit(solution)/shard_map/reduce_scatter | solution.py:388
  689.2 21.2 %collective-permute-start.52 = (bf16[256,2048]{1,0:T(8,128)(2,1)S(1)}, bf16[256,2048]{1,0:T(8,128)(2,1)S(1)}, u32[]{:S(2)}, u32[]{:S(2)}) collective-permute-start(bf16[256,2048]{1,0:T(8,128)(2,1)S(1)} %get-tuple-element.304), channel_id=1, source_target_pairs={{0,1},{1,0},{2,3},{3,2},{4,5},{5,4},{6,7},{7,6},{8,9},{9,8},{10,11... | collective-permute-start | bytes 3145736 | tf_op jit(solution)/shard_map/ppermute | solution.py:54
  724.2 20.7 %collective-permute-start.56 = (bf16[256,2048]{1,0:T(8,128)(2,1)}, bf16[256,2048]{1,0:T(8,128)(2,1)}, u32[]{:S(2)}, u32[]{:S(2)}) collective-permute-start(bf16[256,2048]{1,0:T(8,128)(2,1)} %get-tuple-element.300), channel_id=1, source_target_pairs={{0,1},{1,0},{2,3},{3,2},{4,5},{5,4},{6,7},{7,6},{8,9},{9,8},{10,11... | collective-permute-start | bytes 3145736 | tf_op jit(solution)/shard_map/ppermute | solution.py:54
  725.6 20.7 %collective-permute-start.57 = (bf16[256,2048]{1,0:T(8,128)(2,1)}, bf16[256,2048]{1,0:T(8,128)(2,1)}, u32[]{:S(2)}, u32[]{:S(2)}) collective-permute-start(bf16[256,2048]{1,0:T(8,128)(2,1)} %get-tuple-element.299), channel_id=1, source_target_pairs={{0,2},{1,3},{2,0},{3,1},{4,6},{5,7},{6,4},{7,5},{8,10},{9,11},{10,... | collective-permute-start | bytes 3145736 | tf_op jit(solution)/shard_map/ppermute | solution.py:54
  (141 other events, 1926.1 us)
Sparse Core Ops, SparseCore 0:
  10.2 67.4 all-gather.4
  79.3 27.7 all-gather.6
  108.7 81.4 all-gather.8
  191.6 80.5 all-gather.10
  484.1 90.0 reduce-scatter.4
  576.4 88.0 reduce-scatter.6
  673.4 33.9 reduce-scatter.10
  746.5 67.4 reduce-scatter.8

commit v5 on v4

--- a/solution.py
+++ b/solution.py
@@ -559,7 +559,9 @@
     )
     attn_far[1] = gather_far(attn_near[1])
     out_term = tn(after(grad_attn[0], grad_query[0], *attn_near[1]), context[0])
-    grad_attn[1] = gathered(grad_out1[1], attn_near[1], attn_far[1])
+    grad_attn[1] = gathered(
+        grad_out1[1], attn_near[1], together(attn_far[1], out_term) if attn_far[1] else []
+    )
     out_grad = low(out_term + tn(grad_attn[1], context[1]))
     out_part = scatter_weight(out_grad)
     grad_context = low(nn(after(grad_attn[1], out_grad), out_full))
@@ -576,13 +578,13 @@
     proj_terms = [None] * CHUNKS
     tokens_low[0] = low(nt(after(grad_proj[0], down_part), proj_full))
     near[0] = scatter_near(tokens_low[0])
-    proj_terms[0] = tn(after(seq_tokens[0], tokens_low[0]), grad_proj[0])
+    proj_terms[1] = tn(after(seq_tokens[1], tokens_low[0]), grad_proj[1])
+    proj_terms[0] = tn(after(seq_tokens[0], proj_terms[1], *near[0][1]), grad_proj[0])
     far[0] = scatter_far(near[0])
-    tokens_low[1] = low(nt(after(grad_proj[1], proj_terms[0], *near[0][1]), proj_full))
+    proj_grad = low(proj_terms[1] + proj_terms[0])
+    proj_part = scatter_weight(proj_grad)
+    tokens_low[1] = low(nt(after(grad_proj[1], proj_grad), proj_full))
     near[1] = scatter_near(tokens_low[1], *far[0])
-    proj_terms[1] = tn(after(seq_tokens[1], tokens_low[1], *far[0]), grad_proj[1])
-    proj_grad = low(add_up(proj_terms))
-    proj_part = scatter_weight(after(proj_grad, *near[1][1]))
     far[1] = scatter_far(near[1])
     early = together((*(far[1] or near[1][1]), up_part))
     if far[1]:
@@ -592,7 +594,9 @@
     for c in every:
         tokens_grad[c] = low(grad_sum1[c] + scattered(near[c], far[c]))
     proj_part, out_part, up_part, down_part = map(wide, (proj_part, out_part, up_part, down_part))
-    proj_bias = add_up([jnp.sum(wide(grad_proj[c]), axis=0) for c in every])
+    proj_bias = add_up(
+        [jnp.sum(wide(after(grad_proj[c], tokens_low[1])), axis=0) for c in every]
+    )
     (
         norm2_gain_grad,
         norm2_shift_grad,

time: 835 us -> 809 us (0.969)
  waiting for transfers between devices: 246 us -> 216 us
    reduce_scatter x4, waiting for transfers between devices: 24.9 us -> 0.01 us  [scatter_weight(): return lax.psum_scatter(grad, 'dp', scatter_dimension=0, tiled=True)]
    unnamed x233 -> x237, local copies, waits for them, and re-layouts: 40.1 us -> 40.3 us
  transfers between devices with their start and end apart: 78 -> 78, of which waited for: 45 -> 37; matrix products, arithmetic and copies ran while one was open for 46% -> 47% of each run, Pallas kernels for 11% -> 12%
where the time goes in v5:
time: 809 us; the launch traced here: 797 us
  matrix products  266 us (33%)
  waiting for transfers between devices  216 us (27%)
  Pallas kernels  92.6 us (11%)
  starting transfers between devices  69.2 us (9%)
  local copies, waits for them, and re-layouts  69 us (9%)
  other arithmetic  67.4 us (8%)
  between operations  17.1 us (2%)
    ppermute x63, waiting for transfers between devices, swap(): return lax.ppermute(value, 'tensor', [(i, i ^ bits) for i in range(size)])  214 us
    dot_general x8, matrix products, nn(): lax.dot_general(left, right, (((1,), (0,)), ((), ())), preferred_element_...  102 us
    dot_general x8, matrix products, tn(): lax.dot_general(left, right, (((0,), (0,)), ((), ())), preferred_element_...  91.4 us
    dot_general x8, matrix products, nt(): lax.dot_general(left, right, (((1,), (1,)), ((), ())), preferred_element_...  72.5 us
    ppermute x63, starting transfers between devices, swap(): return lax.ppermute(value, 'tensor', [(i, i ^ bits) for i in range(size)])  63.1 us
    pallas_call x2, Pallas kernels, attend_back(): pl.pallas_call(kernel, out_shape=(jax.ShapeDtypeStruct((part, cols), jnp....  54 us
    unnamed x237, local copies, waits for them, and re-layouts  40.3 us
    pallas_call x2, Pallas kernels, attend(): pl.pallas_call(kernel, out_shape=(jax.ShapeDtypeStruct((part, cols), jnp....  38.6 us
  transfers between devices with their start and end apart: 78, of which 37 were waited for; matrix products, arithmetic and copies ran while one was open for 47% of the time, Pallas kernels for 12%

profile of v5, /device:TPU:0, one launch (start us, length us, event | category | flops | bytes accessed | tf_op | source)
XLA Modules:
  0.0 797.4 jit_solution(15798557795130884581)
XLA Ops:
  20.7 19.0 %collective-permute-done = bf16[256,2048]{1,0:T(8,128)(2,1)} collective-permute-done((bf16[256,2048]{1,0:T(8,128)(2,1)}, bf16[256,2048]{1,0:T(8,128)(2,1)}, u32[]{:S(2)}, u32[]{:S(2)}) %collective-permute-start) | collective-permute-done | bytes 1048608 | tf_op jit(solution)/shard_map/ppermute | solution.py:54
  47.1 7.7 collective-permute-done.2
  61.7 17.3 %collective-permute-done.4 = bf16[256,2048]{1,0:T(8,128)(2,1)S(1)} collective-permute-done((bf16[256,2048]{1,0:T(8,128)(2,1)S(1)}, bf16[256,2048]{1,0:T(8,128)(2,1)S(1)}, u32[]{:S(2)}, u32[]{:S(2)}) %collective-permute-start.4) | collective-permute-done | bytes 1048608 | tf_op jit(solution)/shard_map/ppermute | solution.py:54
  84.7 11.6 %add_convert_fusion.6.q_ref.rest_0_.rest_2_ = bf16[1024,1536]{1,0:T(8,128)(2,1)} fusion(bf16[1024,2048]{1,0:T(8,128)(2,1)} %slice_dynamic-update-slice_fusion.28, bf16[2048,1536]{1,0:T(8,128)(2,1)} %all-gather.5.cloned.1.call-done, f32[1536]{0:T(1024)S(1)} %pad_maximum_fusion.9), kind=kOutput, calls=%fused_computation.22 | convolution fusion | flops 6445596672 | bytes 13637632 | tf_op jit(solution)/shard_map/dot_general | solution.py:26
  101.8 9.6 %add_convert_fusion.5.rest_1_.rest_3_.q_ref = bf16[1024,1536]{1,0:T(8,128)(2,1)} fusion(bf16[1024,2048]{1,0:T(8,128)(2,1)} %slice_dynamic-update-slice_fusion.24, bf16[2048,1536]{1,0:T(8,128)(2,1)S(1)} %copy-done.83, f32[1536]{0:T(1024)S(1)} %pad_maximum_fusion.9), kind=kOutput, calls=%fused_computation.21 | convolution fusion | flops 6445596672 | bytes 13637632 | tf_op jit(solution)/shard_map/dot_general | solution.py:26
  111.4 19.1 %attend.2 = (bf16[1024,512]{1,0:T(8,128)(2,1)}, f32[4,1,1024]{2,1,0:T(1,128)}) custom-call(s32[16]{0:T(128)} %stack.67.lim, bf16[1024,1536]{1,0:T(8,128)(2,1)} %add_convert_fusion.6.q_ref.rest_0_.rest_2_, bf16[1024,1536]{1,0:T(8,128)(2,1)} %add_convert_fusion.6.q_ref.rest_0_.rest_2_, bf16[1024,1536]{1,0:T(8,128)(2,1)} %add_convert_fusion.5.rest_1_.rest_3_.q_ref, ...), custom_call_target="tpu_custom_call" | custom-call | flops 8589934592 | bytes 6291456 | tf_op jit(solution)/shard_map/attend/pallas_call | solution.py:193
  138.7 19.4 %attend.3 = (bf16[1024,512]{1,0:T(8,128)(2,1)}, f32[4,1,1024]{2,1,0:T(1,128)}) custom-call(s32[16]{0:T(128)} %stack.67.lim, bf16[1024,1536]{1,0:T(8,128)(2,1)} %add_convert_fusion.5.rest_1_.rest_3_.q_ref, bf16[1024,1536]{1,0:T(8,128)(2,1)} %add_convert_fusion.6.q_ref.rest_0_.rest_2_, bf16[1024,1536]{1,0:T(8,128)(2,1)} %add_convert_fusion.5.rest_1_.rest_3_.q_ref, ...), custom_call_target="tpu_custom_call" | custom-call | flops 8589934592 | bytes 6291456 | tf_op jit(solution)/shard_map/attend/pallas_call | solution.py:193
  181.9 14.8 %collective-permute-done.12 = bf16[256,2048]{1,0:T(8,128)(2,1)S(1)} collective-permute-done((bf16[256,2048]{1,0:T(8,128)(2,1)S(1)}, bf16[256,2048]{1,0:T(8,128)(2,1)S(1)}, u32[]{:S(2)}, u32[]{:S(2)}) %collective-permute-start.12) | collective-permute-done | bytes 1048608 | tf_op jit(solution)/shard_map/ppermute | solution.py:54
  201.9 30.7 %collective-permute-done.14 = bf16[384,2048]{1,0:T(8,128)(2,1)S(1)} collective-permute-done((bf16[384,2048]{1,0:T(8,128)(2,1)}, bf16[384,2048]{1,0:T(8,128)(2,1)S(1)}, u32[]{:S(2)}, u32[]{:S(2)}) %collective-permute-start.14) | collective-permute-done | bytes 1572896 | tf_op jit(solution)/shard_map/ppermute | solution.py:54
  254.7 17.2 %multiply_convert_fusion.3 = (bf16[1024,2048]{1,0:T(8,128)(2,1)}, f32[1024,2048]{1,0:T(8,128)}) fusion(f32[2048]{0:T(1024)S(1)} %dynamic_slice.49, bf16[1024,2048]{1,0:T(8,128)(2,1)} %slice_dynamic-update-slice_fusion.20, bf16[2048,2048]{1,0:T(8,128)(2,1)} %all-gather.9.cloned.1.call-done), kind=kOutput, calls=%fused_computation.17 | convolution fusion | flops 8610906112 | bytes 25174016 | tf_op jit(solution)/shard_map/dot_general | solution.py:26
  275.9 12.7 %convolution_convert_fusion.5 = bf16[1024,2048]{1,0:T(8,128)(2,1)S(1)} fusion(bf16[1024,2048]{1,0:T(8,128)(2,1)} %get-tuple-element.158, bf16[2048,2048]{1,0:T(8,128)(2,1)} %all-gather.11.cloned.1.call-done), kind=kOutput, calls=%fused_computation.29 | convolution fusion | flops 8592031744 | bytes 16777216 | tf_op jit(solution)/shard_map/dot_general | solution.py:20
  296.3 17.3 %multiply_convert_fusion.2 = (bf16[1024,2048]{1,0:T(8,128)(2,1)}, f32[1024,2048]{1,0:T(8,128)}) fusion(f32[2048]{0:T(1024)S(1)} %dynamic_slice.49, bf16[1024,2048]{1,0:T(8,128)(2,1)S(1)} %slice_dynamic-update-slice_fusion.16, bf16[2048,2048]{1,0:T(8,128)(2,1)} %all-gather.9.cloned.1.call-done), kind=kOutput, calls=%fused_computation.15 | convolution fusion | flops 8610906112 | bytes 25174016 | tf_op jit(solution)/shard_map/dot_general | solution.py:26
  316.3 10.9 %convolution_convert_fusion.4 = bf16[1024,2048]{1,0:T(8,128)(2,1)S(1)} fusion(bf16[1024,2048]{1,0:T(8,128)(2,1)} %get-tuple-element.167, bf16[2048,2048]{1,0:T(8,128)(2,1)S(1)} %bitcast.103), kind=kOutput, calls=%fused_computation.28 | convolution fusion | flops 8592031744 | bytes 16777216 | tf_op jit(solution)/shard_map/dot_general | solution.py:20
  337.7 12.0 %collective-permute-done.26 = bf16[256,2048]{1,0:T(8,128)(2,1)S(1)} collective-permute-done((bf16[256,2048]{1,0:T(8,128)(2,1)S(1)}, bf16[256,2048]{1,0:T(8,128)(2,1)S(1)}, u32[]{:S(2)}, u32[]{:S(2)}) %collective-permute-start.26) | collective-permute-done | bytes 1048608 | tf_op jit(solution)/shard_map/ppermute | solution.py:54
  355.8 29.3 %collective-permute-done.28 = bf16[384,2048]{1,0:T(8,128)(2,1)S(1)} collective-permute-done((bf16[384,2048]{1,0:T(8,128)(2,1)S(1)}, bf16[384,2048]{1,0:T(8,128)(2,1)S(1)}, u32[]{:S(2)}, u32[]{:S(2)}) %collective-permute-start.28) | collective-permute-done | bytes 1572896 | tf_op jit(solution)/shard_map/ppermute | solution.py:54
  393.6 8.1 %collective-permute-done.30 = bf16[128,2048]{1,0:T(8,128)(2,1)S(1)} collective-permute-done((bf16[128,2048]{1,0:T(8,128)(2,1)S(1)}, bf16[128,2048]{1,0:T(8,128)(2,1)S(1)}, u32[]{:S(2)}, u32[]{:S(2)}) %collective-permute-start.30) | collective-permute-done | bytes 524320 | tf_op jit(solution)/shard_map/ppermute | solution.py:54
  406.3 19.4 %convert_reduce_fusion.1 = (f32[2048]{0:T(1024)}, bf16[1024,2048]{1,0:T(8,128)(2,1)}) fusion(f32[1024,2048]{1,0:T(8,128)} %get-tuple-element.375, f32[2048]{0:T(1024)S(1)} %dynamic_slice.49, bf16[1024,2048]{1,0:T(8,128)(2,1)S(1)} %slice_dynamic-update-slice_fusion.12, bf16[2048,2048]{1,0:T(8,128)(2,1)} %all-gather.11.cloned.1.call-done), kind=kOutput, calls=%fused_computation.10 | convolution fusion | flops 8638167040 | bytes 25182208 | tf_op jit(solution)/shard_map/dot_general | solution.py:26
  428.5 10.7 %convolution_convert_fusion.3 = bf16[1024,2048]{1,0:T(8,128)(2,1)S(1)} fusion(bf16[1024,2048]{1,0:T(8,128)(2,1)} %get-tuple-element.179, bf16[2048,2048]{1,0:T(8,128)(2,1)S(1)} %bitcast.99), kind=kOutput, calls=%fused_computation.27 | convolution fusion | flops 8592031744 | bytes 16777216 | tf_op jit(solution)/shard_map/dot_general | solution.py:20
  445.0 11.6 %fusion.50 = f32[2048,2048]{1,0:T(8,128)} fusion(bf16[1024,2048]{1,0:T(8,128)(2,1)S(1)} %slice_dynamic-update-slice_fusion.4, bf16[1024,2048]{1,0:T(8,128)(2,1)S(1)} %copy-done.87), kind=kOutput, calls=%fused_computation.245 | convolution fusion | flops 8589934592 | bytes 25165824 | tf_op jit(solution)/shard_map/dot_general | solution.py:32
  468.1 16.2 %add_convert_fusion.1 = bf16[2048,2048]{1,0:T(8,128)(2,1)} fusion(f32[2048,2048]{1,0:T(8,128)} %fusion.50, bf16[1024,2048]{1,0:T(8,128)(2,1)S(1)} %slice_dynamic-update-slice_fusion.12, bf16[1024,2048]{1,0:T(8,128)(2,1)} %get-tuple-element.158), kind=kOutput, calls=%fused_computation.1 | convolution fusion | flops 8598323200 | bytes 33554432 | tf_op jit(solution)/shard_map/dot_general | solution.py:32
  495.1 17.2 %convert_reduce_fusion = (f32[2048]{0:T(1024)}, bf16[1024,2048]{1,0:T(8,128)(2,1)}) fusion(f32[1024,2048]{1,0:T(8,128)} %get-tuple-element.377, f32[2048]{0:T(1024)S(1)} %dynamic_slice.49, bf16[1024,2048]{1,0:T(8,128)(2,1)S(1)} %copy-done.60, bf16[2048,2048]{1,0:T(8,128)(2,1)S(1)} %bitcast.105), kind=kOutput, calls=%fused_computation.9 | convolution fusion | flops 8638167040 | bytes 25182208 | tf_op jit(solution)/shard_map/dot_general | solution.py:26
  516.7 10.7 %convolution_convert_fusion.2 = bf16[1024,2048]{1,0:T(8,128)(2,1)S(1)} fusion(bf16[1024,2048]{1,0:T(8,128)(2,1)} %get-tuple-element.193, bf16[2048,2048]{1,0:T(8,128)(2,1)S(1)} %bitcast.101), kind=kOutput, calls=%fused_computation.26 | convolution fusion | flops 8592031744 | bytes 16777216 | tf_op jit(solution)/shard_map/dot_general | solution.py:20
  533.1 14.5 %fusion.51 = f32[2048,2048]{1,0:T(8,128)} fusion(bf16[1024,2048]{1,0:T(8,128)(2,1)} %slice_dynamic-update-slice_fusion.20, bf16[1024,2048]{1,0:T(8,128)(2,1)S(1)} %copy-done.88), kind=kOutput, calls=%fused_computation.246 | convolution fusion | flops 8589934592 | bytes 25165824 | tf_op jit(solution)/shard_map/dot_general | solution.py:32
  555.1 16.2 %add_convert_fusion = bf16[2048,2048]{1,0:T(8,128)(2,1)} fusion(f32[2048,2048]{1,0:T(8,128)} %fusion.51, bf16[1024,2048]{1,0:T(8,128)(2,1)S(1)} %copy-done.58, bf16[1024,2048]{1,0:T(8,128)(2,1)} %get-tuple-element.193), kind=kOutput, calls=%fused_computation | convolution fusion | flops 8598323200 | bytes 33554432 | tf_op jit(solution)/shard_map/dot_general | solution.py:32
  588.6 27.0 %attend_back.2 = (bf16[1024,512]{1,0:T(8,128)(2,1)}, f32[2048,512]{1,0:T(8,128)}, f32[2048,512]{1,0:T(8,128)}) custom-call(s32[16]{0:T(128)} %stack.67.lim, bf16[1024,1536]{1,0:T(8,128)(2,1)} %add_convert_fusion.6.q_ref.rest_0_.rest_2_, bf16[1024,512]{1,0:T(8,128)(2,1)} %get-tuple-element.138.o_ref, bf16[1024,512]{1,0:T(8,128)(2,1)} %convolution_convert_fusion.9.do_ref, ...), custom_call_target="tpu_custom_call" | custom-call | flops 21474836480 | bytes 20971520 | tf_op jit(solution)/shard_map/attend_back/pallas_call | solution.py:285
  637.6 27.0 %attend_back.3 = (bf16[1024,512]{1,0:T(8,128)(2,1)}, bf16[2048,512]{1,0:T(8,128)(2,1)}, bf16[2048,512]{1,0:T(8,128)(2,1)}) custom-call(s32[16]{0:T(128)} %stack.67.lim, bf16[1024,1536]{1,0:T(8,128)(2,1)} %add_convert_fusion.5.rest_1_.rest_3_.q_ref, bf16[1024,512]{1,0:T(8,128)(2,1)} %get-tuple-element.146.o_ref, ...), custom_call_target="tpu_custom_call" | custom-call | flops 21474836480 | bytes 20971520 | tf_op jit(solution)/shard_map/attend_back/pallas_call | solution.py:285
  672.4 9.9 %convolution_convert_fusion.1 = bf16[1024,2048]{1,0:T(8,128)(2,1)S(1)} fusion(bf16[1024,1536]{1,0:T(8,128)(2,1)} %pad_maximum_fusion, bf16[2048,1536]{1,0:T(8,128)(2,1)} %all-gather.5.cloned.1.call-done), kind=kOutput, calls=%fused_computation.25 | convolution fusion | flops 6444548096 | bytes 13631488 | tf_op jit(solution)/shard_map/dot_general | solution.py:20
  687.1 12.0 %fusion.21 = f32[2048,1536]{1,0:T(8,128)} fusion(bf16[1024,2048]{1,0:T(8,128)(2,1)} %slice_dynamic-update-slice_fusion.24, bf16[1024,512]{1,0:T(8,128)(2,1)S(1)} %get-tuple-element.348, bf16[1024,512]{1,0:T(8,128)(2,1)S(1)} %copy-done.26, bf16[1024,512]{1,0:T(8,128)(2,1)S(1)} %copy-done.43), kind=kOutput, calls=%fused_computation.222 | convolution fusion | flops 6451888128 | bytes 19922944 | tf_op jit(solution)/shard_map/dot_general | solution.py:32
  700.7 12.3 %add_convert_fusion.2 = bf16[2048,1536]{1,0:T(8,128)(2,1)} fusion(f32[2048,1536]{1,0:T(8,128)} %fusion.21, bf16[1024,2048]{1,0:T(8,128)(2,1)S(1)} %copy-done.54, bf16[1024,512]{1,0:T(8,128)(2,1)S(1)} %copy-done.27, bf16[1024,512]{1,0:T(8,128)(2,1)S(1)} %copy-done.28, bf16[1024,512]{1,0:T(8,128)(2,1)S(1)} %copy-done.45), kind=kOutput, calls=%fused_computation.2 | convolution fusion | flops 6458179584 | bytes 26214400 | tf_op jit(solution)/shard_map/dot_general | solution.py:32
  726.0 9.0 %convolution_convert_fusion = bf16[1024,2048]{1,0:T(8,128)(2,1)S(1)} fusion(bf16[1024,1536]{1,0:T(8,128)(2,1)S(1)} %pad_maximum_fusion.1, bf16[2048,1536]{1,0:T(8,128)(2,1)} %all-gather.5.cloned.1.call-done), kind=kOutput, calls=%fused_computation.24 | convolution fusion | flops 6444548096 | bytes 13631488 | tf_op jit(solution)/shard_map/dot_general | solution.py:20
  742.1 10.9 %collective-permute-done.56 = bf16[256,2048]{1,0:T(8,128)(2,1)S(1)} collective-permute-done((bf16[256,2048]{1,0:T(8,128)(2,1)}, bf16[256,2048]{1,0:T(8,128)(2,1)S(1)}, u32[]{:S(2)}, u32[]{:S(2)}) %collective-permute-start.56) | collective-permute-done | bytes 1048608 | tf_op jit(solution)/shard_map/ppermute | solution.py:54
  757.7 7.2 collective-permute-done.58
  (545 shorter events, 291.6 us)
Async XLA Ops:
  7.2 77.5 %all-gather.5.cloned.1.call-start = ((), (), s32[]{:S(2)}) async-start(), calls=%async_computation.4 | async-start | bytes 7077888 | tf_op jit(solution)/shard_map/all_gather | solution.py:384
  9.5 121.1 %all-gather.7.cloned.1.call-start = ((), (), s32[]{:S(2)}) async-start(), calls=%async_computation.5 | async-start | bytes 2359296 | tf_op jit(solution)/shard_map/all_gather | solution.py:384
  10.2 244.5 %all-gather.9.cloned.1.call-start = ((), (), s32[]{:S(2)}) async-start(), calls=%async_computation.6 | async-start | bytes 9437184 | tf_op jit(solution)/shard_map/all_gather | solution.py:384
  10.9 265.0 %all-gather.11.cloned.1.call-start = ((), (), s32[]{:S(2)}) async-start(), calls=%async_computation.7 | async-start | bytes 9437184 | tf_op jit(solution)/shard_map/all_gather | solution.py:384
  13.3 26.4 %collective-permute-start = (bf16[256,2048]{1,0:T(8,128)(2,1)}, bf16[256,2048]{1,0:T(8,128)(2,1)}, u32[]{:S(2)}, u32[]{:S(2)}) collective-permute-start(bf16[256,2048]{1,0:T(8,128)(2,1)} %get-tuple-element.352), channel_id=1, source_target_pairs={{0,1},{1,0},{2,3},{3,2},{4,5},{5,4},{6,7},{7,6},{8,9},{9,8},{10,11... | collective-permute-start | bytes 3145736 | tf_op jit(solution)/shard_map/ppermute | solution.py:54
  16.2 24.8 %collective-permute-start.1 = (bf16[256,2048]{1,0:T(8,128)(2,1)}, bf16[256,2048]{1,0:T(8,128)(2,1)S(1)}, u32[]{:S(2)}, u32[]{:S(2)}) collective-permute-start(bf16[256,2048]{1,0:T(8,128)(2,1)} %get-tuple-element.352), channel_id=1, source_target_pairs={{0,2},{1,3},{2,0},{3,1},{4,6},{5,7},{6,4},{7,5},{8,10},{9,11},{10,... | collective-permute-start | bytes 3145736 | tf_op jit(solution)/shard_map/ppermute | solution.py:54
  17.8 654.6 %reduce-scatter.5.cloned.1.call-start = ((), (), s32[]{:S(2)}) async-start(), calls=%async_computation.8 | async-start | bytes 9437184 | tf_op jit(solution)/shard_map/reduce_scatter | solution.py:388
  56.2 22.8 %collective-permute-start.4 = (bf16[256,2048]{1,0:T(8,128)(2,1)S(1)}, bf16[256,2048]{1,0:T(8,128)(2,1)S(1)}, u32[]{:S(2)}, u32[]{:S(2)}) collective-permute-start(bf16[256,2048]{1,0:T(8,128)(2,1)S(1)} %copy-done.44), channel_id=1, source_target_pairs={{0,1},{1,0},{2,3},{3,2},{4,5},{5,4},{6,7},{7,6},{8,9},{9,8},{10,11... | collective-permute-start | bytes 3145736 | tf_op jit(solution)/shard_map/ppermute | solution.py:54
  56.8 22.6 %collective-permute-start.5 = (bf16[256,2048]{1,0:T(8,128)(2,1)S(1)}, bf16[256,2048]{1,0:T(8,128)(2,1)S(1)}, u32[]{:S(2)}, u32[]{:S(2)}) collective-permute-start(bf16[256,2048]{1,0:T(8,128)(2,1)S(1)} %copy-done.44), channel_id=1, source_target_pairs={{0,2},{1,3},{2,0},{3,1},{4,6},{5,7},{6,4},{7,5},{8,10},{9,11},{10,... | collective-permute-start | bytes 3145736 | tf_op jit(solution)/shard_map/ppermute | solution.py:54
  136.4 21.8 %collective-permute-start.8 = (bf16[256,2048]{1,0:T(8,128)(2,1)}, bf16[256,2048]{1,0:T(8,128)(2,1)S(1)}, u32[]{:S(2)}, u32[]{:S(2)}) collective-permute-start(bf16[256,2048]{1,0:T(8,128)(2,1)} %get-tuple-element.342), channel_id=1, source_target_pairs={{0,1},{1,0},{2,3},{3,2},{4,5},{5,4},{6,7},{7,6},{8,9},{9,8},{10,11... | collective-permute-start | bytes 3145736 | tf_op jit(solution)/shard_map/ppermute | solution.py:54
  137.4 22.0 %collective-permute-start.9 = (bf16[256,2048]{1,0:T(8,128)(2,1)}, bf16[256,2048]{1,0:T(8,128)(2,1)}, u32[]{:S(2)}, u32[]{:S(2)}) collective-permute-start(bf16[256,2048]{1,0:T(8,128)(2,1)} %get-tuple-element.341), channel_id=1, source_target_pairs={{0,2},{1,3},{2,0},{3,1},{4,6},{5,7},{6,4},{7,5},{8,10},{9,11},{10,... | collective-permute-start | bytes 3145736 | tf_op jit(solution)/shard_map/ppermute | solution.py:54
  176.2 20.6 %collective-permute-start.12 = (bf16[256,2048]{1,0:T(8,128)(2,1)S(1)}, bf16[256,2048]{1,0:T(8,128)(2,1)S(1)}, u32[]{:S(2)}, u32[]{:S(2)}) collective-permute-start(bf16[256,2048]{1,0:T(8,128)(2,1)S(1)} %get-tuple-element.336), channel_id=1, source_target_pairs={{0,1},{1,0},{2,3},{3,2},{4,5},{5,4},{6,7},{7,6},{8,9},{9,8},{10,11... | collective-permute-start | bytes 3145736 | tf_op jit(solution)/shard_map/ppermute | solution.py:54
  199.2 33.4 %collective-permute-start.14 = (bf16[384,2048]{1,0:T(8,128)(2,1)}, bf16[384,2048]{1,0:T(8,128)(2,1)S(1)}, u32[]{:S(2)}, u32[]{:S(2)}) collective-permute-start(bf16[384,2048]{1,0:T(8,128)(2,1)} %get-tuple-element.152), channel_id=1, source_target_pairs={{0,1},{1,0},{2,3},{3,2},{4,5},{5,4},{6,7},{7,6},{8,9},{9,8},{10,11... | collective-permute-start | bytes 4718600 | tf_op jit(solution)/shard_map/ppermute | solution.py:54
  201.0 31.7 %collective-permute-start.15 = (bf16[384,2048]{1,0:T(8,128)(2,1)}, bf16[384,2048]{1,0:T(8,128)(2,1)S(1)}, u32[]{:S(2)}, u32[]{:S(2)}) collective-permute-start(bf16[384,2048]{1,0:T(8,128)(2,1)} %get-tuple-element.153), channel_id=1, source_target_pairs={{0,2},{1,3},{2,0},{3,1},{4,6},{5,7},{6,4},{7,5},{8,10},{9,11},{10,... | collective-permute-start | bytes 4718600 | tf_op jit(solution)/shard_map/ppermute | solution.py:54
  248.5 23.4 %collective-permute-start.18 = (bf16[256,2048]{1,0:T(8,128)(2,1)}, bf16[256,2048]{1,0:T(8,128)(2,1)}, u32[]{:S(2)}, u32[]{:S(2)}) collective-permute-start(bf16[256,2048]{1,0:T(8,128)(2,1)} %get-tuple-element.157), channel_id=1, source_target_pairs={{0,1},{1,0},{2,3},{3,2},{4,5},{5,4},{6,7},{7,6},{8,9},{9,8},{10,11... | collective-permute-start | bytes 3145736 | tf_op jit(solution)/shard_map/ppermute | solution.py:54
  249.3 22.6 %collective-permute-start.19 = (bf16[256,2048]{1,0:T(8,128)(2,1)}, bf16[256,2048]{1,0:T(8,128)(2,1)S(1)}, u32[]{:S(2)}, u32[]{:S(2)}) collective-permute-start(bf16[256,2048]{1,0:T(8,128)(2,1)} %get-tuple-element.157), channel_id=1, source_target_pairs={{0,2},{1,3},{2,0},{3,1},{4,6},{5,7},{6,4},{7,5},{8,10},{9,11},{10,... | collective-permute-start | bytes 3145736 | tf_op jit(solution)/shard_map/ppermute | solution.py:54
  290.0 23.6 %collective-permute-start.22 = (bf16[256,2048]{1,0:T(8,128)(2,1)S(1)}, bf16[256,2048]{1,0:T(8,128)(2,1)S(1)}, u32[]{:S(2)}, u32[]{:S(2)}) collective-permute-start(bf16[256,2048]{1,0:T(8,128)(2,1)S(1)} %get-tuple-element.330), channel_id=1, source_target_pairs={{0,1},{1,0},{2,3},{3,2},{4,5},{5,4},{6,7},{7,6},{8,9},{9,8},{10,11... | collective-permute-start | bytes 3145736 | tf_op jit(solution)/shard_map/ppermute | solution.py:54
  290.9 22.8 %collective-permute-start.23 = (bf16[256,2048]{1,0:T(8,128)(2,1)S(1)}, bf16[256,2048]{1,0:T(8,128)(2,1)S(1)}, u32[]{:S(2)}, u32[]{:S(2)}) collective-permute-start(bf16[256,2048]{1,0:T(8,128)(2,1)S(1)} %get-tuple-element.329), channel_id=1, source_target_pairs={{0,2},{1,3},{2,0},{3,1},{4,6},{5,7},{6,4},{7,5},{8,10},{9,11},{10,... | collective-permute-start | bytes 3145736 | tf_op jit(solution)/shard_map/ppermute | solution.py:54
  331.6 21.6 %collective-permute-start.27 = (bf16[256,2048]{1,0:T(8,128)(2,1)S(1)}, bf16[256,2048]{1,0:T(8,128)(2,1)S(1)}, u32[]{:S(2)}, u32[]{:S(2)}) collective-permute-start(bf16[256,2048]{1,0:T(8,128)(2,1)S(1)} %get-tuple-element.323), channel_id=1, source_target_pairs={{0,2},{1,3},{2,0},{3,1},{4,6},{5,7},{6,4},{7,5},{8,10},{9,11},{10,... | collective-permute-start | bytes 3145736 | tf_op jit(solution)/shard_map/ppermute | solution.py:54
  354.0 31.1 %collective-permute-start.28 = (bf16[384,2048]{1,0:T(8,128)(2,1)S(1)}, bf16[384,2048]{1,0:T(8,128)(2,1)S(1)}, u32[]{:S(2)}, u32[]{:S(2)}) collective-permute-start(bf16[384,2048]{1,0:T(8,128)(2,1)S(1)} %get-tuple-element.173), channel_id=1, source_target_pairs={{0,2},{1,3},{2,0},{3,1},{4,6},{5,7},{6,4},{7,5},{8,10},{9,11},{10,... | collective-permute-start | bytes 4718600 | tf_op jit(solution)/shard_map/ppermute | solution.py:54
  355.3 29.8 %collective-permute-start.29 = (bf16[384,2048]{1,0:T(8,128)(2,1)S(1)}, bf16[384,2048]{1,0:T(8,128)(2,1)S(1)}, u32[]{:S(2)}, u32[]{:S(2)}) collective-permute-start(bf16[384,2048]{1,0:T(8,128)(2,1)S(1)} %get-tuple-element.174), channel_id=1, source_target_pairs={{0,1},{1,0},{2,3},{3,2},{4,5},{5,4},{6,7},{7,6},{8,9},{9,8},{10,11... | collective-permute-start | bytes 4718600 | tf_op jit(solution)/shard_map/ppermute | solution.py:54
  404.6 22.6 %collective-permute-start.32 = (bf16[256,2048]{1,0:T(8,128)(2,1)S(1)}, bf16[256,2048]{1,0:T(8,128)(2,1)S(1)}, u32[]{:S(2)}, u32[]{:S(2)}) collective-permute-start(bf16[256,2048]{1,0:T(8,128)(2,1)S(1)} %get-tuple-element.178), channel_id=1, source_target_pairs={{0,1},{1,0},{2,3},{3,2},{4,5},{5,4},{6,7},{7,6},{8,9},{9,8},{10,11... | collective-permute-start | bytes 3145736 | tf_op jit(solution)/shard_map/ppermute | solution.py:54
  405.1 22.1 %collective-permute-start.33 = (bf16[256,2048]{1,0:T(8,128)(2,1)S(1)}, bf16[256,2048]{1,0:T(8,128)(2,1)S(1)}, u32[]{:S(2)}, u32[]{:S(2)}) collective-permute-start(bf16[256,2048]{1,0:T(8,128)(2,1)S(1)} %get-tuple-element.178), channel_id=1, source_target_pairs={{0,2},{1,3},{2,0},{3,1},{4,6},{5,7},{6,4},{7,5},{8,10},{9,11},{10,... | collective-permute-start | bytes 3145736 | tf_op jit(solution)/shard_map/ppermute | solution.py:54
  442.5 20.9 %collective-permute-start.36 = (bf16[256,2048]{1,0:T(8,128)(2,1)S(1)}, bf16[256,2048]{1,0:T(8,128)(2,1)S(1)}, u32[]{:S(2)}, u32[]{:S(2)}) collective-permute-start(bf16[256,2048]{1,0:T(8,128)(2,1)S(1)} %get-tuple-element.318), channel_id=1, source_target_pairs={{0,1},{1,0},{2,3},{3,2},{4,5},{5,4},{6,7},{7,6},{8,9},{9,8},{10,11... | collective-permute-start | bytes 3145736 | tf_op jit(solution)/shard_map/ppermute | solution.py:54
  443.6 20.4 %collective-permute-start.37 = (bf16[256,2048]{1,0:T(8,128)(2,1)S(1)}, bf16[256,2048]{1,0:T(8,128)(2,1)S(1)}, u32[]{:S(2)}, u32[]{:S(2)}) collective-permute-start(bf16[256,2048]{1,0:T(8,128)(2,1)S(1)} %get-tuple-element.317), channel_id=1, source_target_pairs={{0,2},{1,3},{2,0},{3,1},{4,6},{5,7},{6,4},{7,5},{8,10},{9,11},{10,... | collective-permute-start | bytes 3145736 | tf_op jit(solution)/shard_map/ppermute | solution.py:54
  485.3 281.0 %reduce-scatter.7.cloned.1.call-start = ((), (), s32[]{:S(2)}) async-start(), calls=%async_computation.9 | async-start | bytes 9437184 | tf_op jit(solution)/shard_map/reduce_scatter | solution.py:388
  494.0 22.4 %collective-permute-start.40 = (bf16[256,2048]{1,0:T(8,128)(2,1)S(1)}, bf16[256,2048]{1,0:T(8,128)(2,1)S(1)}, u32[]{:S(2)}, u32[]{:S(2)}) collective-permute-start(bf16[256,2048]{1,0:T(8,128)(2,1)S(1)} %get-tuple-element.187), channel_id=1, source_target_pairs={{0,1},{1,0},{2,3},{3,2},{4,5},{5,4},{6,7},{7,6},{8,9},{9,8},{10,11... | collective-permute-start | bytes 3145736 | tf_op jit(solution)/shard_map/ppermute | solution.py:54
  494.4 22.0 %collective-permute-start.41 = (bf16[256,2048]{1,0:T(8,128)(2,1)S(1)}, bf16[256,2048]{1,0:T(8,128)(2,1)S(1)}, u32[]{:S(2)}, u32[]{:S(2)}) collective-permute-start(bf16[256,2048]{1,0:T(8,128)(2,1)S(1)} %get-tuple-element.187), channel_id=1, source_target_pairs={{0,2},{1,3},{2,0},{3,1},{4,6},{5,7},{6,4},{7,5},{8,10},{9,11},{10,... | collective-permute-start | bytes 3145736 | tf_op jit(solution)/shard_map/ppermute | solution.py:54
  571.3 212.2 %reduce-scatter.11.cloned.1.call-start = ((), (), s32[]{:S(2)}) async-start(), calls=%async_computation.11 | async-start | bytes 2359296 | tf_op jit(solution)/shard_map/reduce_scatter | solution.py:388
  582.7 32.9 %collective-permute-start.48 = (bf16[256,2048]{1,0:T(8,128)(2,1)S(1)}, bf16[256,2048]{1,0:T(8,128)(2,1)S(1)}, u32[]{:S(2)}, u32[]{:S(2)}) collective-permute-start(bf16[256,2048]{1,0:T(8,128)(2,1)S(1)} %get-tuple-element.204), channel_id=1, source_target_pairs={{0,1},{1,0},{2,3},{3,2},{4,5},{5,4},{6,7},{7,6},{8,9},{9,8},{10,11... | collective-permute-start | bytes 3145736 | tf_op jit(solution)/shard_map/ppermute | solution.py:54
  583.8 31.9 %collective-permute-start.49 = (bf16[256,2048]{1,0:T(8,128)(2,1)S(1)}, bf16[256,2048]{1,0:T(8,128)(2,1)S(1)}, u32[]{:S(2)}, u32[]{:S(2)}) collective-permute-start(bf16[256,2048]{1,0:T(8,128)(2,1)S(1)} %get-tuple-element.204), channel_id=1, source_target_pairs={{0,2},{1,3},{2,0},{3,1},{4,6},{5,7},{6,4},{7,5},{8,10},{9,11},{10,... | collective-permute-start | bytes 3145736 | tf_op jit(solution)/shard_map/ppermute | solution.py:54
  668.9 118.9 %reduce-scatter.9.cloned.1.call-start = ((), (), s32[]{:S(2)}) async-start(), calls=%async_computation.10 | async-start | bytes 7077888 | tf_op jit(solution)/shard_map/reduce_scatter | solution.py:388
  (143 other events, 1841.6 us)
Sparse Core Ops, SparseCore 0:
  10.2 67.4 all-gather.4
  79.3 27.8 all-gather.6
  108.7 81.4 all-gather.8
  191.6 80.5 all-gather.10
  485.4 88.1 reduce-scatter.4
  575.8 87.9 reduce-scatter.6
  669.1 34.0 reduce-scatter.10
  713.2 67.8 reduce-scatter.8

commit v6 on v5

--- a/solution.py
+++ b/solution.py
@@ -576,27 +576,32 @@
     tokens_low, tokens_grad = lists(2)
 
     proj_terms = [None] * CHUNKS
-    tokens_low[0] = low(nt(after(grad_proj[0], down_part), proj_full))
+    proj_terms[0] = tn(after(seq_tokens[0], down_part), grad_proj[0])
+    proj_terms[1] = tn(after(seq_tokens[1], proj_terms[0]), grad_proj[1])
+    proj_grad = low(add_up(proj_terms))
+    proj_part = scatter_weight(proj_grad)
+    tokens_low[0] = low(nt(after(grad_proj[0], proj_grad), proj_full))
     near[0] = scatter_near(tokens_low[0])
-    proj_terms[1] = tn(after(seq_tokens[1], tokens_low[0]), grad_proj[1])
-    proj_terms[0] = tn(after(seq_tokens[0], proj_terms[1], *near[0][1]), grad_proj[0])
-    far[0] = scatter_far(near[0])
-    proj_grad = low(proj_terms[1] + proj_terms[0])
-    proj_part = scatter_weight(proj_grad)
-    tokens_low[1] = low(nt(after(grad_proj[1], proj_grad), proj_full))
-    near[1] = scatter_near(tokens_low[1], *far[0])
-    far[1] = scatter_far(near[1])
-    early = together((*(far[1] or near[1][1]), up_part))
-    if far[1]:
-        far[1] = early[:-1]
-    up_part = early[-1]
+    tokens_low[1] = low(nt(after(grad_proj[1], tokens_low[0]), proj_full))
+    far[0] = scatter_far(near[0], tokens_low[1])
+    near[1] = scatter_near(tokens_low[1], *(far[0] or near[0][1]))
+    proj_bias = add_up(
+        [jnp.sum(wide(after(grad_proj[c], tokens_low[1])), axis=0) for c in every]
+    )
+    sums = total_of(
+        [after(add_up([vec2[c][i] for c in every]), up_part) for i in range(3)]
+        + [add_up([vec1[c][i] for c in every]) for i in range(3)]
+        + [
+            placed(up_bias_part, hid_start, FF),
+            placed(proj_bias[:head_cols], col_start, width),
+            placed(proj_bias[2 * head_cols :], col_start, width),
+        ]
+    )
     out_part = after(out_part, up_part)
+    far[1] = scatter_far(near[1], sums[0])
     for c in every:
         tokens_grad[c] = low(grad_sum1[c] + scattered(near[c], far[c]))
     proj_part, out_part, up_part, down_part = map(wide, (proj_part, out_part, up_part, down_part))
-    proj_bias = add_up(
-        [jnp.sum(wide(after(grad_proj[c], tokens_low[1])), axis=0) for c in every]
-    )
     (
         norm2_gain_grad,
         norm2_shift_grad,
@@ -607,15 +612,7 @@
         up_bias_grad,
         query_bias_grad,
         value_bias_grad,
-    ) = total_of(
-        [after(add_up([vec2[c][i] for c in every]), up_part) for i in range(3)]
-        + [add_up([vec1[c][i] for c in every]) for i in range(3)]
-        + [
-            placed(up_bias_part, hid_start, FF),
-            placed(proj_bias[:head_cols], col_start, width),
-            placed(proj_bias[2 * head_cols :], col_start, width),
-        ]
-    )
+    ) = sums
     return (
         jnp.concatenate(layer_out, axis=0),
         jnp.concatenate(tokens_grad, axis=0),

time: 809 us -> 807 us (level)
    unnamed x237 -> x245, local copies, waits for them, and re-layouts: 40.3 us -> 38.3 us
  transfers between devices with their start and end apart: 78 -> 78, of which waited for: 37 -> 39; matrix products, arithmetic and copies ran while one was open for 47% -> 47% of each run, Pallas kernels for 12% -> 12%
where the time goes in v6:
time: 807 us; the launch traced here: 797 us
  matrix products  265 us (33%)
  waiting for transfers between devices  219 us (27%)
  Pallas kernels  95.3 us (12%)
  starting transfers between devices  70.9 us (9%)
  local copies, waits for them, and re-layouts  66.9 us (8%)
  other arithmetic  63.1 us (8%)
  between operations  16.9 us (2%)
    ppermute x63, waiting for transfers between devices, swap(): return lax.ppermute(value, 'tensor', [(i, i ^ bits) for i in range(size)])  214 us
    dot_general x8, matrix products, nn(): lax.dot_general(left, right, (((1,), (0,)), ((), ())), preferred_element_...  102 us
    dot_general x8, matrix products, tn(): lax.dot_general(left, right, (((0,), (0,)), ((), ())), preferred_element_...  92.3 us
    dot_general x8, matrix products, nt(): lax.dot_general(left, right, (((1,), (1,)), ((), ())), preferred_element_...  71.2 us
    ppermute x63, starting transfers between devices, swap(): return lax.ppermute(value, 'tensor', [(i, i ^ bits) for i in range(size)])  64.8 us
    pallas_call x2, Pallas kernels, attend_back(): pl.pallas_call(kernel, out_shape=(jax.ShapeDtypeStruct((part, cols), jnp....  55 us
    pallas_call x2, Pallas kernels, attend(): pl.pallas_call(kernel, out_shape=(jax.ShapeDtypeStruct((part, cols), jnp....  40.3 us
    unnamed x245, local copies, waits for them, and re-layouts  38.3 us
  transfers between devices with their start and end apart: 78, of which 39 were waited for; matrix products, arithmetic and copies ran while one was open for 47% of the time, Pallas kernels for 12%

profile of v6, /device:TPU:0, one launch (start us, length us, event | category | flops | bytes accessed | tf_op | source)
XLA Modules:
  0.0 797.0 jit_solution(6796564282920989521)
XLA Ops:
  20.7 19.0 %collective-permute-done = bf16[256,2048]{1,0:T(8,128)(2,1)} collective-permute-done((bf16[256,2048]{1,0:T(8,128)(2,1)}, bf16[256,2048]{1,0:T(8,128)(2,1)}, u32[]{:S(2)}, u32[]{:S(2)}) %collective-permute-start) | collective-permute-done | bytes 1048608 | tf_op jit(solution)/shard_map/ppermute | solution.py:54
  47.1 7.7 collective-permute-done.2
  61.7 17.3 %collective-permute-done.4 = bf16[256,2048]{1,0:T(8,128)(2,1)S(1)} collective-permute-done((bf16[256,2048]{1,0:T(8,128)(2,1)S(1)}, bf16[256,2048]{1,0:T(8,128)(2,1)S(1)}, u32[]{:S(2)}, u32[]{:S(2)}) %collective-permute-start.4) | collective-permute-done | bytes 1048608 | tf_op jit(solution)/shard_map/ppermute | solution.py:54
  84.7 11.6 %add_convert_fusion.6.q_ref.rest_0_.rest_2_ = bf16[1024,1536]{1,0:T(8,128)(2,1)} fusion(bf16[1024,2048]{1,0:T(8,128)(2,1)} %slice_dynamic-update-slice_fusion.28, bf16[2048,1536]{1,0:T(8,128)(2,1)} %all-gather.5.cloned.1.call-done, f32[1536]{0:T(1024)S(1)} %pad_maximum_fusion.9), kind=kOutput, calls=%fused_computation.22 | convolution fusion | flops 6445596672 | bytes 13637632 | tf_op jit(solution)/shard_map/dot_general | solution.py:26
  101.8 9.6 %add_convert_fusion.5.rest_1_.rest_3_.q_ref = bf16[1024,1536]{1,0:T(8,128)(2,1)} fusion(bf16[1024,2048]{1,0:T(8,128)(2,1)} %slice_dynamic-update-slice_fusion.24, bf16[2048,1536]{1,0:T(8,128)(2,1)S(1)} %copy-done.85, f32[1536]{0:T(1024)S(1)} %pad_maximum_fusion.9), kind=kOutput, calls=%fused_computation.21 | convolution fusion | flops 6445596672 | bytes 13637632 | tf_op jit(solution)/shard_map/dot_general | solution.py:26
  111.4 20.1 %attend.2 = (bf16[1024,512]{1,0:T(8,128)(2,1)}, f32[4,1,1024]{2,1,0:T(1,128)}) custom-call(s32[16]{0:T(128)} %stack.67.lim, bf16[1024,1536]{1,0:T(8,128)(2,1)} %add_convert_fusion.6.q_ref.rest_0_.rest_2_, bf16[1024,1536]{1,0:T(8,128)(2,1)} %add_convert_fusion.6.q_ref.rest_0_.rest_2_, bf16[1024,1536]{1,0:T(8,128)(2,1)} %add_convert_fusion.5.rest_1_.rest_3_.q_ref, ...), custom_call_target="tpu_custom_call" | custom-call | flops 8589934592 | bytes 6291456 | tf_op jit(solution)/shard_map/attend/pallas_call | solution.py:193
  139.6 20.3 %attend.3 = (bf16[1024,512]{1,0:T(8,128)(2,1)}, f32[4,1,1024]{2,1,0:T(1,128)}) custom-call(s32[16]{0:T(128)} %stack.67.lim, bf16[1024,1536]{1,0:T(8,128)(2,1)} %add_convert_fusion.5.rest_1_.rest_3_.q_ref, bf16[1024,1536]{1,0:T(8,128)(2,1)} %add_convert_fusion.6.q_ref.rest_0_.rest_2_, bf16[1024,1536]{1,0:T(8,128)(2,1)} %add_convert_fusion.5.rest_1_.rest_3_.q_ref, ...), custom_call_target="tpu_custom_call" | custom-call | flops 8589934592 | bytes 6291456 | tf_op jit(solution)/shard_map/attend/pallas_call | solution.py:193
  182.3 14.6 %collective-permute-done.12 = bf16[256,2048]{1,0:T(8,128)(2,1)S(1)} collective-permute-done((bf16[256,2048]{1,0:T(8,128)(2,1)S(1)}, bf16[256,2048]{1,0:T(8,128)(2,1)S(1)}, u32[]{:S(2)}, u32[]{:S(2)}) %collective-permute-start.12) | collective-permute-done | bytes 1048608 | tf_op jit(solution)/shard_map/ppermute | solution.py:54
  202.2 30.0 %collective-permute-done.14 = bf16[384,2048]{1,0:T(8,128)(2,1)S(1)} collective-permute-done((bf16[384,2048]{1,0:T(8,128)(2,1)}, bf16[384,2048]{1,0:T(8,128)(2,1)S(1)}, u32[]{:S(2)}, u32[]{:S(2)}) %collective-permute-start.14) | collective-permute-done | bytes 1572896 | tf_op jit(solution)/shard_map/ppermute | solution.py:54
  255.0 17.2 %multiply_convert_fusion.3 = (bf16[1024,2048]{1,0:T(8,128)(2,1)}, f32[1024,2048]{1,0:T(8,128)}) fusion(f32[2048]{0:T(1024)S(1)} %dynamic_slice.49, bf16[1024,2048]{1,0:T(8,128)(2,1)} %slice_dynamic-update-slice_fusion.20, bf16[2048,2048]{1,0:T(8,128)(2,1)} %all-gather.9.cloned.1.call-done), kind=kOutput, calls=%fused_computation.17 | convolution fusion | flops 8610906112 | bytes 25174016 | tf_op jit(solution)/shard_map/dot_general | solution.py:26
  276.5 12.7 %convolution_convert_fusion.5 = bf16[1024,2048]{1,0:T(8,128)(2,1)S(1)} fusion(bf16[1024,2048]{1,0:T(8,128)(2,1)} %get-tuple-element.155, bf16[2048,2048]{1,0:T(8,128)(2,1)} %all-gather.11.cloned.1.call-done), kind=kOutput, calls=%fused_computation.29 | convolution fusion | flops 8592031744 | bytes 16777216 | tf_op jit(solution)/shard_map/dot_general | solution.py:20
  296.6 17.3 %multiply_convert_fusion.2 = (bf16[1024,2048]{1,0:T(8,128)(2,1)}, f32[1024,2048]{1,0:T(8,128)}) fusion(f32[2048]{0:T(1024)S(1)} %dynamic_slice.49, bf16[1024,2048]{1,0:T(8,128)(2,1)S(1)} %slice_dynamic-update-slice_fusion.16, bf16[2048,2048]{1,0:T(8,128)(2,1)} %all-gather.9.cloned.1.call-done), kind=kOutput, calls=%fused_computation.15 | convolution fusion | flops 8610906112 | bytes 25174016 | tf_op jit(solution)/shard_map/dot_general | solution.py:26
  316.3 10.9 %convolution_convert_fusion.4 = bf16[1024,2048]{1,0:T(8,128)(2,1)S(1)} fusion(bf16[1024,2048]{1,0:T(8,128)(2,1)} %get-tuple-element.164, bf16[2048,2048]{1,0:T(8,128)(2,1)S(1)} %bitcast.103), kind=kOutput, calls=%fused_computation.28 | convolution fusion | flops 8592031744 | bytes 16777216 | tf_op jit(solution)/shard_map/dot_general | solution.py:20
  338.0 11.7 %collective-permute-done.26 = bf16[256,2048]{1,0:T(8,128)(2,1)S(1)} collective-permute-done((bf16[256,2048]{1,0:T(8,128)(2,1)S(1)}, bf16[256,2048]{1,0:T(8,128)(2,1)S(1)}, u32[]{:S(2)}, u32[]{:S(2)}) %collective-permute-start.26) | collective-permute-done | bytes 1048608 | tf_op jit(solution)/shard_map/ppermute | solution.py:54
  355.7 29.7 %collective-permute-done.28 = bf16[384,2048]{1,0:T(8,128)(2,1)S(1)} collective-permute-done((bf16[384,2048]{1,0:T(8,128)(2,1)S(1)}, bf16[384,2048]{1,0:T(8,128)(2,1)S(1)}, u32[]{:S(2)}, u32[]{:S(2)}) %collective-permute-start.28) | collective-permute-done | bytes 1572896 | tf_op jit(solution)/shard_map/ppermute | solution.py:54
  393.4 8.6 %collective-permute-done.30 = bf16[128,2048]{1,0:T(8,128)(2,1)S(1)} collective-permute-done((bf16[128,2048]{1,0:T(8,128)(2,1)S(1)}, bf16[128,2048]{1,0:T(8,128)(2,1)S(1)}, u32[]{:S(2)}, u32[]{:S(2)}) %collective-permute-start.30) | collective-permute-done | bytes 524320 | tf_op jit(solution)/shard_map/ppermute | solution.py:54
  406.1 19.5 %convert_reduce_fusion.1 = (f32[2048]{0:T(1024)}, bf16[1024,2048]{1,0:T(8,128)(2,1)}) fusion(f32[1024,2048]{1,0:T(8,128)} %get-tuple-element.369, f32[2048]{0:T(1024)S(1)} %dynamic_slice.49, bf16[1024,2048]{1,0:T(8,128)(2,1)S(1)} %slice_dynamic-update-slice_fusion.12, bf16[2048,2048]{1,0:T(8,128)(2,1)} %all-gather.11.cloned.1.call-done), kind=kOutput, calls=%fused_computation.10 | convolution fusion | flops 8638167040 | bytes 25182208 | tf_op jit(solution)/shard_map/dot_general | solution.py:26
  429.0 10.7 %convolution_convert_fusion.3 = bf16[1024,2048]{1,0:T(8,128)(2,1)S(1)} fusion(bf16[1024,2048]{1,0:T(8,128)(2,1)} %get-tuple-element.176, bf16[2048,2048]{1,0:T(8,128)(2,1)S(1)} %bitcast.99), kind=kOutput, calls=%fused_computation.27 | convolution fusion | flops 8592031744 | bytes 16777216 | tf_op jit(solution)/shard_map/dot_general | solution.py:20
  444.9 11.6 %fusion.50 = f32[2048,2048]{1,0:T(8,128)} fusion(bf16[1024,2048]{1,0:T(8,128)(2,1)S(1)} %slice_dynamic-update-slice_fusion.4, bf16[1024,2048]{1,0:T(8,128)(2,1)S(1)} %copy-done.89), kind=kOutput, calls=%fused_computation.245 | convolution fusion | flops 8589934592 | bytes 25165824 | tf_op jit(solution)/shard_map/dot_general | solution.py:32
  456.6 7.0 collective-permute-done.36
  468.0 16.2 %add_convert_fusion.1 = bf16[2048,2048]{1,0:T(8,128)(2,1)} fusion(f32[2048,2048]{1,0:T(8,128)} %fusion.50, bf16[1024,2048]{1,0:T(8,128)(2,1)S(1)} %slice_dynamic-update-slice_fusion.12, bf16[1024,2048]{1,0:T(8,128)(2,1)} %get-tuple-element.155), kind=kOutput, calls=%fused_computation.1 | convolution fusion | flops 8598323200 | bytes 33554432 | tf_op jit(solution)/shard_map/dot_general | solution.py:32
  495.5 17.2 %convert_reduce_fusion = (f32[2048]{0:T(1024)}, bf16[1024,2048]{1,0:T(8,128)(2,1)}) fusion(f32[1024,2048]{1,0:T(8,128)} %get-tuple-element.371, f32[2048]{0:T(1024)S(1)} %dynamic_slice.49, bf16[1024,2048]{1,0:T(8,128)(2,1)S(1)} %copy-done.62, bf16[2048,2048]{1,0:T(8,128)(2,1)S(1)} %bitcast.105), kind=kOutput, calls=%fused_computation.9 | convolution fusion | flops 8638167040 | bytes 25182208 | tf_op jit(solution)/shard_map/dot_general | solution.py:26
  517.4 10.7 %convolution_convert_fusion.2 = bf16[1024,2048]{1,0:T(8,128)(2,1)S(1)} fusion(bf16[1024,2048]{1,0:T(8,128)(2,1)} %get-tuple-element.190, bf16[2048,2048]{1,0:T(8,128)(2,1)S(1)} %bitcast.101), kind=kOutput, calls=%fused_computation.26 | convolution fusion | flops 8592031744 | bytes 16777216 | tf_op jit(solution)/shard_map/dot_general | solution.py:20
  533.6 14.2 %fusion.51 = f32[2048,2048]{1,0:T(8,128)} fusion(bf16[1024,2048]{1,0:T(8,128)(2,1)} %slice_dynamic-update-slice_fusion.20, bf16[1024,2048]{1,0:T(8,128)(2,1)S(1)} %copy-done.90), kind=kOutput, calls=%fused_computation.246 | convolution fusion | flops 8589934592 | bytes 25165824 | tf_op jit(solution)/shard_map/dot_general | solution.py:32
  555.5 16.1 %add_convert_fusion = bf16[2048,2048]{1,0:T(8,128)(2,1)} fusion(f32[2048,2048]{1,0:T(8,128)} %fusion.51, bf16[1024,2048]{1,0:T(8,128)(2,1)S(1)} %copy-done.60, bf16[1024,2048]{1,0:T(8,128)(2,1)} %get-tuple-element.190), kind=kOutput, calls=%fused_computation | convolution fusion | flops 8598323200 | bytes 33554432 | tf_op jit(solution)/shard_map/dot_general | solution.py:32
  588.6 27.4 %attend_back.2 = (bf16[1024,512]{1,0:T(8,128)(2,1)}, f32[2048,512]{1,0:T(8,128)}, f32[2048,512]{1,0:T(8,128)}) custom-call(s32[16]{0:T(128)} %stack.67.lim, bf16[1024,1536]{1,0:T(8,128)(2,1)} %add_convert_fusion.6.q_ref.rest_0_.rest_2_, bf16[1024,512]{1,0:T(8,128)(2,1)} %get-tuple-element.135.o_ref, bf16[1024,512]{1,0:T(8,128)(2,1)} %convolution_convert_fusion.9.do_ref, ...), custom_call_target="tpu_custom_call" | custom-call | flops 21474836480 | bytes 20971520 | tf_op jit(solution)/shard_map/attend_back/pallas_call | solution.py:285
  638.6 27.5 %attend_back.3 = (bf16[1024,512]{1,0:T(8,128)(2,1)}, bf16[2048,512]{1,0:T(8,128)(2,1)}, bf16[2048,512]{1,0:T(8,128)(2,1)}) custom-call(s32[16]{0:T(128)} %stack.67.lim, bf16[1024,1536]{1,0:T(8,128)(2,1)} %add_convert_fusion.5.rest_1_.rest_3_.q_ref, bf16[1024,512]{1,0:T(8,128)(2,1)} %get-tuple-element.143.o_ref, ...), custom_call_target="tpu_custom_call" | custom-call | flops 21474836480 | bytes 20971520 | tf_op jit(solution)/shard_map/attend_back/pallas_call | solution.py:285
  670.4 12.2 %fusion.21 = f32[2048,1536]{1,0:T(8,128)} fusion(bf16[1024,2048]{1,0:T(8,128)(2,1)} %slice_dynamic-update-slice_fusion.28, bf16[1024,512]{1,0:T(8,128)(2,1)S(1)} %get-tuple-element.341, bf16[1024,512]{1,0:T(8,128)(2,1)} %get-tuple-element.339, bf16[1024,512]{1,0:T(8,128)(2,1)} %get-tuple-element.200), kind=kOutput, calls=%fused_computation.222 | convolution fusion | flops 6451888128 | bytes 19922944 | tf_op jit(solution)/shard_map/dot_general | solution.py:32
  682.6 13.5 %add_convert_fusion.2 = bf16[2048,1536]{1,0:T(8,128)(2,1)} fusion(f32[2048,1536]{1,0:T(8,128)} %fusion.21, bf16[1024,2048]{1,0:T(8,128)(2,1)} %slice_dynamic-update-slice_fusion.24, bf16[1024,512]{1,0:T(8,128)(2,1)S(1)} %copy-done.24, bf16[1024,512]{1,0:T(8,128)(2,1)S(1)} %copy-done.26, bf16[1024,512]{1,0:T(8,128)(2,1)S(1)} %copy-done.50), kind=kOutput, calls=%fused_computation.2 | convolution fusion | flops 6458179584 | bytes 26214400 | tf_op jit(solution)/shard_map/dot_general | solution.py:32
  700.0 9.4 %convolution_convert_fusion.1 = bf16[1024,2048]{1,0:T(8,128)(2,1)S(1)} fusion(bf16[1024,1536]{1,0:T(8,128)(2,1)S(1)} %pad_maximum_fusion, bf16[2048,1536]{1,0:T(8,128)(2,1)} %all-gather.5.cloned.1.call-done), kind=kOutput, calls=%fused_computation.25 | convolution fusion | flops 6444548096 | bytes 13631488 | tf_op jit(solution)/shard_map/dot_general | solution.py:20
  711.4 8.3 %convolution_convert_fusion = bf16[1024,2048]{1,0:T(8,128)(2,1)} fusion(bf16[1024,1536]{1,0:T(8,128)(2,1)S(1)} %pad_maximum_fusion.1, bf16[2048,1536]{1,0:T(8,128)(2,1)S(1)} %bitcast.107), kind=kOutput, calls=%fused_computation.24 | convolution fusion | flops 6444548096 | bytes 13631488 | tf_op jit(solution)/shard_map/dot_general | solution.py:20
  756.1 9.4 %collective-permute-done.56 = bf16[256,2048]{1,0:T(8,128)(2,1)S(1)} collective-permute-done((bf16[256,2048]{1,0:T(8,128)(2,1)S(1)}, bf16[256,2048]{1,0:T(8,128)(2,1)S(1)}, u32[]{:S(2)}, u32[]{:S(2)}) %collective-permute-start.56) | collective-permute-done | bytes 1048608 | tf_op jit(solution)/shard_map/ppermute | solution.py:54
  (554 shorter events, 291.0 us)
Async XLA Ops:
  7.2 77.5 %all-gather.5.cloned.1.call-start = ((), (), s32[]{:S(2)}) async-start(), calls=%async_computation.4 | async-start | bytes 7077888 | tf_op jit(solution)/shard_map/all_gather | solution.py:384
  9.5 122.0 %all-gather.7.cloned.1.call-start = ((), (), s32[]{:S(2)}) async-start(), calls=%async_computation.5 | async-start | bytes 2359296 | tf_op jit(solution)/shard_map/all_gather | solution.py:384
  10.2 244.8 %all-gather.9.cloned.1.call-start = ((), (), s32[]{:S(2)}) async-start(), calls=%async_computation.6 | async-start | bytes 9437184 | tf_op jit(solution)/shard_map/all_gather | solution.py:384
  10.9 265.6 %all-gather.11.cloned.1.call-start = ((), (), s32[]{:S(2)}) async-start(), calls=%async_computation.7 | async-start | bytes 9437184 | tf_op jit(solution)/shard_map/all_gather | solution.py:384
  13.3 26.4 %collective-permute-start = (bf16[256,2048]{1,0:T(8,128)(2,1)}, bf16[256,2048]{1,0:T(8,128)(2,1)}, u32[]{:S(2)}, u32[]{:S(2)}) collective-permute-start(bf16[256,2048]{1,0:T(8,128)(2,1)} %get-tuple-element.346), channel_id=1, source_target_pairs={{0,1},{1,0},{2,3},{3,2},{4,5},{5,4},{6,7},{7,6},{8,9},{9,8},{10,11... | collective-permute-start | bytes 3145736 | tf_op jit(solution)/shard_map/ppermute | solution.py:54
  16.2 24.8 %collective-permute-start.1 = (bf16[256,2048]{1,0:T(8,128)(2,1)}, bf16[256,2048]{1,0:T(8,128)(2,1)S(1)}, u32[]{:S(2)}, u32[]{:S(2)}) collective-permute-start(bf16[256,2048]{1,0:T(8,128)(2,1)} %get-tuple-element.346), channel_id=1, source_target_pairs={{0,2},{1,3},{2,0},{3,1},{4,6},{5,7},{6,4},{7,5},{8,10},{9,11},{10,... | collective-permute-start | bytes 3145736 | tf_op jit(solution)/shard_map/ppermute | solution.py:54
  17.8 652.6 %reduce-scatter.5.cloned.1.call-start = ((), (), s32[]{:S(2)}) async-start(), calls=%async_computation.8 | async-start | bytes 9437184 | tf_op jit(solution)/shard_map/reduce_scatter | solution.py:388
  56.2 22.8 %collective-permute-start.4 = (bf16[256,2048]{1,0:T(8,128)(2,1)S(1)}, bf16[256,2048]{1,0:T(8,128)(2,1)S(1)}, u32[]{:S(2)}, u32[]{:S(2)}) collective-permute-start(bf16[256,2048]{1,0:T(8,128)(2,1)S(1)} %copy-done.49), channel_id=1, source_target_pairs={{0,1},{1,0},{2,3},{3,2},{4,5},{5,4},{6,7},{7,6},{8,9},{9,8},{10,11... | collective-permute-start | bytes 3145736 | tf_op jit(solution)/shard_map/ppermute | solution.py:54
  56.8 22.6 %collective-permute-start.5 = (bf16[256,2048]{1,0:T(8,128)(2,1)S(1)}, bf16[256,2048]{1,0:T(8,128)(2,1)S(1)}, u32[]{:S(2)}, u32[]{:S(2)}) collective-permute-start(bf16[256,2048]{1,0:T(8,128)(2,1)S(1)} %copy-done.49), channel_id=1, source_target_pairs={{0,2},{1,3},{2,0},{3,1},{4,6},{5,7},{6,4},{7,5},{8,10},{9,11},{10,... | collective-permute-start | bytes 3145736 | tf_op jit(solution)/shard_map/ppermute | solution.py:54
  137.3 22.6 %collective-permute-start.8 = (bf16[256,2048]{1,0:T(8,128)(2,1)}, bf16[256,2048]{1,0:T(8,128)(2,1)S(1)}, u32[]{:S(2)}, u32[]{:S(2)}) collective-permute-start(bf16[256,2048]{1,0:T(8,128)(2,1)} %get-tuple-element.336), channel_id=1, source_target_pairs={{0,1},{1,0},{2,3},{3,2},{4,5},{5,4},{6,7},{7,6},{8,9},{9,8},{10,11... | collective-permute-start | bytes 3145736 | tf_op jit(solution)/shard_map/ppermute | solution.py:54
  138.3 21.7 %collective-permute-start.9 = (bf16[256,2048]{1,0:T(8,128)(2,1)}, bf16[256,2048]{1,0:T(8,128)(2,1)}, u32[]{:S(2)}, u32[]{:S(2)}) collective-permute-start(bf16[256,2048]{1,0:T(8,128)(2,1)} %get-tuple-element.335), channel_id=1, source_target_pairs={{0,2},{1,3},{2,0},{3,1},{4,6},{5,7},{6,4},{7,5},{8,10},{9,11},{10,... | collective-permute-start | bytes 3145736 | tf_op jit(solution)/shard_map/ppermute | solution.py:54
  175.8 21.0 %collective-permute-start.12 = (bf16[256,2048]{1,0:T(8,128)(2,1)S(1)}, bf16[256,2048]{1,0:T(8,128)(2,1)S(1)}, u32[]{:S(2)}, u32[]{:S(2)}) collective-permute-start(bf16[256,2048]{1,0:T(8,128)(2,1)S(1)} %get-tuple-element.330), channel_id=1, source_target_pairs={{0,1},{1,0},{2,3},{3,2},{4,5},{5,4},{6,7},{7,6},{8,9},{9,8},{10,11... | collective-permute-start | bytes 3145736 | tf_op jit(solution)/shard_map/ppermute | solution.py:54
  199.3 32.9 %collective-permute-start.14 = (bf16[384,2048]{1,0:T(8,128)(2,1)}, bf16[384,2048]{1,0:T(8,128)(2,1)S(1)}, u32[]{:S(2)}, u32[]{:S(2)}) collective-permute-start(bf16[384,2048]{1,0:T(8,128)(2,1)} %get-tuple-element.149), channel_id=1, source_target_pairs={{0,1},{1,0},{2,3},{3,2},{4,5},{5,4},{6,7},{7,6},{8,9},{9,8},{10,11... | collective-permute-start | bytes 4718600 | tf_op jit(solution)/shard_map/ppermute | solution.py:54
  201.4 31.0 %collective-permute-start.15 = (bf16[384,2048]{1,0:T(8,128)(2,1)}, bf16[384,2048]{1,0:T(8,128)(2,1)S(1)}, u32[]{:S(2)}, u32[]{:S(2)}) collective-permute-start(bf16[384,2048]{1,0:T(8,128)(2,1)} %get-tuple-element.150), channel_id=1, source_target_pairs={{0,2},{1,3},{2,0},{3,1},{4,6},{5,7},{6,4},{7,5},{8,10},{9,11},{10,... | collective-permute-start | bytes 4718600 | tf_op jit(solution)/shard_map/ppermute | solution.py:54
  249.1 23.1 %collective-permute-start.18 = (bf16[256,2048]{1,0:T(8,128)(2,1)}, bf16[256,2048]{1,0:T(8,128)(2,1)}, u32[]{:S(2)}, u32[]{:S(2)}) collective-permute-start(bf16[256,2048]{1,0:T(8,128)(2,1)} %get-tuple-element.154), channel_id=1, source_target_pairs={{0,1},{1,0},{2,3},{3,2},{4,5},{5,4},{6,7},{7,6},{8,9},{9,8},{10,11... | collective-permute-start | bytes 3145736 | tf_op jit(solution)/shard_map/ppermute | solution.py:54
  250.3 21.9 %collective-permute-start.19 = (bf16[256,2048]{1,0:T(8,128)(2,1)}, bf16[256,2048]{1,0:T(8,128)(2,1)S(1)}, u32[]{:S(2)}, u32[]{:S(2)}) collective-permute-start(bf16[256,2048]{1,0:T(8,128)(2,1)} %get-tuple-element.154), channel_id=1, source_target_pairs={{0,2},{1,3},{2,0},{3,1},{4,6},{5,7},{6,4},{7,5},{8,10},{9,11},{10,... | collective-permute-start | bytes 3145736 | tf_op jit(solution)/shard_map/ppermute | solution.py:54
  290.6 23.3 %collective-permute-start.22 = (bf16[256,2048]{1,0:T(8,128)(2,1)S(1)}, bf16[256,2048]{1,0:T(8,128)(2,1)S(1)}, u32[]{:S(2)}, u32[]{:S(2)}) collective-permute-start(bf16[256,2048]{1,0:T(8,128)(2,1)S(1)} %get-tuple-element.324), channel_id=1, source_target_pairs={{0,1},{1,0},{2,3},{3,2},{4,5},{5,4},{6,7},{7,6},{8,9},{9,8},{10,11... | collective-permute-start | bytes 3145736 | tf_op jit(solution)/shard_map/ppermute | solution.py:54
  291.8 22.1 %collective-permute-start.23 = (bf16[256,2048]{1,0:T(8,128)(2,1)S(1)}, bf16[256,2048]{1,0:T(8,128)(2,1)S(1)}, u32[]{:S(2)}, u32[]{:S(2)}) collective-permute-start(bf16[256,2048]{1,0:T(8,128)(2,1)S(1)} %get-tuple-element.323), channel_id=1, source_target_pairs={{0,2},{1,3},{2,0},{3,1},{4,6},{5,7},{6,4},{7,5},{8,10},{9,11},{10,... | collective-permute-start | bytes 3145736 | tf_op jit(solution)/shard_map/ppermute | solution.py:54
  331.6 21.9 %collective-permute-start.27 = (bf16[256,2048]{1,0:T(8,128)(2,1)S(1)}, bf16[256,2048]{1,0:T(8,128)(2,1)S(1)}, u32[]{:S(2)}, u32[]{:S(2)}) collective-permute-start(bf16[256,2048]{1,0:T(8,128)(2,1)S(1)} %get-tuple-element.317), channel_id=1, source_target_pairs={{0,2},{1,3},{2,0},{3,1},{4,6},{5,7},{6,4},{7,5},{8,10},{9,11},{10,... | collective-permute-start | bytes 3145736 | tf_op jit(solution)/shard_map/ppermute | solution.py:54
  354.3 31.1 %collective-permute-start.28 = (bf16[384,2048]{1,0:T(8,128)(2,1)S(1)}, bf16[384,2048]{1,0:T(8,128)(2,1)S(1)}, u32[]{:S(2)}, u32[]{:S(2)}) collective-permute-start(bf16[384,2048]{1,0:T(8,128)(2,1)S(1)} %get-tuple-element.170), channel_id=1, source_target_pairs={{0,2},{1,3},{2,0},{3,1},{4,6},{5,7},{6,4},{7,5},{8,10},{9,11},{10,... | collective-permute-start | bytes 4718600 | tf_op jit(solution)/shard_map/ppermute | solution.py:54
  355.6 29.8 %collective-permute-start.29 = (bf16[384,2048]{1,0:T(8,128)(2,1)S(1)}, bf16[384,2048]{1,0:T(8,128)(2,1)S(1)}, u32[]{:S(2)}, u32[]{:S(2)}) collective-permute-start(bf16[384,2048]{1,0:T(8,128)(2,1)S(1)} %get-tuple-element.171), channel_id=1, source_target_pairs={{0,1},{1,0},{2,3},{3,2},{4,5},{5,4},{6,7},{7,6},{8,9},{9,8},{10,11... | collective-permute-start | bytes 4718600 | tf_op jit(solution)/shard_map/ppermute | solution.py:54
  405.0 22.1 %collective-permute-start.32 = (bf16[256,2048]{1,0:T(8,128)(2,1)S(1)}, bf16[256,2048]{1,0:T(8,128)(2,1)S(1)}, u32[]{:S(2)}, u32[]{:S(2)}) collective-permute-start(bf16[256,2048]{1,0:T(8,128)(2,1)S(1)} %get-tuple-element.175), channel_id=1, source_target_pairs={{0,1},{1,0},{2,3},{3,2},{4,5},{5,4},{6,7},{7,6},{8,9},{9,8},{10,11... | collective-permute-start | bytes 3145736 | tf_op jit(solution)/shard_map/ppermute | solution.py:54
  405.0 22.1 %collective-permute-start.33 = (bf16[256,2048]{1,0:T(8,128)(2,1)S(1)}, bf16[256,2048]{1,0:T(8,128)(2,1)S(1)}, u32[]{:S(2)}, u32[]{:S(2)}) collective-permute-start(bf16[256,2048]{1,0:T(8,128)(2,1)S(1)} %get-tuple-element.175), channel_id=1, source_target_pairs={{0,2},{1,3},{2,0},{3,1},{4,6},{5,7},{6,4},{7,5},{8,10},{9,11},{10,... | collective-permute-start | bytes 3145736 | tf_op jit(solution)/shard_map/ppermute | solution.py:54
  485.2 244.3 %reduce-scatter.7.cloned.1.call-start = ((), (), s32[]{:S(2)}) async-start(), calls=%async_computation.9 | async-start | bytes 9437184 | tf_op jit(solution)/shard_map/reduce_scatter | solution.py:388
  493.9 22.4 %collective-permute-start.40 = (bf16[256,2048]{1,0:T(8,128)(2,1)S(1)}, bf16[256,2048]{1,0:T(8,128)(2,1)S(1)}, u32[]{:S(2)}, u32[]{:S(2)}) collective-permute-start(bf16[256,2048]{1,0:T(8,128)(2,1)S(1)} %get-tuple-element.184), channel_id=1, source_target_pairs={{0,1},{1,0},{2,3},{3,2},{4,5},{5,4},{6,7},{7,6},{8,9},{9,8},{10,11... | collective-permute-start | bytes 3145736 | tf_op jit(solution)/shard_map/ppermute | solution.py:54
  494.3 21.9 %collective-permute-start.41 = (bf16[256,2048]{1,0:T(8,128)(2,1)S(1)}, bf16[256,2048]{1,0:T(8,128)(2,1)S(1)}, u32[]{:S(2)}, u32[]{:S(2)}) collective-permute-start(bf16[256,2048]{1,0:T(8,128)(2,1)S(1)} %get-tuple-element.184), channel_id=1, source_target_pairs={{0,2},{1,3},{2,0},{3,1},{4,6},{5,7},{6,4},{7,5},{8,10},{9,11},{10,... | collective-permute-start | bytes 3145736 | tf_op jit(solution)/shard_map/ppermute | solution.py:54
  571.7 200.0 %reduce-scatter.11.cloned.1.call-start = ((), (), s32[]{:S(2)}) async-start(), calls=%async_computation.11 | async-start | bytes 2359296 | tf_op jit(solution)/shard_map/reduce_scatter | solution.py:388
  583.1 32.8 %collective-permute-start.48 = (bf16[256,2048]{1,0:T(8,128)(2,1)S(1)}, bf16[256,2048]{1,0:T(8,128)(2,1)S(1)}, u32[]{:S(2)}, u32[]{:S(2)}) collective-permute-start(bf16[256,2048]{1,0:T(8,128)(2,1)S(1)} %get-tuple-element.201), channel_id=1, source_target_pairs={{0,1},{1,0},{2,3},{3,2},{4,5},{5,4},{6,7},{7,6},{8,9},{9,8},{10,11... | collective-permute-start | bytes 3145736 | tf_op jit(solution)/shard_map/ppermute | solution.py:54
  584.0 32.0 %collective-permute-start.49 = (bf16[256,2048]{1,0:T(8,128)(2,1)S(1)}, bf16[256,2048]{1,0:T(8,128)(2,1)S(1)}, u32[]{:S(2)}, u32[]{:S(2)}) collective-permute-start(bf16[256,2048]{1,0:T(8,128)(2,1)S(1)} %get-tuple-element.201), channel_id=1, source_target_pairs={{0,2},{1,3},{2,0},{3,1},{4,6},{5,7},{6,4},{7,5},{8,10},{9,11},{10,... | collective-permute-start | bytes 3145736 | tf_op jit(solution)/shard_map/ppermute | solution.py:54
  632.1 155.4 %reduce-scatter.9.cloned.1.call-start = ((), (), s32[]{:S(2)}) async-start(), calls=%async_computation.10 | async-start | bytes 7077888 | tf_op jit(solution)/shard_map/reduce_scatter | solution.py:388
  739.9 25.6 %collective-permute-start.56 = (bf16[256,2048]{1,0:T(8,128)(2,1)S(1)}, bf16[256,2048]{1,0:T(8,128)(2,1)S(1)}, u32[]{:S(2)}, u32[]{:S(2)}) collective-permute-start(bf16[256,2048]{1,0:T(8,128)(2,1)S(1)} %get-tuple-element.296), channel_id=1, source_target_pairs={{0,1},{1,0},{2,3},{3,2},{4,5},{5,4},{6,7},{7,6},{8,9},{9,8},{10,11... | collective-permute-start | bytes 3145736 | tf_op jit(solution)/shard_map/ppermute | solution.py:54
  741.0 25.2 %collective-permute-start.57 = (bf16[256,2048]{1,0:T(8,128)(2,1)S(1)}, bf16[256,2048]{1,0:T(8,128)(2,1)S(1)}, u32[]{:S(2)}, u32[]{:S(2)}) collective-permute-start(bf16[256,2048]{1,0:T(8,128)(2,1)S(1)} %get-tuple-element.295), channel_id=1, source_target_pairs={{0,2},{1,3},{2,0},{3,1},{4,6},{5,7},{6,4},{7,5},{8,10},{9,11},{10,... | collective-permute-start | bytes 3145736 | tf_op jit(solution)/shard_map/ppermute | solution.py:54
  (147 other events, 1917.9 us)
Sparse Core Ops, SparseCore 0:
  10.2 67.4 all-gather.4
  79.3 27.8 all-gather.6
  108.7 81.4 all-gather.8
  191.7 80.5 all-gather.10
  485.3 88.9 reduce-scatter.4
  576.5 87.9 reduce-scatter.6
  667.3 34.4 reduce-scatter.10
  704.1 69.0 reduce-scatter.8

commit v7 on v6

--- a/solution.py
+++ b/solution.py
@@ -577,19 +577,19 @@
 
     proj_terms = [None] * CHUNKS
     proj_terms[0] = tn(after(seq_tokens[0], down_part), grad_proj[0])
-    proj_terms[1] = tn(after(seq_tokens[1], proj_terms[0]), grad_proj[1])
+    tokens_low[0] = low(nt(after(grad_proj[0], proj_terms[0]), proj_full))
+    near[0] = scatter_near(tokens_low[0])
+    proj_terms[1] = tn(after(seq_tokens[1], tokens_low[0]), grad_proj[1])
     proj_grad = low(add_up(proj_terms))
-    proj_part = scatter_weight(proj_grad)
-    tokens_low[0] = low(nt(after(grad_proj[0], proj_grad), proj_full))
-    near[0] = scatter_near(tokens_low[0])
-    tokens_low[1] = low(nt(after(grad_proj[1], tokens_low[0]), proj_full))
-    far[0] = scatter_far(near[0], tokens_low[1])
+    proj_part = scatter_weight(after(proj_grad, *near[0][1]))
+    tokens_low[1] = low(nt(after(grad_proj[1], proj_grad, *near[0][1]), proj_full))
+    far[0] = scatter_far(near[0])
     near[1] = scatter_near(tokens_low[1], *(far[0] or near[0][1]))
     proj_bias = add_up(
         [jnp.sum(wide(after(grad_proj[c], tokens_low[1])), axis=0) for c in every]
     )
     sums = total_of(
-        [after(add_up([vec2[c][i] for c in every]), up_part) for i in range(3)]
+        [after(add_up([vec2[c][i] for c in every]), up_part, *far[0]) for i in range(3)]
         + [add_up([vec1[c][i] for c in every]) for i in range(3)]
         + [
             placed(up_bias_part, hid_start, FF),

time: 807 us -> 819 us (1.015)
    ppermute x63, waiting for transfers between devices: 214 us -> 224 us  [swap(): return lax.ppermute(value, 'tensor', [(i, i ^ bits) for i in range(size)])]
    unnamed x245 -> x231, local copies, waits for them, and re-layouts: 38.3 us -> 39.1 us
  transfers between devices with their start and end apart: 78 -> 78, of which waited for: 39 -> 45; matrix products, arithmetic and copies ran while one was open for 47% -> 47% of each run, Pallas kernels for 12% -> 11%
where the time goes in v7:
time: 819 us; the launch traced here: 808 us
  matrix products  268 us (33%)
  waiting for transfers between devices  227 us (28%)
  Pallas kernels  92 us (11%)
  local copies, waits for them, and re-layouts  69 us (8%)
  other arithmetic  68.1 us (8%)
  starting transfers between devices  66.8 us (8%)
  between operations  17 us (2%)
    ppermute x63, waiting for transfers between devices, swap(): return lax.ppermute(value, 'tensor', [(i, i ^ bits) for i in range(size)])  224 us
    dot_general x8, matrix products, nn(): lax.dot_general(left, right, (((1,), (0,)), ((), ())), preferred_element_...  102 us
    dot_general x8, matrix products, tn(): lax.dot_general(left, right, (((0,), (0,)), ((), ())), preferred_element_...  92.2 us
    dot_general x8, matrix products, nt(): lax.dot_general(left, right, (((1,), (1,)), ((), ())), preferred_element_...  74.2 us
    ppermute x63, starting transfers between devices, swap(): return lax.ppermute(value, 'tensor', [(i, i ^ bits) for i in range(size)])  61.6 us
    pallas_call x2, Pallas kernels, attend_back(): pl.pallas_call(kernel, out_shape=(jax.ShapeDtypeStruct((part, cols), jnp....  53.8 us
    unnamed x231, local copies, waits for them, and re-layouts  39.1 us
    pallas_call x2, Pallas kernels, attend(): pl.pallas_call(kernel, out_shape=(jax.ShapeDtypeStruct((part, cols), jnp....  38.2 us
  transfers between devices with their start and end apart: 78, of which 45 were waited for; matrix products, arithmetic and copies ran while one was open for 47% of the time, Pallas kernels for 11%

profile of v7, /device:TPU:0, one launch (start us, length us, event | category | flops | bytes accessed | tf_op | source)
XLA Modules:
  0.0 808.2 jit_solution(15698031118344406133)
XLA Ops:
  20.7 19.0 %collective-permute-done = bf16[256,2048]{1,0:T(8,128)(2,1)} collective-permute-done((bf16[256,2048]{1,0:T(8,128)(2,1)}, bf16[256,2048]{1,0:T(8,128)(2,1)}, u32[]{:S(2)}, u32[]{:S(2)}) %collective-permute-start) | collective-permute-done | bytes 1048608 | tf_op jit(solution)/shard_map/ppermute | solution.py:54
  47.1 7.7 collective-permute-done.2
  61.7 17.3 %collective-permute-done.4 = bf16[256,2048]{1,0:T(8,128)(2,1)S(1)} collective-permute-done((bf16[256,2048]{1,0:T(8,128)(2,1)S(1)}, bf16[256,2048]{1,0:T(8,128)(2,1)S(1)}, u32[]{:S(2)}, u32[]{:S(2)}) %collective-permute-start.4) | collective-permute-done | bytes 1048608 | tf_op jit(solution)/shard_map/ppermute | solution.py:54
  84.7 11.6 %add_convert_fusion.6.q_ref.rest_0_.rest_2_ = bf16[1024,1536]{1,0:T(8,128)(2,1)} fusion(bf16[1024,2048]{1,0:T(8,128)(2,1)} %slice_dynamic-update-slice_fusion.28, bf16[2048,1536]{1,0:T(8,128)(2,1)} %all-gather.5.cloned.1.call-done, f32[1536]{0:T(1024)S(1)} %pad_maximum_fusion.9), kind=kOutput, calls=%fused_computation.22 | convolution fusion | flops 6445596672 | bytes 13637632 | tf_op jit(solution)/shard_map/dot_general | solution.py:26
  101.8 9.6 %add_convert_fusion.5.rest_1_.rest_3_.q_ref = bf16[1024,1536]{1,0:T(8,128)(2,1)} fusion(bf16[1024,2048]{1,0:T(8,128)(2,1)} %slice_dynamic-update-slice_fusion.24, bf16[2048,1536]{1,0:T(8,128)(2,1)S(1)} %copy-done.80, f32[1536]{0:T(1024)S(1)} %pad_maximum_fusion.9), kind=kOutput, calls=%fused_computation.21 | convolution fusion | flops 6445596672 | bytes 13637632 | tf_op jit(solution)/shard_map/dot_general | solution.py:26
  111.4 19.0 %attend.2 = (bf16[1024,512]{1,0:T(8,128)(2,1)}, f32[4,1,1024]{2,1,0:T(1,128)}) custom-call(s32[16]{0:T(128)} %stack.67.lim, bf16[1024,1536]{1,0:T(8,128)(2,1)} %add_convert_fusion.6.q_ref.rest_0_.rest_2_, bf16[1024,1536]{1,0:T(8,128)(2,1)} %add_convert_fusion.6.q_ref.rest_0_.rest_2_, bf16[1024,1536]{1,0:T(8,128)(2,1)} %add_convert_fusion.5.rest_1_.rest_3_.q_ref, ...), custom_call_target="tpu_custom_call" | custom-call | flops 8589934592 | bytes 6291456 | tf_op jit(solution)/shard_map/attend/pallas_call | solution.py:193
  138.6 19.2 %attend.3 = (bf16[1024,512]{1,0:T(8,128)(2,1)}, f32[4,1,1024]{2,1,0:T(1,128)}) custom-call(s32[16]{0:T(128)} %stack.67.lim, bf16[1024,1536]{1,0:T(8,128)(2,1)} %add_convert_fusion.5.rest_1_.rest_3_.q_ref, bf16[1024,1536]{1,0:T(8,128)(2,1)} %add_convert_fusion.6.q_ref.rest_0_.rest_2_, bf16[1024,1536]{1,0:T(8,128)(2,1)} %add_convert_fusion.5.rest_1_.rest_3_.q_ref, ...), custom_call_target="tpu_custom_call" | custom-call | flops 8589934592 | bytes 6291456 | tf_op jit(solution)/shard_map/attend/pallas_call | solution.py:193
  181.0 15.4 %collective-permute-done.12 = bf16[256,2048]{1,0:T(8,128)(2,1)S(1)} collective-permute-done((bf16[256,2048]{1,0:T(8,128)(2,1)S(1)}, bf16[256,2048]{1,0:T(8,128)(2,1)S(1)}, u32[]{:S(2)}, u32[]{:S(2)}) %collective-permute-start.12) | collective-permute-done | bytes 1048608 | tf_op jit(solution)/shard_map/ppermute | solution.py:54
  200.9 31.2 %collective-permute-done.14 = bf16[384,2048]{1,0:T(8,128)(2,1)S(1)} collective-permute-done((bf16[384,2048]{1,0:T(8,128)(2,1)}, bf16[384,2048]{1,0:T(8,128)(2,1)S(1)}, u32[]{:S(2)}, u32[]{:S(2)}) %collective-permute-start.14) | collective-permute-done | bytes 1572896 | tf_op jit(solution)/shard_map/ppermute | solution.py:54
  254.0 17.1 %multiply_convert_fusion.3 = (bf16[1024,2048]{1,0:T(8,128)(2,1)}, f32[1024,2048]{1,0:T(8,128)}) fusion(f32[2048]{0:T(1024)S(1)} %dynamic_slice.49, bf16[1024,2048]{1,0:T(8,128)(2,1)} %slice_dynamic-update-slice_fusion.20, bf16[2048,2048]{1,0:T(8,128)(2,1)} %all-gather.9.cloned.1.call-done), kind=kOutput, calls=%fused_computation.17 | convolution fusion | flops 8610906112 | bytes 25174016 | tf_op jit(solution)/shard_map/dot_general | solution.py:26
  275.1 12.7 %convolution_convert_fusion.5 = bf16[1024,2048]{1,0:T(8,128)(2,1)S(1)} fusion(bf16[1024,2048]{1,0:T(8,128)(2,1)} %get-tuple-element.156, bf16[2048,2048]{1,0:T(8,128)(2,1)} %all-gather.11.cloned.1.call-done), kind=kOutput, calls=%fused_computation.29 | convolution fusion | flops 8592031744 | bytes 16777216 | tf_op jit(solution)/shard_map/dot_general | solution.py:20
  295.5 17.2 %multiply_convert_fusion.2 = (bf16[1024,2048]{1,0:T(8,128)(2,1)}, f32[1024,2048]{1,0:T(8,128)}) fusion(f32[2048]{0:T(1024)S(1)} %dynamic_slice.49, bf16[1024,2048]{1,0:T(8,128)(2,1)S(1)} %slice_dynamic-update-slice_fusion.16, bf16[2048,2048]{1,0:T(8,128)(2,1)} %all-gather.9.cloned.1.call-done), kind=kOutput, calls=%fused_computation.15 | convolution fusion | flops 8610906112 | bytes 25174016 | tf_op jit(solution)/shard_map/dot_general | solution.py:26
  315.9 10.9 %convolution_convert_fusion.4 = bf16[1024,2048]{1,0:T(8,128)(2,1)S(1)} fusion(bf16[1024,2048]{1,0:T(8,128)(2,1)} %get-tuple-element.165, bf16[2048,2048]{1,0:T(8,128)(2,1)S(1)} %bitcast.103), kind=kOutput, calls=%fused_computation.28 | convolution fusion | flops 8592031744 | bytes 16777216 | tf_op jit(solution)/shard_map/dot_general | solution.py:20
  337.0 13.1 %collective-permute-done.26 = bf16[256,2048]{1,0:T(8,128)(2,1)S(1)} collective-permute-done((bf16[256,2048]{1,0:T(8,128)(2,1)S(1)}, bf16[256,2048]{1,0:T(8,128)(2,1)S(1)}, u32[]{:S(2)}, u32[]{:S(2)}) %collective-permute-start.26) | collective-permute-done | bytes 1048608 | tf_op jit(solution)/shard_map/ppermute | solution.py:54
  355.2 30.0 %collective-permute-done.28 = bf16[384,2048]{1,0:T(8,128)(2,1)S(1)} collective-permute-done((bf16[384,2048]{1,0:T(8,128)(2,1)S(1)}, bf16[384,2048]{1,0:T(8,128)(2,1)S(1)}, u32[]{:S(2)}, u32[]{:S(2)}) %collective-permute-start.28) | collective-permute-done | bytes 1572896 | tf_op jit(solution)/shard_map/ppermute | solution.py:54
  393.3 7.7 collective-permute-done.30
  406.1 19.4 %convert_reduce_fusion.1 = (f32[2048]{0:T(1024)}, bf16[1024,2048]{1,0:T(8,128)(2,1)}) fusion(f32[1024,2048]{1,0:T(8,128)} %get-tuple-element.371, f32[2048]{0:T(1024)S(1)} %dynamic_slice.49, bf16[1024,2048]{1,0:T(8,128)(2,1)S(1)} %slice_dynamic-update-slice_fusion.12, bf16[2048,2048]{1,0:T(8,128)(2,1)} %all-gather.11.cloned.1.call-done), kind=kOutput, calls=%fused_computation.10 | convolution fusion | flops 8638167040 | bytes 25182208 | tf_op jit(solution)/shard_map/dot_general | solution.py:26
  427.8 10.7 %convolution_convert_fusion.3 = bf16[1024,2048]{1,0:T(8,128)(2,1)S(1)} fusion(bf16[1024,2048]{1,0:T(8,128)(2,1)} %get-tuple-element.177, bf16[2048,2048]{1,0:T(8,128)(2,1)S(1)} %bitcast.99), kind=kOutput, calls=%fused_computation.27 | convolution fusion | flops 8592031744 | bytes 16777216 | tf_op jit(solution)/shard_map/dot_general | solution.py:20
  444.3 11.5 %fusion.50 = f32[2048,2048]{1,0:T(8,128)} fusion(bf16[1024,2048]{1,0:T(8,128)(2,1)S(1)} %slice_dynamic-update-slice_fusion.4, bf16[1024,2048]{1,0:T(8,128)(2,1)S(1)} %copy-done.84), kind=kOutput, calls=%fused_computation.245 | convolution fusion | flops 8589934592 | bytes 25165824 | tf_op jit(solution)/shard_map/dot_general | solution.py:32
  455.8 7.6 collective-permute-done.36
  467.4 16.2 %add_convert_fusion.1 = bf16[2048,2048]{1,0:T(8,128)(2,1)} fusion(f32[2048,2048]{1,0:T(8,128)} %fusion.50, bf16[1024,2048]{1,0:T(8,128)(2,1)S(1)} %slice_dynamic-update-slice_fusion.12, bf16[1024,2048]{1,0:T(8,128)(2,1)} %get-tuple-element.156), kind=kOutput, calls=%fused_computation.1 | convolution fusion | flops 8598323200 | bytes 33554432 | tf_op jit(solution)/shard_map/dot_general | solution.py:32
  494.7 17.2 %convert_reduce_fusion = (f32[2048]{0:T(1024)}, bf16[1024,2048]{1,0:T(8,128)(2,1)}) fusion(f32[1024,2048]{1,0:T(8,128)} %get-tuple-element.373, f32[2048]{0:T(1024)S(1)} %dynamic_slice.49, bf16[1024,2048]{1,0:T(8,128)(2,1)S(1)} %copy-done.57, bf16[2048,2048]{1,0:T(8,128)(2,1)S(1)} %bitcast.105), kind=kOutput, calls=%fused_computation.9 | convolution fusion | flops 8638167040 | bytes 25182208 | tf_op jit(solution)/shard_map/dot_general | solution.py:26
  516.1 10.7 %convolution_convert_fusion.2 = bf16[1024,2048]{1,0:T(8,128)(2,1)S(1)} fusion(bf16[1024,2048]{1,0:T(8,128)(2,1)} %get-tuple-element.191, bf16[2048,2048]{1,0:T(8,128)(2,1)S(1)} %bitcast.101), kind=kOutput, calls=%fused_computation.26 | convolution fusion | flops 8592031744 | bytes 16777216 | tf_op jit(solution)/shard_map/dot_general | solution.py:20
  532.8 14.3 %fusion.51 = f32[2048,2048]{1,0:T(8,128)} fusion(bf16[1024,2048]{1,0:T(8,128)(2,1)} %slice_dynamic-update-slice_fusion.20, bf16[1024,2048]{1,0:T(8,128)(2,1)S(1)} %copy-done.85), kind=kOutput, calls=%fused_computation.246 | convolution fusion | flops 8589934592 | bytes 25165824 | tf_op jit(solution)/shard_map/dot_general | solution.py:32
  555.2 16.2 %add_convert_fusion = bf16[2048,2048]{1,0:T(8,128)(2,1)} fusion(f32[2048,2048]{1,0:T(8,128)} %fusion.51, bf16[1024,2048]{1,0:T(8,128)(2,1)S(1)} %copy-done.55, bf16[1024,2048]{1,0:T(8,128)(2,1)} %get-tuple-element.191), kind=kOutput, calls=%fused_computation | convolution fusion | flops 8598323200 | bytes 33554432 | tf_op jit(solution)/shard_map/dot_general | solution.py:32
  588.4 26.9 %attend_back.2 = (bf16[1024,512]{1,0:T(8,128)(2,1)}, f32[2048,512]{1,0:T(8,128)}, f32[2048,512]{1,0:T(8,128)}) custom-call(s32[16]{0:T(128)} %stack.67.lim, bf16[1024,1536]{1,0:T(8,128)(2,1)} %add_convert_fusion.6.q_ref.rest_0_.rest_2_, bf16[1024,512]{1,0:T(8,128)(2,1)} %get-tuple-element.136.o_ref, bf16[1024,512]{1,0:T(8,128)(2,1)} %convolution_convert_fusion.9.do_ref, ...), custom_call_target="tpu_custom_call" | custom-call | flops 21474836480 | bytes 20971520 | tf_op jit(solution)/shard_map/attend_back/pallas_call | solution.py:285
  637.6 26.9 %attend_back.3 = (bf16[1024,512]{1,0:T(8,128)(2,1)}, bf16[2048,512]{1,0:T(8,128)(2,1)}, bf16[2048,512]{1,0:T(8,128)(2,1)}) custom-call(s32[16]{0:T(128)} %stack.67.lim, bf16[1024,1536]{1,0:T(8,128)(2,1)} %add_convert_fusion.5.rest_1_.rest_3_.q_ref, bf16[1024,512]{1,0:T(8,128)(2,1)} %get-tuple-element.144.o_ref, ...), custom_call_target="tpu_custom_call" | custom-call | flops 21474836480 | bytes 20971520 | tf_op jit(solution)/shard_map/attend_back/pallas_call | solution.py:285
  672.3 12.3 %fusion.21 = f32[2048,1536]{1,0:T(8,128)} fusion(bf16[1024,2048]{1,0:T(8,128)(2,1)} %slice_dynamic-update-slice_fusion.28, bf16[1024,512]{1,0:T(8,128)(2,1)} %get-tuple-element.343, bf16[1024,512]{1,0:T(8,128)(2,1)} %get-tuple-element.341, bf16[1024,512]{1,0:T(8,128)(2,1)} %get-tuple-element.201), kind=kOutput, calls=%fused_computation.222 | convolution fusion | flops 6451888128 | bytes 19922944 | tf_op jit(solution)/shard_map/dot_general | solution.py:32
  684.6 8.9 %convolution_convert_fusion.1 = bf16[1024,2048]{1,0:T(8,128)(2,1)S(1)} fusion(bf16[1024,1536]{1,0:T(8,128)(2,1)S(1)} %copy-done.11, bf16[2048,1536]{1,0:T(8,128)(2,1)} %all-gather.5.cloned.1.call-done), kind=kOutput, calls=%fused_computation.25 | convolution fusion | flops 6444548096 | bytes 13631488 | tf_op jit(solution)/shard_map/dot_general | solution.py:20
  699.0 13.3 %add_convert_fusion.2 = bf16[2048,1536]{1,0:T(8,128)(2,1)} fusion(f32[2048,1536]{1,0:T(8,128)} %fusion.21, bf16[1024,2048]{1,0:T(8,128)(2,1)} %slice_dynamic-update-slice_fusion.24, bf16[1024,512]{1,0:T(8,128)(2,1)S(1)} %get-tuple-element.344, bf16[1024,512]{1,0:T(8,128)(2,1)S(1)} %copy-done.26, bf16[1024,512]{1,0:T(8,128)(2,1)S(1)} %copy-done.45), kind=kOutput, calls=%fused_computation.2 | convolution fusion | flops 6458179584 | bytes 26214400 | tf_op jit(solution)/shard_map/dot_general | solution.py:32
  716.9 11.9 %convolution_convert_fusion = bf16[1024,2048]{1,0:T(8,128)(2,1)} fusion(bf16[1024,1536]{1,0:T(8,128)(2,1)S(1)} %pad_maximum_fusion.1, bf16[2048,1536]{1,0:T(8,128)(2,1)} %all-gather.5.cloned.1.call-done), kind=kOutput, calls=%fused_computation.24 | convolution fusion | flops 6444548096 | bytes 13631488 | tf_op jit(solution)/shard_map/dot_general | solution.py:20
  765.9 10.9 %collective-permute-done.56 = bf16[256,2048]{1,0:T(8,128)(2,1)S(1)} collective-permute-done((bf16[256,2048]{1,0:T(8,128)(2,1)S(1)}, bf16[256,2048]{1,0:T(8,128)(2,1)S(1)}, u32[]{:S(2)}, u32[]{:S(2)}) %collective-permute-start.56) | collective-permute-done | bytes 1048608 | tf_op jit(solution)/shard_map/ppermute | solution.py:54
  (539 shorter events, 297.7 us)
Async XLA Ops:
  7.2 77.5 %all-gather.5.cloned.1.call-start = ((), (), s32[]{:S(2)}) async-start(), calls=%async_computation.4 | async-start | bytes 7077888 | tf_op jit(solution)/shard_map/all_gather | solution.py:384
  9.5 120.9 %all-gather.7.cloned.1.call-start = ((), (), s32[]{:S(2)}) async-start(), calls=%async_computation.5 | async-start | bytes 2359296 | tf_op jit(solution)/shard_map/all_gather | solution.py:384
  10.2 243.8 %all-gather.9.cloned.1.call-start = ((), (), s32[]{:S(2)}) async-start(), calls=%async_computation.6 | async-start | bytes 9437184 | tf_op jit(solution)/shard_map/all_gather | solution.py:384
  10.9 264.1 %all-gather.11.cloned.1.call-start = ((), (), s32[]{:S(2)}) async-start(), calls=%async_computation.7 | async-start | bytes 9437184 | tf_op jit(solution)/shard_map/all_gather | solution.py:384
  13.3 26.4 %collective-permute-start = (bf16[256,2048]{1,0:T(8,128)(2,1)}, bf16[256,2048]{1,0:T(8,128)(2,1)}, u32[]{:S(2)}, u32[]{:S(2)}) collective-permute-start(bf16[256,2048]{1,0:T(8,128)(2,1)} %get-tuple-element.348), channel_id=1, source_target_pairs={{0,1},{1,0},{2,3},{3,2},{4,5},{5,4},{6,7},{7,6},{8,9},{9,8},{10,11... | collective-permute-start | bytes 3145736 | tf_op jit(solution)/shard_map/ppermute | solution.py:54
  16.2 24.8 %collective-permute-start.1 = (bf16[256,2048]{1,0:T(8,128)(2,1)}, bf16[256,2048]{1,0:T(8,128)(2,1)S(1)}, u32[]{:S(2)}, u32[]{:S(2)}) collective-permute-start(bf16[256,2048]{1,0:T(8,128)(2,1)} %get-tuple-element.348), channel_id=1, source_target_pairs={{0,2},{1,3},{2,0},{3,1},{4,6},{5,7},{6,4},{7,5},{8,10},{9,11},{10,... | collective-permute-start | bytes 3145736 | tf_op jit(solution)/shard_map/ppermute | solution.py:54
  17.8 654.5 %reduce-scatter.5.cloned.1.call-start = ((), (), s32[]{:S(2)}) async-start(), calls=%async_computation.8 | async-start | bytes 9437184 | tf_op jit(solution)/shard_map/reduce_scatter | solution.py:388
  56.2 22.8 %collective-permute-start.4 = (bf16[256,2048]{1,0:T(8,128)(2,1)S(1)}, bf16[256,2048]{1,0:T(8,128)(2,1)S(1)}, u32[]{:S(2)}, u32[]{:S(2)}) collective-permute-start(bf16[256,2048]{1,0:T(8,128)(2,1)S(1)} %copy-done.44), channel_id=1, source_target_pairs={{0,1},{1,0},{2,3},{3,2},{4,5},{5,4},{6,7},{7,6},{8,9},{9,8},{10,11... | collective-permute-start | bytes 3145736 | tf_op jit(solution)/shard_map/ppermute | solution.py:54
  56.8 22.6 %collective-permute-start.5 = (bf16[256,2048]{1,0:T(8,128)(2,1)S(1)}, bf16[256,2048]{1,0:T(8,128)(2,1)S(1)}, u32[]{:S(2)}, u32[]{:S(2)}) collective-permute-start(bf16[256,2048]{1,0:T(8,128)(2,1)S(1)} %copy-done.44), channel_id=1, source_target_pairs={{0,2},{1,3},{2,0},{3,1},{4,6},{5,7},{6,4},{7,5},{8,10},{9,11},{10,... | collective-permute-start | bytes 3145736 | tf_op jit(solution)/shard_map/ppermute | solution.py:54
  136.2 21.6 %collective-permute-start.8 = (bf16[256,2048]{1,0:T(8,128)(2,1)}, bf16[256,2048]{1,0:T(8,128)(2,1)S(1)}, u32[]{:S(2)}, u32[]{:S(2)}) collective-permute-start(bf16[256,2048]{1,0:T(8,128)(2,1)} %get-tuple-element.338), channel_id=1, source_target_pairs={{0,1},{1,0},{2,3},{3,2},{4,5},{5,4},{6,7},{7,6},{8,9},{9,8},{10,11... | collective-permute-start | bytes 3145736 | tf_op jit(solution)/shard_map/ppermute | solution.py:54
  137.2 22.0 %collective-permute-start.9 = (bf16[256,2048]{1,0:T(8,128)(2,1)}, bf16[256,2048]{1,0:T(8,128)(2,1)}, u32[]{:S(2)}, u32[]{:S(2)}) collective-permute-start(bf16[256,2048]{1,0:T(8,128)(2,1)} %get-tuple-element.337), channel_id=1, source_target_pairs={{0,2},{1,3},{2,0},{3,1},{4,6},{5,7},{6,4},{7,5},{8,10},{9,11},{10,... | collective-permute-start | bytes 3145736 | tf_op jit(solution)/shard_map/ppermute | solution.py:54
  198.8 33.4 %collective-permute-start.14 = (bf16[384,2048]{1,0:T(8,128)(2,1)}, bf16[384,2048]{1,0:T(8,128)(2,1)S(1)}, u32[]{:S(2)}, u32[]{:S(2)}) collective-permute-start(bf16[384,2048]{1,0:T(8,128)(2,1)} %get-tuple-element.150), channel_id=1, source_target_pairs={{0,1},{1,0},{2,3},{3,2},{4,5},{5,4},{6,7},{7,6},{8,9},{9,8},{10,11... | collective-permute-start | bytes 4718600 | tf_op jit(solution)/shard_map/ppermute | solution.py:54
  200.1 32.2 %collective-permute-start.15 = (bf16[384,2048]{1,0:T(8,128)(2,1)}, bf16[384,2048]{1,0:T(8,128)(2,1)S(1)}, u32[]{:S(2)}, u32[]{:S(2)}) collective-permute-start(bf16[384,2048]{1,0:T(8,128)(2,1)} %get-tuple-element.151), channel_id=1, source_target_pairs={{0,2},{1,3},{2,0},{3,1},{4,6},{5,7},{6,4},{7,5},{8,10},{9,11},{10,... | collective-permute-start | bytes 4718600 | tf_op jit(solution)/shard_map/ppermute | solution.py:54
  247.9 23.2 %collective-permute-start.18 = (bf16[256,2048]{1,0:T(8,128)(2,1)}, bf16[256,2048]{1,0:T(8,128)(2,1)}, u32[]{:S(2)}, u32[]{:S(2)}) collective-permute-start(bf16[256,2048]{1,0:T(8,128)(2,1)} %get-tuple-element.155), channel_id=1, source_target_pairs={{0,1},{1,0},{2,3},{3,2},{4,5},{5,4},{6,7},{7,6},{8,9},{9,8},{10,11... | collective-permute-start | bytes 3145736 | tf_op jit(solution)/shard_map/ppermute | solution.py:54
  248.6 22.5 %collective-permute-start.19 = (bf16[256,2048]{1,0:T(8,128)(2,1)}, bf16[256,2048]{1,0:T(8,128)(2,1)S(1)}, u32[]{:S(2)}, u32[]{:S(2)}) collective-permute-start(bf16[256,2048]{1,0:T(8,128)(2,1)} %get-tuple-element.155), channel_id=1, source_target_pairs={{0,2},{1,3},{2,0},{3,1},{4,6},{5,7},{6,4},{7,5},{8,10},{9,11},{10,... | collective-permute-start | bytes 3145736 | tf_op jit(solution)/shard_map/ppermute | solution.py:54
  289.2 23.6 %collective-permute-start.22 = (bf16[256,2048]{1,0:T(8,128)(2,1)S(1)}, bf16[256,2048]{1,0:T(8,128)(2,1)S(1)}, u32[]{:S(2)}, u32[]{:S(2)}) collective-permute-start(bf16[256,2048]{1,0:T(8,128)(2,1)S(1)} %get-tuple-element.326), channel_id=1, source_target_pairs={{0,1},{1,0},{2,3},{3,2},{4,5},{5,4},{6,7},{7,6},{8,9},{9,8},{10,11... | collective-permute-start | bytes 3145736 | tf_op jit(solution)/shard_map/ppermute | solution.py:54
  290.0 22.9 %collective-permute-start.23 = (bf16[256,2048]{1,0:T(8,128)(2,1)S(1)}, bf16[256,2048]{1,0:T(8,128)(2,1)S(1)}, u32[]{:S(2)}, u32[]{:S(2)}) collective-permute-start(bf16[256,2048]{1,0:T(8,128)(2,1)S(1)} %get-tuple-element.325), channel_id=1, source_target_pairs={{0,2},{1,3},{2,0},{3,1},{4,6},{5,7},{6,4},{7,5},{8,10},{9,11},{10,... | collective-permute-start | bytes 3145736 | tf_op jit(solution)/shard_map/ppermute | solution.py:54
  331.2 22.0 %collective-permute-start.27 = (bf16[256,2048]{1,0:T(8,128)(2,1)S(1)}, bf16[256,2048]{1,0:T(8,128)(2,1)S(1)}, u32[]{:S(2)}, u32[]{:S(2)}) collective-permute-start(bf16[256,2048]{1,0:T(8,128)(2,1)S(1)} %get-tuple-element.319), channel_id=1, source_target_pairs={{0,2},{1,3},{2,0},{3,1},{4,6},{5,7},{6,4},{7,5},{8,10},{9,11},{10,... | collective-permute-start | bytes 3145736 | tf_op jit(solution)/shard_map/ppermute | solution.py:54
  354.1 31.1 %collective-permute-start.28 = (bf16[384,2048]{1,0:T(8,128)(2,1)S(1)}, bf16[384,2048]{1,0:T(8,128)(2,1)S(1)}, u32[]{:S(2)}, u32[]{:S(2)}) collective-permute-start(bf16[384,2048]{1,0:T(8,128)(2,1)S(1)} %get-tuple-element.171), channel_id=1, source_target_pairs={{0,2},{1,3},{2,0},{3,1},{4,6},{5,7},{6,4},{7,5},{8,10},{9,11},{10,... | collective-permute-start | bytes 4718600 | tf_op jit(solution)/shard_map/ppermute | solution.py:54
  354.6 30.6 %collective-permute-start.29 = (bf16[384,2048]{1,0:T(8,128)(2,1)S(1)}, bf16[384,2048]{1,0:T(8,128)(2,1)S(1)}, u32[]{:S(2)}, u32[]{:S(2)}) collective-permute-start(bf16[384,2048]{1,0:T(8,128)(2,1)S(1)} %get-tuple-element.172), channel_id=1, source_target_pairs={{0,1},{1,0},{2,3},{3,2},{4,5},{5,4},{6,7},{7,6},{8,9},{9,8},{10,11... | collective-permute-start | bytes 4718600 | tf_op jit(solution)/shard_map/ppermute | solution.py:54
  403.4 23.1 %collective-permute-start.32 = (bf16[256,2048]{1,0:T(8,128)(2,1)S(1)}, bf16[256,2048]{1,0:T(8,128)(2,1)S(1)}, u32[]{:S(2)}, u32[]{:S(2)}) collective-permute-start(bf16[256,2048]{1,0:T(8,128)(2,1)S(1)} %get-tuple-element.176), channel_id=1, source_target_pairs={{0,1},{1,0},{2,3},{3,2},{4,5},{5,4},{6,7},{7,6},{8,9},{9,8},{10,11... | collective-permute-start | bytes 3145736 | tf_op jit(solution)/shard_map/ppermute | solution.py:54
  404.0 22.5 %collective-permute-start.33 = (bf16[256,2048]{1,0:T(8,128)(2,1)S(1)}, bf16[256,2048]{1,0:T(8,128)(2,1)S(1)}, u32[]{:S(2)}, u32[]{:S(2)}) collective-permute-start(bf16[256,2048]{1,0:T(8,128)(2,1)S(1)} %get-tuple-element.176), channel_id=1, source_target_pairs={{0,2},{1,3},{2,0},{3,1},{4,6},{5,7},{6,4},{7,5},{8,10},{9,11},{10,... | collective-permute-start | bytes 3145736 | tf_op jit(solution)/shard_map/ppermute | solution.py:54
  442.2 21.2 %collective-permute-start.36 = (bf16[256,2048]{1,0:T(8,128)(2,1)S(1)}, bf16[256,2048]{1,0:T(8,128)(2,1)S(1)}, u32[]{:S(2)}, u32[]{:S(2)}) collective-permute-start(bf16[256,2048]{1,0:T(8,128)(2,1)S(1)} %get-tuple-element.314), channel_id=1, source_target_pairs={{0,1},{1,0},{2,3},{3,2},{4,5},{5,4},{6,7},{7,6},{8,9},{9,8},{10,11... | collective-permute-start | bytes 3145736 | tf_op jit(solution)/shard_map/ppermute | solution.py:54
  484.6 257.7 %reduce-scatter.7.cloned.1.call-start = ((), (), s32[]{:S(2)}) async-start(), calls=%async_computation.9 | async-start | bytes 9437184 | tf_op jit(solution)/shard_map/reduce_scatter | solution.py:388
  493.2 21.5 %collective-permute-start.40 = (bf16[256,2048]{1,0:T(8,128)(2,1)S(1)}, bf16[256,2048]{1,0:T(8,128)(2,1)S(1)}, u32[]{:S(2)}, u32[]{:S(2)}) collective-permute-start(bf16[256,2048]{1,0:T(8,128)(2,1)S(1)} %get-tuple-element.185), channel_id=1, source_target_pairs={{0,1},{1,0},{2,3},{3,2},{4,5},{5,4},{6,7},{7,6},{8,9},{9,8},{10,11... | collective-permute-start | bytes 3145736 | tf_op jit(solution)/shard_map/ppermute | solution.py:54
  493.7 21.5 %collective-permute-start.41 = (bf16[256,2048]{1,0:T(8,128)(2,1)S(1)}, bf16[256,2048]{1,0:T(8,128)(2,1)S(1)}, u32[]{:S(2)}, u32[]{:S(2)}) collective-permute-start(bf16[256,2048]{1,0:T(8,128)(2,1)S(1)} %get-tuple-element.185), channel_id=1, source_target_pairs={{0,2},{1,3},{2,0},{3,1},{4,6},{5,7},{6,4},{7,5},{8,10},{9,11},{10,... | collective-permute-start | bytes 3145736 | tf_op jit(solution)/shard_map/ppermute | solution.py:54
  571.4 211.4 %reduce-scatter.11.cloned.1.call-start = ((), (), s32[]{:S(2)}) async-start(), calls=%async_computation.11 | async-start | bytes 2359296 | tf_op jit(solution)/shard_map/reduce_scatter | solution.py:388
  583.0 32.2 %collective-permute-start.48 = (bf16[256,2048]{1,0:T(8,128)(2,1)S(1)}, bf16[256,2048]{1,0:T(8,128)(2,1)S(1)}, u32[]{:S(2)}, u32[]{:S(2)}) collective-permute-start(bf16[256,2048]{1,0:T(8,128)(2,1)S(1)} %get-tuple-element.202), channel_id=1, source_target_pairs={{0,1},{1,0},{2,3},{3,2},{4,5},{5,4},{6,7},{7,6},{8,9},{9,8},{10,11... | collective-permute-start | bytes 3145736 | tf_op jit(solution)/shard_map/ppermute | solution.py:54
  583.8 31.4 %collective-permute-start.49 = (bf16[256,2048]{1,0:T(8,128)(2,1)S(1)}, bf16[256,2048]{1,0:T(8,128)(2,1)S(1)}, u32[]{:S(2)}, u32[]{:S(2)}) collective-permute-start(bf16[256,2048]{1,0:T(8,128)(2,1)S(1)} %get-tuple-element.202), channel_id=1, source_target_pairs={{0,2},{1,3},{2,0},{3,1},{4,6},{5,7},{6,4},{7,5},{8,10},{9,11},{10,... | collective-permute-start | bytes 3145736 | tf_op jit(solution)/shard_map/ppermute | solution.py:54
  668.8 129.7 %reduce-scatter.9.cloned.1.call-start = ((), (), s32[]{:S(2)}) async-start(), calls=%async_computation.10 | async-start | bytes 7077888 | tf_op jit(solution)/shard_map/reduce_scatter | solution.py:388
  751.3 25.5 %collective-permute-start.56 = (bf16[256,2048]{1,0:T(8,128)(2,1)S(1)}, bf16[256,2048]{1,0:T(8,128)(2,1)S(1)}, u32[]{:S(2)}, u32[]{:S(2)}) collective-permute-start(bf16[256,2048]{1,0:T(8,128)(2,1)S(1)} %get-tuple-element.298), channel_id=1, source_target_pairs={{0,1},{1,0},{2,3},{3,2},{4,5},{5,4},{6,7},{7,6},{8,9},{9,8},{10,11... | collective-permute-start | bytes 3145736 | tf_op jit(solution)/shard_map/ppermute | solution.py:54
  752.3 25.2 %collective-permute-start.57 = (bf16[256,2048]{1,0:T(8,128)(2,1)S(1)}, bf16[256,2048]{1,0:T(8,128)(2,1)S(1)}, u32[]{:S(2)}, u32[]{:S(2)}) collective-permute-start(bf16[256,2048]{1,0:T(8,128)(2,1)S(1)} %get-tuple-element.297), channel_id=1, source_target_pairs={{0,2},{1,3},{2,0},{3,1},{4,6},{5,7},{6,4},{7,5},{8,10},{9,11},{10,... | collective-permute-start | bytes 3145736 | tf_op jit(solution)/shard_map/ppermute | solution.py:54
  (140 other events, 1848.5 us)
Sparse Core Ops, SparseCore 0:
  10.2 67.4 all-gather.4
  79.3 27.8 all-gather.6
  108.7 81.4 all-gather.8
  191.7 80.5 all-gather.10
  484.7 87.6 reduce-scatter.4
  574.5 87.9 reduce-scatter.6
  668.9 33.1 reduce-scatter.10
  714.9 67.3 reduce-scatter.8
